TPU v7x, 512 devices: a whole 4x4x16 slice. The times are simulated.
512 devices in a mesh: section: 16 (over z), batch: 32 (over x, y, core).
Axes of the slice: x: 4, y: 4, z: 16, core: 2. Of those that a mesh axis runs over, the one named last changes fastest.
Arguments:
- images: bfloat16 [32, 256, 1536], P('batch'), may hold values from -10 to 10
- weights: bfloat16 [16, 6, 256, 256], P('section'), may hold values from -0.375 to 0.375
- bn_mean: float32 [16, 1536], P('section'), may hold values from -3 to 3
- bn_var: float32 [16, 1536], P('section'), may hold values from 0.25 to 2
- bn_gain: float32 [16, 1536], P('section'), may hold values from 0.1 to 1.9
- bn_bias: float32 [16, 1536], P('section'), may hold values from -3 to 3
Outputs:
- image_grad: bfloat16 [32, 256, 1536], P('batch', 'section')
- loss_value: float32 [], replicated
All inputs are finite; a program needn't handle non-finite values.
Results may differ from a plain program's by a relative error of at most 0.013.
Values may be sent and summed in bfloat16 or wider, within the bound.
No kernel may reach another device: no remote copies, remote signals or barrier semaphores. Data moves between devices by JAX's collectives and lax.ppermute only.
A program may use at most 64 MiB of HBM per device.

v0:
```python
import jax
import jax.numpy as jnp
from jax import lax
from jax.sharding import PartitionSpec as P

BLOCK = 512
MICRO = 8


EPS = 1e-05
HIGHEST = lax.Precision.HIGHEST


def from_behind(value, axis, steps):
    count = lax.axis_size(axis)
    first, last = (max(0, -steps), min(count, count - steps))
    return lax.ppermute(value, axis, [(source, source + steps) for source in range(first, last)])


def group_forward(hidden, weight):
    row_total = hidden.shape[0]
    groups, in_width, out_width = weight.shape
    pieces = hidden.reshape(row_total, groups, in_width)
    result = jnp.einsum("rgi,gio->rgo", pieces, weight, preferred_element_type=jnp.float32)
    return result.reshape(row_total, groups * out_width)


def group_backward(upstream, weight):
    row_total = upstream.shape[0]
    groups, in_width, out_width = weight.shape
    pieces = upstream.reshape(row_total, groups, out_width)
    result = jnp.einsum("rgo,gio->rgi", pieces, weight, preferred_element_type=jnp.float32)
    return result.reshape(row_total, groups * in_width)


def block_gram(pre_act, center, block_width):
    row_total, channels = pre_act.shape
    centered = (pre_act - center).reshape(row_total, channels // block_width, block_width)
    return jnp.einsum("rbi,rbj->bij", centered, centered, precision=HIGHEST)


def shards(images, weights, bn_mean, bn_var, bn_gain, bn_bias):
    sections = lax.axis_size("section")
    position = lax.axis_index("section")
    group_rows = images.shape[1]
    channels = images.shape[2]
    micro_rows = group_rows // MICRO
    block_count = channels // BLOCK
    row_total = group_rows * lax.axis_size("batch")
    weight = weights[0]
    run_mean = bn_mean[0]
    run_var = bn_var[0]
    bn_scale = bn_gain[0] * lax.rsqrt(run_var + EPS)
    bn_shift = bn_bias[0]
    source = images[0].reshape(MICRO, micro_rows, channels)
    tick_count = MICRO + sections - 1
    gram_shape = (1, 1, 1)
    stored_type = jnp.float32

    def forward_tick(tick_index, loop_vars):
        incoming, stored, sum_pre, sum_gram = loop_vars
        offset_raw = tick_index - position
        in_range = (offset_raw >= 0) & (offset_raw < MICRO)
        slot_index = jnp.clip(offset_raw, 0, MICRO - 1)
        entering = lax.dynamic_index_in_dim(source, slot_index, 0, keepdims=False)
        hidden = jnp.where(position == 0, entering, incoming)

        def forward_active_step(hidden_in):
            pre_act = group_forward(hidden_in, weight)
            emitted = jax.nn.silu((pre_act - run_mean) * bn_scale + bn_shift).astype(jnp.bfloat16)
            block_sums = jnp.zeros(gram_shape, jnp.float32)
            return (pre_act, emitted, jnp.sum(pre_act, axis=0), block_sums)

        def forward_bubble_step(hidden_in):
            return (
                jnp.zeros((micro_rows, channels), jnp.float32),
                jnp.zeros((micro_rows, channels), jnp.bfloat16),
                jnp.zeros((channels,), jnp.float32),
                jnp.zeros(gram_shape, jnp.float32),
            )

        pre_act, emitted, part_sum, block_sums = lax.cond(
            in_range, forward_active_step, forward_bubble_step, hidden
        )
        previous = lax.dynamic_index_in_dim(stored, slot_index, 0, keepdims=False)
        stored = lax.dynamic_update_index_in_dim(
            stored, jnp.where(in_range, pre_act, previous), slot_index, 0
        )
        incoming = from_behind(emitted, "section", 1)
        return (incoming, stored, sum_pre + part_sum, sum_gram + block_sums)

    start_vars = (
        jnp.zeros((micro_rows, channels), jnp.bfloat16),
        jnp.zeros((MICRO, micro_rows, channels), stored_type),
        jnp.zeros((channels,), jnp.float32),
        jnp.zeros(gram_shape, jnp.float32),
    )
    incoming, stored, sum_pre, sum_gram = lax.fori_loop(0, tick_count, forward_tick, start_vars)
    total_sum = lax.psum(sum_pre, "batch")
    batch_mean = total_sum / row_total
    flat_saved = stored.reshape(group_rows, channels)
    covariance = lax.psum(block_gram(flat_saved, batch_mean, BLOCK), "batch") / row_total
    var_blocks = run_var.reshape(block_count, BLOCK)
    deviation = covariance - var_blocks[:, :, None] * jnp.eye(BLOCK, dtype=jnp.float32)[None]
    layer_term = jnp.sum((batch_mean - run_mean) ** 2) + 0.25 * jnp.sum(deviation**2)
    loss_value = lax.psum(layer_term, "section") / (sections * channels)
    mean_pull = 2.0 * (batch_mean - run_mean)

    def backward_tick(tick_index, loop_vars):
        incoming, image_grads = loop_vars
        offset_raw = tick_index - (sections - 1 - position)
        in_range = (offset_raw >= 0) & (offset_raw < MICRO)
        slot_index = jnp.clip(offset_raw, 0, MICRO - 1)
        stored_item = lax.dynamic_index_in_dim(stored, slot_index, 0, keepdims=False)

        def backward_active_step(operands):
            item_in, upstream = operands
            active = (item_in - run_mean) * bn_scale + bn_shift
            sig_value = jax.nn.sigmoid(active)
            silu_slope = sig_value * (1.0 + active * (1.0 - sig_value))
            centered = (item_in - batch_mean).reshape(micro_rows, block_count, BLOCK)
            cov_pull = jnp.einsum("rbi,bij->rbj", centered, deviation, precision=HIGHEST).reshape(
                micro_rows, channels
            )
            pre_grad = (
                upstream.astype(jnp.float32) * silu_slope * bn_scale + mean_pull + cov_pull
            ).astype(jnp.bfloat16)
            return group_backward(pre_grad, weight).astype(jnp.bfloat16)

        def backward_bubble_step(operands):
            return jnp.zeros((micro_rows, channels), jnp.bfloat16)

        sent_back = lax.cond(
            in_range, backward_active_step, backward_bubble_step, (stored_item, incoming)
        )
        previous = lax.dynamic_index_in_dim(image_grads, slot_index, 0, keepdims=False)
        image_grads = lax.dynamic_update_index_in_dim(
            image_grads, jnp.where(in_range, sent_back, previous), slot_index, 0
        )
        incoming = from_behind(sent_back, "section", -1)
        return (incoming, image_grads)

    back_vars = (
        jnp.zeros((micro_rows, channels), jnp.bfloat16),
        jnp.zeros((MICRO, micro_rows, channels), jnp.bfloat16),
    )
    incoming, image_grads = lax.fori_loop(0, tick_count, backward_tick, back_vars)
    flat_grads = image_grads.reshape(group_rows, channels)
    own_term = jnp.where(
        position == 0,
        flat_grads.astype(jnp.float32),
        jnp.zeros((group_rows, channels), jnp.float32),
    )
    own_rows = lax.psum_scatter(
        own_term.astype(jnp.bfloat16), "section", scatter_dimension=0, tiled=True
    )
    return (own_rows[None], loss_value)


def solution(mesh):
    placed = (
        P("batch", None, None),
        P("section", None, None, None),
        P("section", None),
        P("section", None),
        P("section", None),
        P("section", None),
    )
    return jax.shard_map(
        shards,
        mesh=mesh,
        in_specs=placed,
        out_specs=(P("batch", "section", None), P()),
        check_vma=False,
    )
```

profile of v0, /device:TPU:1, one launch (start us, length us, event | category | flops | bytes accessed | tf_op | source)
XLA Modules:
  0.0 871.1 jit_solution(1067873683740494981)
XLA Ops:
  8.2 213.9 %while.37 = (s32[]{:T(128)}, bf16[32,1536]{1,0:T(8,128)(2,1)S(1)}, f32[8,32,1536]{2,1,0:T(8,128)S(1)}, f32[1536]{0:T(1024)S(1)}, s32[]{:T(128)}, /*index=5*/pred...) while((s32[]{:T(128)}, bf16[32,1536]{1,0:T(8,128)(2,1)S(1)}, ...), condition=%wide.region_4.5_spmd.clone, body=%wide.region_0.4_spmd.clone.sunk | while | flops 25708040 | bytes 3520875 | solution.py:98
  8.2 5.4 conditional.6
  16.6 5.4 conditional.6
  27.4 5.4 conditional.6
  38.2 5.4 conditional.6
  48.9 5.4 conditional.6
  60.4 5.4 conditional.6
  71.4 5.4 conditional.6
  82.6 5.4 conditional.6
  94.1 8.5 collective-permute-start.1
  111.0 7.8 collective-permute-start.1
  129.8 8.7 collective-permute-start.1
  148.1 9.7 %collective-permute-start.1 = (bf16[32,1536]{1,0:T(8,128)(2,1)S(1)}, bf16[32,1536]{1,0:T(8,128)(2,1)S(1)}, u32[]{:S(2)}, u32[]{:S(2)}) collective-permute-start(bf16[32,1536]{1,0:T(8,128)(2,1)S(1)} %get-tuple-element.842), channel_id=1, source_target_pairs={{0,32},{32,64},{64,96},{96,128},{128,160},{160,192},{192,224},{224... | collective-permute-start | bytes 294920 | tf_op jit(solution)/shard_map/while/body/eval_jaxpr/ppermute | solution.py:17
  160.4 5.2 collective-permute-start.1
  182.5 5.4 collective-permute-start.1
  190.4 5.2 collective-permute-start.1
  198.6 5.4 collective-permute-start.1
  213.4 7.1 collective-permute-start.1
  222.1 91.5 %psum.21 = f32[1536]{0:T(1024)S(1)} all-reduce(f32[1536]{0:T(1024)S(1)} %get-tuple-element.603), channel_id=1, replica_groups=mesh['section'=16,'batch'=32] {'batch'}, use_global_device_ids=true, to_apply=%region_5.6 | all-reduce | flops 1536 | bytes 12288 | tf_op jit(solution)/shard_map/psum | solution.py:99
  325.6 162.1 %all-reduce.2.cloned.1.call-done = f32[3,512,512]{2,1,0:T(8,128)} async-done(((f32[3,512,512]{2,1,0:T(8,128)}), f32[3,512,512]{2,1,0:T(8,128)}) %all-reduce.2.cloned.1.call-update) | async-done | bytes 3145744 | tf_op jit(solution)/shard_map/psum | solution.py:102
  492.5 295.6 %while.36 = (s32[]{:T(128)}, bf16[32,1536]{1,0:T(8,128)(2,1)S(1)}, bf16[8,32,1536]{2,1,0:T(8,128)(2,1)}, s32[]{:T(128)}, f32[8,32,1536]{2,1,0:T(8,128)}, /*index...) while((s32[]{:T(128)}, bf16[32,1536]{1,0:T(8,128)(2,1)S(1)}, ...), condition=%wide.region_10.11_spmd, body=%wide.region_7.10_spmd.sunk | while | flops 328089600 | bytes 7834472 | solution.py:147
  585.3 90.6 %collective-permute-done = bf16[32,1536]{1,0:T(8,128)(2,1)S(1)} collective-permute-done((bf16[32,1536]{1,0:T(8,128)(2,1)S(1)}, bf16[32,1536]{1,0:T(8,128)(2,1)S(1)}, u32[]{:S(2)}, u32[]{:S(2)}) %collective-permute-start) | collective-permute-done | bytes 98336 | tf_op jit(solution)/shard_map/while/body/eval_jaxpr/ppermute | solution.py:17
  676.0 7.3 conditional.5
  689.8 7.3 conditional.5
  705.3 7.3 conditional.5
  719.6 7.3 conditional.5
  733.0 7.3 conditional.5
  747.6 7.3 conditional.5
  761.5 7.3 conditional.5
  775.4 7.3 conditional.5
  791.4 20.6 %psum.23 = f32[]{:T(128)} all-reduce(f32[]{:T(128)S(6)} %add.132), channel_id=1, replica_groups=mesh['section'=16,'batch'=32] {'section'}, use_global_device_ids=true, to_apply=%region_14.15 | all-reduce | flops 1 | bytes 8 | tf_op jit(solution)/shard_map/psum | solution.py:106
  812.6 50.5 %reduce-scatter.2.cloned.1.call-done = bf16[16,1536]{1,0:T(8,128)(2,1)} async-done(((bf16[256,1536]{1,0:T(8,128)(2,1)}), bf16[16,1536]{1,0:T(8,128)(2,1)}) %reduce-scatter.2.cloned.1.call-update) | async-done | bytes 49168 | tf_op jit(solution)/shard_map/reduce_scatter | solution.py:154
  (457 shorter events, 384.3 us)
Async XLA Ops:
  7.2 480.5 %all-reduce.2.cloned.1.call-start = ((), (), s32[]{:S(2)}) async-start(), calls=%async_computation.1 | async-start | bytes 6291456 | tf_op jit(solution)/shard_map/psum | solution.py:102
  94.1 10.1 %collective-permute-start.1 = (bf16[32,1536]{1,0:T(8,128)(2,1)S(1)}, bf16[32,1536]{1,0:T(8,128)(2,1)S(1)}, u32[]{:S(2)}, u32[]{:S(2)}) collective-permute-start(bf16[32,1536]{1,0:T(8,128)(2,1)S(1)} %get-tuple-element.842), channel_id=1, source_target_pairs={{0,32},{32,64},{64,96},{96,128},{128,160},{160,192},{192,224},{224... | collective-permute-start | bytes 294920 | tf_op jit(solution)/shard_map/while/body/eval_jaxpr/ppermute | solution.py:17
  111.0 10.1 %collective-permute-start.1 = (bf16[32,1536]{1,0:T(8,128)(2,1)S(1)}, bf16[32,1536]{1,0:T(8,128)(2,1)S(1)}, u32[]{:S(2)}, u32[]{:S(2)}) collective-permute-start(bf16[32,1536]{1,0:T(8,128)(2,1)S(1)} %get-tuple-element.842), channel_id=1, source_target_pairs={{0,32},{32,64},{64,96},{96,128},{128,160},{160,192},{192,224},{224... | collective-permute-start | bytes 294920 | tf_op jit(solution)/shard_map/while/body/eval_jaxpr/ppermute | solution.py:17
  121.8 7.3 collective-permute-start.1
  129.8 10.3 %collective-permute-start.1 = (bf16[32,1536]{1,0:T(8,128)(2,1)S(1)}, bf16[32,1536]{1,0:T(8,128)(2,1)S(1)}, u32[]{:S(2)}, u32[]{:S(2)}) collective-permute-start(bf16[32,1536]{1,0:T(8,128)(2,1)S(1)} %get-tuple-element.842), channel_id=1, source_target_pairs={{0,32},{32,64},{64,96},{96,128},{128,160},{160,192},{192,224},{224... | collective-permute-start | bytes 294920 | tf_op jit(solution)/shard_map/while/body/eval_jaxpr/ppermute | solution.py:17
  140.9 6.6 collective-permute-start.1
  148.1 11.5 %collective-permute-start.1 = (bf16[32,1536]{1,0:T(8,128)(2,1)S(1)}, bf16[32,1536]{1,0:T(8,128)(2,1)S(1)}, u32[]{:S(2)}, u32[]{:S(2)}) collective-permute-start(bf16[32,1536]{1,0:T(8,128)(2,1)S(1)} %get-tuple-element.842), channel_id=1, source_target_pairs={{0,32},{32,64},{64,96},{96,128},{128,160},{160,192},{192,224},{224... | collective-permute-start | bytes 294920 | tf_op jit(solution)/shard_map/while/body/eval_jaxpr/ppermute | solution.py:17
  160.4 7.4 collective-permute-start.1
  175.2 6.6 collective-permute-start.1
  182.5 7.2 collective-permute-start.1
  190.4 7.5 collective-permute-start.1
  198.6 7.0 collective-permute-start.1
  206.4 6.3 collective-permute-start.1
  213.4 8.7 collective-permute-start.1
  324.3 538.8 %reduce-scatter.2.cloned.1.call-start = ((), (), s32[]{:S(2)}) async-start(), calls=%async_computation.2 | async-start | bytes 835584 | tf_op jit(solution)/shard_map/reduce_scatter | solution.py:154
  514.8 6.6 collective-permute-start
  521.3 6.6 collective-permute-start
  527.9 7.1 collective-permute-start
  535.1 7.7 collective-permute-start
  542.7 7.2 collective-permute-start
  556.0 6.1 collective-permute-start
  562.2 6.6 collective-permute-start
  568.8 6.6 collective-permute-start
  575.3 7.1 collective-permute-start
  582.5 93.5 %collective-permute-start = (bf16[32,1536]{1,0:T(8,128)(2,1)S(1)}, bf16[32,1536]{1,0:T(8,128)(2,1)S(1)}, u32[]{:S(2)}, u32[]{:S(2)}) collective-permute-start(bf16[32,1536]{1,0:T(8,128)(2,1)S(1)} %get-tuple-element.944), channel_id=1, source_target_pairs={{32,0},{64,32},{96,64},{128,96},{160,128},{192,160},{224,192},{256... | collective-permute-start | bytes 294920 | tf_op jit(solution)/shard_map/while/body/eval_jaxpr/ppermute | solution.py:17
  683.3 6.6 collective-permute-start
  697.2 8.1 collective-permute-start
  712.6 7.0 collective-permute-start
  726.9 6.1 collective-permute-start
  740.4 7.3 collective-permute-start
  754.9 6.6 collective-permute-start
  768.8 6.6 collective-permute-start
  (19 other events, 517.4 us)
Sparse Core Ops, SparseCore 0:
  324.5 163.1 all-reduce.1
  790.4 72.7 reduce-scatter.1
where the time goes:
time: 885 us; the launch traced here: 871 us
  waiting for transfers between devices  415 us (47%)
  starting transfers between devices  148 us (17%)
  blocking collectives  112 us (13%)
  other arithmetic  70.8 us (8%)
  local copies, waits for them, and re-layouts  62.6 us (7%)
  matrix products  43.3 us (5%)
  between operations  17.1 us (2%)
    ppermute x46, waiting for transfers between devices, from_behind(): lax.ppermute(value, axis, [(source, source + steps) for source in range(f...  202 us
    psum x1, waiting for transfers between devices, shards(): lax.psum(block_gram(flat_saved, batch_mean, BLOCK), 'batch') / row_total  162 us
    ppermute x46, starting transfers between devices, from_behind(): lax.ppermute(value, axis, [(source, source + steps) for source in range(f...  148 us
    psum x1, blocking collectives, shards(): total_sum = lax.psum(sum_pre, 'batch')  91.5 us
    reduce_scatter x1, waiting for transfers between devices, shards(): lax.psum_scatter(own_term.astype(jnp.bfloat16), 'section', scatter_dimens...  50.5 us
    dynamic_slice x23, local copies, waits for them, and re-layouts, backward_tick(): lax.dynamic_index_in_dim(image_grads, slot_index, 0, keepdims=False)  20.8 us
    psum x1, blocking collectives, shards(): loss_value = lax.psum(layer_term, 'section') / (sections * channels)  20.6 us
  transfers between devices with their start and end apart: 48, of which 48 were waited for; matrix products, arithmetic and copies ran while one was open for 5% of the time, Pallas kernels for 0%

commit v1 on v0

v1 whole, which is shorter than its diff:
```python
import jax
import jax.numpy as jnp
import numpy as np
from jax import lax
from jax.experimental import pallas as pl
from jax.experimental.pallas import tpu as pltpu
from jax.sharding import Mesh, PartitionSpec as P

EPS = 1e-05
HIGHEST = lax.Precision.HIGHEST
F32 = jnp.float32
BF16 = jnp.bfloat16

LAYERS = 16
GW = 256
BLOCKS = 3
CHIPS = 16
SLICE = GW // CHIPS
PROWS = 8
BROWS = 64
ROWS = 2 * BROWS
HOME = CHIPS * BROWS
PARTS = 8
PIECE = GW // PARTS
TAIL = 8
TOTAL = HOME * PARTS


def split2(value):
    high = lax.reduce_precision(value, 8, 7)
    return high.astype(BF16), (value - high).astype(BF16)


def split3(value):
    high = value.astype(BF16).astype(F32)
    rest = value - high
    middle = rest.astype(BF16).astype(F32)
    return high, middle, rest - middle


def forward_kernel(x_ref, w_ref, par_ref, xs_ref, slope_ref):
    x = x_ref[...]
    for layer in range(LAYERS):
        xs_ref[layer] = x
        weight = w_ref[:, layer].reshape(GW, GW)
        packed = par_ref[layer, SLICE:SLICE + PROWS].astype(F32)
        scale = packed[0:1] + packed[4:5]
        shift = packed[1:2] + packed[5:6]
        active = jnp.dot(x, weight, preferred_element_type=F32) * scale + shift
        gate = 1.0 / (1.0 + jnp.exp(-active))
        slope_ref[layer] = gate * (1.0 + active * (1.0 - gate)) * scale
        x = (active * gate).astype(BF16)


def gram_kernel(x_ref, wl_ref, out_ref, zc_ref):
    means = []
    for g in range(2):
        z = jnp.dot(x_ref[:, g].reshape(HOME, GW), wl_ref[g, 0:GW], preferred_element_type=F32)
        mean = jnp.sum(z, axis=0, keepdims=True) * (1.0 / HOME)
        zc_ref[g] = (z - mean).astype(BF16)
        means.append(mean)
    parts = [split3(mean) for mean in means]
    tail = [parts[g][term] for term in range(3) for g in range(2)]
    tail = jnp.concatenate(tail + [jnp.zeros((2, GW), F32)], axis=0).astype(BF16)
    for at, (a, b) in enumerate(((0, 0), (0, 1), (1, 1))):
        gram = lax.dot_general(
            zc_ref[a], zc_ref[b], (((0,), (0,)), ((), ())), preferred_element_type=F32
        ).astype(BF16)
        for j in range(PARTS):
            out_ref[j, at * PIECE:(at + 1) * PIECE] = gram[j * PIECE:(j + 1) * PIECE]
    for j in range(PARTS):
        out_ref[j, 3 * PIECE:3 * PIECE + TAIL] = tail


def all_means(r_ref):
    rows = r_ref[:, 3 * PIECE:3 * PIECE + TAIL].astype(F32)
    return [rows[:, g] + rows[:, 2 + g] + rows[:, 4 + g] for g in range(2)]


def deviation_kernel(j_ref, r_ref, wl_ref, e_ref, scratch_ref):
    row_at = j_ref[0] * PIECE
    means = all_means(r_ref)
    shifted = [m - jnp.mean(m, axis=0, keepdims=True) for m in means]
    total = jnp.sum(r_ref[:, 0:3 * PIECE].astype(F32), axis=0) * (1.0 / TOTAL)
    diagonal = (
        lax.broadcasted_iota(jnp.int32, (PIECE, GW), 0) + row_at
        == lax.broadcasted_iota(jnp.int32, (PIECE, GW), 1)
    )
    for at, (a, b) in enumerate(((0, 0), (0, 1), (1, 1))):
        scratch_ref[...] = lax.dot_general(
            shifted[a], shifted[b], (((0,), (0,)), ((), ())), precision=HIGHEST, preferred_element_type=F32
        )
        part = total[at * PIECE:(at + 1) * PIECE] + scratch_ref[pl.ds(row_at, PIECE), :] * (1.0 / PARTS)
        if a == b:
            packed = wl_ref[a, GW:GW + PROWS].astype(F32)
            part = part - jnp.where(diagonal, packed[3:4] + packed[7:8], 0.0)
        e_ref[at * PIECE:(at + 1) * PIECE] = part.astype(BF16)


def pull_kernel(j_ref, e_ref, r_ref, wl_ref, zc_ref, out_ref):
    means = all_means(r_ref)
    mine = r_ref[j_ref[0], 3 * PIECE:3 * PIECE + TAIL].astype(F32)
    mats = [e_ref[:, at * PIECE:(at + 1) * PIECE].reshape(GW, GW) for at in range(3)]
    whole = [m.astype(F32) for m in mats]
    loss = 0.25 * (
        jnp.sum(whole[0] * whole[0], keepdims=True)
        + 2.0 * jnp.sum(whole[1] * whole[1], keepdims=True)
        + jnp.sum(whole[2] * whole[2], keepdims=True)
    )
    away, offset = [], []
    for g in range(2):
        packed = wl_ref[g, GW:GW + PROWS].astype(F32)
        mean = jnp.mean(means[g], axis=0, keepdims=True)
        gap = mean - (packed[2:3] + packed[6:7])
        loss = loss + jnp.sum(gap * gap, keepdims=True)
        away.append(2.0 * gap)
        own = mine[g:g + 1] + mine[2 + g:3 + g] + mine[4 + g:5 + g]
        offset.append(jnp.broadcast_to(own - mean, (8, GW)))
    tail = [jnp.broadcast_to(part, (1, GW)) for part in split3(loss)]
    tail = jnp.concatenate(tail + [jnp.zeros((TAIL - 3, GW), F32)], axis=0).astype(BF16)
    tail = jnp.broadcast_to(tail[None], (CHIPS, TAIL, GW))
    plain, crossed = (((1,), (0,)), ((), ())), (((1,), (1,)), ((), ()))

    def product(lhs, rhs, dims, precision=None):
        return lax.dot_general(lhs, rhs, dims, precision=precision, preferred_element_type=F32)

    for g in range(2):
        first, second = (plain, crossed) if g == 0 else (plain, plain)
        at, bt = (0, 1) if g == 0 else (1, 2)
        row = (
            product(offset[0], whole[at], first, HIGHEST) + product(offset[1], whole[bt], second, HIGHEST)
        )[0:1] + away[g]
        pull = product(zc_ref[0], mats[at], first) + product(zc_ref[1], mats[bt], second) + row
        out_ref[:, g, 0:BROWS] = pull.astype(BF16).reshape(CHIPS, BROWS, GW)
        out_ref[:, g, BROWS:BROWS + TAIL] = tail


def backward_kernel(q_ref, slope_ref, w_ref, out_ref):
    loss = jnp.zeros((1, GW), F32)
    grad = None
    for layer in reversed(range(LAYERS)):
        rows = q_ref[layer, 0, BROWS:BROWS + TAIL].astype(F32)
        loss = loss + (rows[0:1] + rows[1:2] + rows[2:3])
        pull = q_ref[layer, :, 0:BROWS].reshape(ROWS, GW)
        if grad is not None:
            pull = (grad * slope_ref[layer] + pull.astype(F32)).astype(BF16)
        weight = w_ref[:, layer].reshape(GW, GW)
        grad = lax.dot_general(
            pull, weight, (((1,), (1,)), ((), ())), preferred_element_type=F32
        ).astype(BF16).astype(F32)
    tail = jnp.concatenate(list(split3(loss)) + [jnp.zeros((TAIL - 3, GW), F32)], axis=0).astype(BF16)
    grad = grad.astype(BF16)
    for b in range(2):
        for strip in range(4):
            at = b * BROWS + strip * 16
            out_ref[strip, b, 0:16] = grad[at:at + 16]
            out_ref[strip, b, 16:16 + TAIL] = tail


VMEM = pl.BlockSpec(memory_space=pltpu.VMEM)
SMEM = pl.BlockSpec(memory_space=pltpu.SMEM)


def kernel_call(kernel, outs, count, name, scalars=0, scratch=()):
    return pl.pallas_call(
        kernel,
        out_shape=[jax.ShapeDtypeStruct(shape, dtype) for shape, dtype in outs],
        in_specs=[SMEM] * scalars + [VMEM] * (count - scalars),
        out_specs=[VMEM] * len(outs),
        scratch_shapes=list(scratch),
        name=name,
    )


def shards(images, weights, bn_mean, bn_var, bn_gain, bn_bias):
    k, q, c = lax.axis_index("k"), lax.axis_index("q"), lax.axis_index("c")
    block = jnp.minimum(k, BLOCKS - 1)
    chip = lax.axis_index(("x", "y"))
    part = (q * 2 + c).astype(jnp.int32).reshape(1)

    scale = bn_gain[0] * lax.rsqrt(bn_var[0] + EPS)
    shift = bn_bias[0] - bn_mean[0] * scale
    packed = jnp.stack(split2(jnp.stack([scale, shift, bn_mean[0], bn_var[0]])))
    packed = packed.reshape(PROWS, BLOCKS, 2, GW)
    packed = lax.dynamic_index_in_dim(packed, c, 2, keepdims=False).transpose(1, 0, 2)
    slab = weights[0].reshape(BLOCKS, 2, GW, GW)
    slab = lax.dynamic_slice(slab, (0, c, chip * SLICE, 0), (BLOCKS, 1, SLICE, GW))[:, 0]
    message = jnp.concatenate([slab, packed], axis=1)
    message = jnp.concatenate([message, message[BLOCKS - 1:]], axis=0)
    message = jnp.broadcast_to(message[:, None], (4, 4, SLICE + PROWS, GW)).reshape(LAYERS, SLICE + PROWS, GW)
    layer_parts = lax.all_to_all(message, ("k", "q"), 0, 0, tiled=True)

    own = layer_parts[:, 0:SLICE]
    chain_weights = lax.all_to_all(
        jnp.broadcast_to(own[None], (CHIPS, LAYERS, SLICE, GW)), ("x", "y"), 0, 0, tiled=True
    )

    rows = lax.dynamic_index_in_dim(images[0].reshape(4, 4, 16, BLOCKS * 2 * GW), q, 1, keepdims=False)
    rows = lax.dynamic_index_in_dim(rows.reshape(BROWS, BLOCKS, 2, GW), block, 1, keepdims=False)
    rows = lax.all_to_all(rows.transpose(1, 0, 2), "c", 0, 0, tiled=True).reshape(ROWS, GW)

    xs, slope = kernel_call(
        forward_kernel, [((LAYERS, ROWS, GW), BF16), ((LAYERS, ROWS, GW), F32)], 3, "fwd"
    )(rows, chain_weights, layer_parts)

    home = lax.all_to_all(xs.reshape(2 * CHIPS, BROWS, GW), ("x", "y", "c"), 0, 0, tiled=True)
    mine = jnp.concatenate(
        [
            lax.dynamic_index_in_dim(chain_weights, chip, 1, keepdims=False).reshape(GW, GW),
            lax.dynamic_index_in_dim(layer_parts, chip, 0, keepdims=False)[SLICE:],
        ],
        axis=0,
    )
    both = lax.all_gather(mine, "c", axis=0)
    pieces, centered = kernel_call(
        gram_kernel, [((PARTS, 3 * PIECE + TAIL, GW), BF16), ((2, HOME, GW), BF16)], 2, "gram"
    )(home.reshape(CHIPS, 2, BROWS, GW), both)
    pieces = lax.all_to_all(pieces, ("q", "c"), 0, 0, tiled=True)
    (deviation,) = kernel_call(
        deviation_kernel, [((3 * PIECE, GW), BF16)], 3, "deviation", 1, [pltpu.VMEM((GW, GW), F32)]
    )(part, pieces, both)
    deviation = lax.all_gather(deviation, ("q", "c"), axis=0)
    (pulls,) = kernel_call(pull_kernel, [((CHIPS, 2, BROWS + TAIL, GW), BF16)], 5, "pull", 1)(
        part, deviation, pieces, both, centered
    )
    pulls = lax.all_to_all(pulls.reshape(2 * CHIPS, BROWS + TAIL, GW), ("x", "y", "c"), 0, 0, tiled=True)

    (grads,) = kernel_call(backward_kernel, [((4, 2, 16 + TAIL, GW), BF16)], 3, "bwd")(
        pulls.reshape(LAYERS, 2, BROWS + TAIL, GW), slope, chain_weights
    )
    grads = lax.all_to_all(grads.reshape(8, 16 + TAIL, GW), ("k", "c"), 0, 0, tiled=True)
    grads = grads.reshape(4, 2, 16 + TAIL, GW)[:BLOCKS]
    terms = grads[:, 0, 16:19, 0].astype(F32)
    loss = jnp.sum(terms) / (LAYERS * BLOCKS * 2 * GW)
    image_grad = grads[:, :, 0:16].transpose(2, 0, 1, 3).reshape(1, 16, BLOCKS * 2 * GW)
    return image_grad, loss


def solution(mesh):
    fine = Mesh(np.asarray(mesh.devices).reshape(4, 4, 4, 4, 2), ("k", "q", "x", "y", "c"))
    batch, section = ("x", "y", "c"), ("k", "q")
    return jax.shard_map(
        shards,
        mesh=fine,
        in_specs=(
            P(batch, None, None),
            P(section, None, None, None),
            P(section, None),
            P(section, None),
            P(section, None),
            P(section, None),
        ),
        out_specs=(P(batch, section, None), P()),
        check_vma=False,
    )
```

time: 885 us -> 199 us (0.22); the launches traced: 871 us -> 198 us
  waiting for transfers between devices: 415 us -> 38 us
  starting transfers between devices: 148 us -> 33.6 us
  other arithmetic: 70.8 us -> 2.22 us
  local copies, waits for them, and re-layouts: 62.6 us -> 6.55 us
  matrix products: 43.3 us -> 0 us
  Pallas kernels: 0 us -> 20.8 us
  blocking collectives: 112 us -> 94.5 us
  between operations: 17.1 us -> 2.55 us
    ppermute x46 -> x0, waiting for transfers between devices: 202 us -> none  [from_behind(): lax.ppermute(value, axis, [(source, source + steps) for source in range(f...]
    psum x1 -> x0, waiting for transfers between devices: 162 us -> none  [shards(): lax.psum(block_gram(flat_saved, batch_mean, BLOCK), 'batch') / row_total]
    ppermute x46 -> x0, starting transfers between devices: 148 us -> none  [from_behind(): lax.ppermute(value, axis, [(source, source + steps) for source in range(f...]
    psum x2 -> x0, blocking collectives: 112 us -> none  [the longest x1 91.5 us: shards(): total_sum = lax.psum(sum_pre, 'batch')]
    all_to_all x0 -> x3, blocking collectives: none -> 75.6 us  [the longest x1 33.9 us: shards(): lax.all_to_all(jnp.broadcast_to(own[None], (CHIPS, LAYERS, SLICE, GW)), (...]
    reduce_scatter x1 -> x0, waiting for transfers between devices: 50.5 us -> none  [shards(): lax.psum_scatter(own_term.astype(jnp.bfloat16), 'section', scatter_dimens...]
    dot_general x25 -> x0, matrix products: 43.3 us -> none  [the longest x8 15.4 us: backward_active_step(): jnp.einsum('rbi,bij->rbj', centered, deviation, precision=HIGHEST)]
    all_to_all x0 -> x4, waiting for transfers between devices: none -> 38 us  [the longest x1 13.2 us: shards(): lax.all_to_all(xs.reshape(2 * CHIPS, BROWS, GW), ('x', 'y', 'c'), 0, 0, t...]
  transfers between devices with their start and end apart: 48 -> 4, of which waited for: 48 -> 4; matrix products, arithmetic and copies ran while one was open for 5% -> 1% of each run, Pallas kernels for 0% -> 0%
where the time goes in v1:
time: 199 us; the launch traced here: 198 us
  blocking collectives  94.5 us (47%)
  waiting for transfers between devices  38 us (19%)
  starting transfers between devices  33.6 us (17%)
  Pallas kernels  20.8 us (10%)
  local copies, waits for them, and re-layouts  6.55 us (3%)
  between operations  2.55 us (1%)
  other arithmetic  2.22 us (1%)
    all_to_all x1, blocking collectives, shards(): lax.all_to_all(jnp.broadcast_to(own[None], (CHIPS, LAYERS, SLICE, GW)), (...  33.9 us
    all_to_all x1, blocking collectives, shards(): lax.all_to_all(pulls.reshape(2 * CHIPS, BROWS + TAIL, GW), ('x', 'y', 'c'...  23.5 us
    all_to_all x1, blocking collectives, shards(): lax.all_to_all(grads.reshape(8, 16 + TAIL, GW), ('k', 'c'), 0, 0, tiled=T...  18.2 us
    all_gather x1, blocking collectives, shards(): deviation = lax.all_gather(deviation, ('q', 'c'), axis=0)  16.8 us
    all_to_all x1, starting transfers between devices, shards(): layer_parts = lax.all_to_all(message, ('k', 'q'), 0, 0, tiled=True)  15.7 us
    all_to_all x1, waiting for transfers between devices, shards(): lax.all_to_all(xs.reshape(2 * CHIPS, BROWS, GW), ('x', 'y', 'c'), 0, 0, t...  13.2 us
    all_to_all x1, waiting for transfers between devices, shards(): pieces = lax.all_to_all(pieces, ('q', 'c'), 0, 0, tiled=True)  12 us
    all_to_all x1, waiting for transfers between devices, shards(): layer_parts = lax.all_to_all(message, ('k', 'q'), 0, 0, tiled=True)  11.7 us
  transfers between devices with their start and end apart: 4, of which 4 were waited for; matrix products, arithmetic and copies ran while one was open for 1% of the time, Pallas kernels for 0%

profile of v1, /device:TPU:1, one launch (start us, length us, event | category | flops | bytes accessed | tf_op | source)
XLA Modules:
  0.0 198.2 jit_solution(18140397241315372845)
XLA Ops:
  0.7 0.8 fusion.5
  1.5 0.7 reduce-precision_convert_fusion
  2.3 0.8 dynamic-slice_bitcast_fusion.1
  3.1 0.7 broadcast_in_dim.4
  3.8 15.7 %all-to-all-start.1 = ((bf16[16,24,256]{2,1,0:T(8,128)(2,1)}), bf16[16,24,256]{2,1,0:T(8,128)(2,1)S(1)}, u32[]{:S(2)}, u32[]{:S(2)}) async-start(bf16[16,24,256]{2,1,0:T(8,128)(2,1)} %bitcast.13), calls=%async_computation.1 | async-start | bytes 393216 | tf_op jit(solution)/shard_map/all_to_all | solution.py:191
  19.6 0.1 reshape.177
  19.6 0.1 constant_dynamic-slice_fusion.2
  19.7 0.6 copy.20
  20.4 11.7 %all-to-all-done.1.par_ref = bf16[16,24,256]{2,1,0:T(8,128)(2,1)S(1)} async-done(((bf16[16,24,256]{2,1,0:T(8,128)(2,1)}), bf16[16,24,256]{2,1,0:T(8,128)(2,1)S(1)}, u32[]{:S(2)}, u32[]{:S(2)}) %all-to-all-start.1) | async-done | bytes 196640 | tf_op jit(solution)/shard_map/all_to_all | solution.py:191
  32.0 8.1 %all-to-all-start = ((bf16[2,64,256]{2,1,0:T(8,128)(2,1)}), bf16[2,64,256]{2,1,0:T(8,128)(2,1)S(1)}, u32[]{:S(2)}, u32[]{:S(2)}) async-start(bf16[2,64,256]{2,1,0:T(8,128)(2,1)} %bitcast.40), calls=%async_computation | async-start | bytes 131072 | tf_op jit(solution)/shard_map/all_to_all | solution.py:200
  40.2 1.1 all-to-all-done
  41.2 0.2 broadcast_in_dim.5
  41.4 33.9 %all_to_all.35.w_ref = bf16[16,16,16,256]{3,2,1,0:T(8,128)(2,1)} all-to-all(bf16[16,16,16,256]{3,2,1,0:T(8,128)(2,1)S(1)} %broadcast_in_dim.5), channel_id=1, replica_groups=mesh['k'=4,'q'=4,'x'=4,'y'=4,'c'=2] {'x','y'}, dimensions={0} | all-to-all | bytes 4194304 | tf_op jit(solution)/shard_map/all_to_all | solution.py:194
  75.3 5.6 %fwd.1 = (bf16[16,128,256]{2,1,0:T(8,128)(2,1)}, f32[16,128,256]{2,1,0:T(8,128)}) custom-call(bf16[128,256]{1,0:T(8,128)(2,1)} %bitcast.54, bf16[16,16,16,256]{3,2,1,0:T(8,128)(2,1)} %all_to_all.35.w_ref, bf16[16,24,256]{2,1,0:T(8,128)(2,1)} %copy-done.3), custom_call_target="tpu_custom_call" | custom-call | tf_op jit(solution)/shard_map/fwd/pallas_call | solution.py:202
  81.0 5.6 %all-to-all-start.3 = ((bf16[32,64,256]{2,1,0:T(8,128)(2,1)}), bf16[32,64,256]{2,1,0:T(8,128)(2,1)S(1)}, u32[]{:S(2)}, u32[]{:S(2)}) async-start(bf16[32,64,256]{2,1,0:T(8,128)(2,1)} %bitcast.51), calls=%async_computation.3 | async-start | bytes 2097152 | tf_op jit(solution)/shard_map/all_to_all | solution.py:206
  86.6 0.7 dynamic-slice_bitcast_fusion.2
  87.3 0.9 constant_dynamic-slice_fusion
  88.2 2.1 %all-gather = bf16[528,256]{1,0:T(8,128)(2,1)} all-gather(bf16[264,256]{1,0:T(8,128)(2,1)S(1)} %pad_maximum_fusion), channel_id=2, replica_groups=mesh['k'=4,'q'=4,'x'=4,'y'=4,'c'=2] {'c'}, dimensions={0}, use_global_device_ids=true | all-gather | bytes 405504 | tf_op jit(solution)/shard_map/all_gather | solution.py:214
  90.4 13.2 %all-to-all-done.3 = bf16[32,64,256]{2,1,0:T(8,128)(2,1)S(1)} async-done(((bf16[32,64,256]{2,1,0:T(8,128)(2,1)}), bf16[32,64,256]{2,1,0:T(8,128)(2,1)S(1)}, u32[]{:S(2)}, u32[]{:S(2)}) %all-to-all-start.3) | async-done | bytes 1048608 | tf_op jit(solution)/shard_map/all_to_all | solution.py:206
  103.6 1.0 copy-done.1
  104.6 3.4 %gram.1 = (bf16[8,104,256]{2,1,0:T(8,128)(2,1)}, bf16[2,1024,256]{2,1,0:T(8,128)(2,1)}) custom-call(bf16[16,2,64,256]{3,2,1,0:T(8,128)(2,1)} %bitcast.49, bf16[2,264,256]{2,1,0:T(8,128)(2,1)} %bitcast.46), custom_call_target="tpu_custom_call" | custom-call | tf_op jit(solution)/shard_map/gram/pallas_call | solution.py:215
  108.0 4.1 %all-to-all-start.4 = ((bf16[8,104,256]{2,1,0:T(8,128)(2,1)}), bf16[8,104,256]{2,1,0:T(8,128)(2,1)S(1)}, u32[]{:S(2)}, u32[]{:S(2)}) async-start(bf16[8,104,256]{2,1,0:T(8,128)(2,1)} %get-tuple-element.7), calls=%async_computation.4 | async-start | bytes 851968 | tf_op jit(solution)/shard_map/all_to_all | solution.py:218
  112.1 12.0 %all-to-all-done.4.r_ref = bf16[8,104,256]{2,1,0:T(8,128)(2,1)S(1)} async-done(((bf16[8,104,256]{2,1,0:T(8,128)(2,1)}), bf16[8,104,256]{2,1,0:T(8,128)(2,1)S(1)}, u32[]{:S(2)}, u32[]{:S(2)}) %all-to-all-start.4) | async-done | bytes 426016 | tf_op jit(solution)/shard_map/all_to_all | solution.py:218
  124.1 0.8 copy-done.2
  124.9 2.6 %deviation.1 = bf16[96,256]{1,0:T(8,128)(2,1)} custom-call(s32[1]{0:T(128)} %bitcast.j_ref, bf16[8,104,256]{2,1,0:T(8,128)(2,1)} %copy-done.2, bf16[2,264,256]{2,1,0:T(8,128)(2,1)} %bitcast.47), custom_call_target="tpu_custom_call" | custom-call | tf_op jit(solution)/shard_map/deviation/pallas_call | solution.py:219
  127.5 16.8 %all-gather.1 = bf16[768,256]{1,0:T(8,128)(2,1)} all-gather(bf16[96,256]{1,0:T(8,128)(2,1)} %deviation.1), channel_id=3, replica_groups=mesh['k'=4,'q'=4,'x'=4,'y'=4,'c'=2] {'q','c'}, dimensions={0}, use_global_device_ids=true | all-gather | bytes 442368 | tf_op jit(solution)/shard_map/all_gather | solution.py:222
  144.3 3.9 %pull.1 = bf16[16,2,72,256]{3,2,1,0:T(8,128)(2,1)} custom-call(s32[1]{0:T(128)} %bitcast.j_ref, bf16[8,96,256]{2,1,0:T(8,128)(2,1)} %bitcast.50, bf16[8,104,256]{2,1,0:T(8,128)(2,1)} %copy-done.2, bf16[2,264,256]{2,1,0:T(8,128)(2,1)} %bitcast.48, bf16[2,1024,256]{2,1,0:T(8,128)(2,1)} %get-tuple-element.8.zc_ref), custom_call_target="tpu_custom_call" | custom-call | tf_op jit(solution)/shard_map/pull/pallas_call | solution.py:223
  148.2 23.5 %all_to_all.36 = bf16[32,72,256]{2,1,0:T(8,128)(2,1)} all-to-all(bf16[32,72,256]{2,1,0:T(8,128)(2,1)} %bitcast.44), channel_id=1, replica_groups=mesh['k'=4,'q'=4,'x'=4,'y'=4,'c'=2] {'x','y','c'}, dimensions={0} | all-to-all | bytes 2359296 | tf_op jit(solution)/shard_map/all_to_all | solution.py:226
  171.7 5.3 %bwd.1 = bf16[4,2,24,256]{3,2,1,0:T(8,128)(2,1)} custom-call(bf16[16,2,72,256]{3,2,1,0:T(8,128)(2,1)} %bitcast.45, f32[16,128,256]{2,1,0:T(8,128)} %get-tuple-element.9.slope_ref, bf16[16,16,16,256]{3,2,1,0:T(8,128)(2,1)} %all_to_all.35.w_ref), custom_call_target="tpu_custom_call" | custom-call | tf_op jit(solution)/shard_map/bwd/pallas_call | solution.py:228
  177.0 18.2 %all_to_all.37 = bf16[8,24,256]{2,1,0:T(8,128)(2,1)S(1)} all-to-all(bf16[8,24,256]{2,1,0:T(8,128)(2,1)} %bitcast.53), channel_id=1, replica_groups=mesh['k'=4,'q'=4,'x'=4,'y'=4,'c'=2] {'k','c'}, dimensions={0} | all-to-all | bytes 196608 | tf_op jit(solution)/shard_map/all_to_all | solution.py:231
  195.1 0.6 convert_reduce_fusion
  195.8 0.7 reshape.187
  (19 shorter events, 0.2 us)
Async XLA Ops:
  0.6 18.9 %copy-start = (bf16[1,256,1536]{2,1,0:T(8,128)(2,1)S(1)}, bf16[1,256,1536]{2,1,0:T(8,128)(2,1)}, u32[]{:S(2)}) copy-start(bf16[1,256,1536]{2,1,0:T(8,128)(2,1)} %param.6) | copy-start | bytes 2359300
  3.8 28.2 %all-to-all-start.1 = ((bf16[16,24,256]{2,1,0:T(8,128)(2,1)}), bf16[16,24,256]{2,1,0:T(8,128)(2,1)S(1)}, u32[]{:S(2)}, u32[]{:S(2)}) async-start(bf16[16,24,256]{2,1,0:T(8,128)(2,1)} %bitcast.13), calls=%async_computation.1 | async-start | bytes 393216 | tf_op jit(solution)/shard_map/all_to_all | solution.py:191
  32.0 43.3 %copy-start.3 = (bf16[16,24,256]{2,1,0:T(8,128)(2,1)}, bf16[16,24,256]{2,1,0:T(8,128)(2,1)S(1)}, u32[]{:S(2)}) copy-start(bf16[16,24,256]{2,1,0:T(8,128)(2,1)S(1)} %all-to-all-done.1.par_ref) | copy-start | bytes 589828
  32.0 9.2 %all-to-all-start = ((bf16[2,64,256]{2,1,0:T(8,128)(2,1)}), bf16[2,64,256]{2,1,0:T(8,128)(2,1)S(1)}, u32[]{:S(2)}, u32[]{:S(2)}) async-start(bf16[2,64,256]{2,1,0:T(8,128)(2,1)} %bitcast.40), calls=%async_computation | async-start | bytes 131072 | tf_op jit(solution)/shard_map/all_to_all | solution.py:200
  41.2 34.1 %copy-start.4 = (bf16[2,64,256]{2,1,0:T(8,128)(2,1)}, bf16[2,64,256]{2,1,0:T(8,128)(2,1)S(1)}, u32[]{:S(2)}) copy-start(bf16[2,64,256]{2,1,0:T(8,128)(2,1)S(1)} %all-to-all-done) | copy-start | bytes 196612
  81.0 22.7 %all-to-all-start.3 = ((bf16[32,64,256]{2,1,0:T(8,128)(2,1)}), bf16[32,64,256]{2,1,0:T(8,128)(2,1)S(1)}, u32[]{:S(2)}, u32[]{:S(2)}) async-start(bf16[32,64,256]{2,1,0:T(8,128)(2,1)} %bitcast.51), calls=%async_computation.3 | async-start | bytes 2097152 | tf_op jit(solution)/shard_map/all_to_all | solution.py:206
  103.6 1.0 copy-start.1
  108.0 16.1 %all-to-all-start.4 = ((bf16[8,104,256]{2,1,0:T(8,128)(2,1)}), bf16[8,104,256]{2,1,0:T(8,128)(2,1)S(1)}, u32[]{:S(2)}, u32[]{:S(2)}) async-start(bf16[8,104,256]{2,1,0:T(8,128)(2,1)} %get-tuple-element.7), calls=%async_computation.4 | async-start | bytes 851968 | tf_op jit(solution)/shard_map/all_to_all | solution.py:218
  124.1 0.8 copy-start.2

commit v2 on v1

v2 whole, which is shorter than its diff:
```python
import math

import jax
import jax.numpy as jnp
import numpy as np
from jax import lax
from jax.experimental import pallas as pl
from jax.experimental.pallas import tpu as pltpu
from jax.sharding import Mesh, PartitionSpec as P

EPS = 1e-05
HIGHEST = lax.Precision.HIGHEST
F32 = jnp.float32
BF16 = jnp.bfloat16

LAYERS = 16
GW = 256
BLOCKS = 3
CHIPS = 16
SLICE = GW // (2 * CHIPS)
PROWS = 8
ROWS = 128
HALF = ROWS // 2
HOME = CHIPS * HALF
LANES = 128
PARTS = 8
PIECE = GW // PARTS
TAIL = 8
TOTAL = HOME * PARTS


def split3(value):
    high = value.astype(BF16).astype(F32)
    rest = value - high
    middle = rest.astype(BF16).astype(F32)
    return high, middle, rest - middle


def pack_kernel(w_ref, images_ref, mean_ref, var_ref, gain_ref, bias_ref, out_ref, x_ref, slab_ref, sems):
    chip = lax.axis_index("x") * 4 + lax.axis_index("y")
    row = (lax.axis_index("c") * CHIPS + chip) * SLICE
    half = lax.axis_index("h")
    group = 2 * jnp.minimum(lax.axis_index("k"), BLOCKS - 1) + lax.axis_index("g")
    slab = pltpu.make_async_copy(w_ref.at[0, :, pl.ds(pl.multiple_of(row, SLICE), SLICE), :], slab_ref, sems.at[0])
    slab.start()
    copies = []
    for strip in range(4):
        source = images_ref.at[
            0, pl.ds(pl.multiple_of(strip * 64 + half * 32, 32), 32), pl.ds(pl.multiple_of(group * GW, GW), GW)
        ]
        copies.append(pltpu.make_async_copy(source, x_ref.at[strip * 32:strip * 32 + 32], sems.at[1 + strip]))
        copies[-1].start()
    scale = gain_ref[...] * lax.rsqrt(var_ref[...] + EPS)
    packed = [scale, bias_ref[...] - mean_ref[...] * scale, mean_ref[...], var_ref[...]]
    high = [value.astype(BF16).astype(F32) for value in packed]
    packed = jnp.concatenate(high + [value - top for value, top in zip(packed, high)], axis=0).astype(BF16)
    slab.wait()
    for k in range(4):
        for g in range(2):
            at = 2 * min(k, BLOCKS - 1) + g
            for h in range(2):
                out_ref[k, h, g, 0:SLICE] = slab_ref[at]
                out_ref[k, h, g, SLICE:] = packed[:, at * GW:(at + 1) * GW]
    for copy in copies:
        copy.wait()


def in_order(own, other, core):
    return jnp.concatenate([lax.select(core == 0, own, other), lax.select(core == 0, other, own)], axis=0)


def layer_weight(own_ref, other_ref, core, layer):
    return in_order(own_ref[:, layer].reshape(GW // 2, GW), other_ref[:, layer].reshape(GW // 2, GW), core)


def forward_kernel(j_ref, x_ref, par_ref, own_ref, other_ref, xs_ref, slope_ref):
    core = j_ref[0] % 2
    x = x_ref[...]
    for layer in range(LAYERS):
        xs_ref[layer] = x
        weight = layer_weight(own_ref, other_ref, core, layer)
        packed = par_ref[layer, SLICE:SLICE + PROWS].astype(F32)
        scale = packed[0:1] + packed[4:5]
        shift = packed[1:2] + packed[5:6]
        active = jnp.dot(x, weight, preferred_element_type=F32) * scale + shift
        gate = 1.0 / (1.0 + jnp.exp(-active))
        x = (active * gate).astype(BF16)
        slope_ref[layer] = (gate * (1.0 + active * (1.0 - gate)) * scale).astype(BF16)


def gram_kernel(j_ref, x_ref, mine_ref, theirs_ref, keep_ref, send_ref, tail_ref, par_ref, zc_ref):
    core, side = j_ref[0] % 2, j_ref[0] // 2 % 2
    means = []
    for g in range(2):
        layer = lax.select(side == g, mine_ref[...], theirs_ref[...])
        packed = layer[GW:].astype(F32)
        par_ref[g] = packed[0:4] + packed[4:8]
        weight = in_order(layer[0:GW // 2], layer[GW // 2:GW], core)
        z = jnp.dot(x_ref[:, g].reshape(HOME, GW), weight, preferred_element_type=F32)
        mean = jnp.sum(z, axis=0, keepdims=True) * (1.0 / HOME)
        zc_ref[g] = (z - mean).astype(BF16)
        means.append(mean)
    parts = [split3(mean) for mean in means]
    tail = [parts[g][term] for term in range(3) for g in range(2)]
    tail = jnp.concatenate(tail + [jnp.zeros((2, GW), F32)], axis=0).astype(BF16)
    tail_ref[...] = tail
    send_ref[4 * 3 * PIECE:] = tail
    for at, (a, b) in enumerate(((0, 0), (0, 1), (1, 1))):
        gram = lax.dot_general(zc_ref[a], zc_ref[b], (((0,), (0,)), ((), ())), preferred_element_type=F32)
        low, high = gram[0:GW // 2], gram[GW // 2:]
        keep, send = lax.select(core == 0, low, high), lax.select(core == 0, high, low).astype(BF16)
        for j in range(4):
            rows = pl.ds((3 * j + at) * PIECE, PIECE)
            keep_ref[rows] = keep[j * PIECE:(j + 1) * PIECE]
            send_ref[rows] = send[j * PIECE:(j + 1) * PIECE]


def chip_kernel(j_ref, keep_ref, tail_ref, got_ref, out_ref):
    core = j_ref[0] % 2
    tails = in_order(tail_ref[...], got_ref[4 * 3 * PIECE:], core)
    for j in range(4):
        rows = pl.ds(3 * j * PIECE, 3 * PIECE)
        out_ref[j, 0:3 * PIECE] = (keep_ref[rows] + got_ref[rows].astype(F32)).astype(BF16)
        out_ref[j, 3 * PIECE:] = tails


def mean_of(rows, g):
    return rows[..., g, :] + rows[..., 2 + g, :] + rows[..., 4 + g, :]


def all_means(r_ref):
    rows = r_ref[:, 3 * PIECE:].astype(F32)
    cores = rows[:, 0:TAIL], rows[:, TAIL:]
    return [jnp.concatenate([mean_of(core, g) for core in cores], axis=0) for g in range(2)]


def deviation_kernel(j_ref, r_ref, par_ref, e_ref, scratch_ref):
    row_at = (j_ref[0] % 2 * 4 + j_ref[0] // 2) * PIECE
    means = all_means(r_ref)
    shifted = [m - jnp.mean(m, axis=0, keepdims=True) for m in means]
    total = jnp.sum(r_ref[:, 0:3 * PIECE].astype(F32), axis=0) * (1.0 / TOTAL)
    diagonal = (
        lax.broadcasted_iota(jnp.int32, (PIECE, GW), 0) + row_at
        == lax.broadcasted_iota(jnp.int32, (PIECE, GW), 1)
    )
    for at, (a, b) in enumerate(((0, 0), (0, 1), (1, 1))):
        scratch_ref[...] = lax.dot_general(
            shifted[a], shifted[b], (((0,), (0,)), ((), ())), precision=HIGHEST, preferred_element_type=F32
        )
        part = total[at * PIECE:(at + 1) * PIECE] + scratch_ref[pl.ds(row_at, PIECE), :] * (1.0 / PARTS)
        if a == b:
            part = part - jnp.where(diagonal, par_ref[a, 3:4], 0.0)
        for j in range(4):
            e_ref[j, at * PIECE:(at + 1) * PIECE] = part.astype(BF16)


def pull_kernel(e_ref, r_ref, tail_ref, par_ref, zc_ref, out_ref):
    means = all_means(r_ref)
    mine = tail_ref[...].astype(F32)
    mats = [e_ref[:, :, at * PIECE:(at + 1) * PIECE].reshape(GW, GW) for at in range(3)]
    whole = [m.astype(F32) for m in mats]
    loss = 0.25 * (
        jnp.sum(whole[0] * whole[0], keepdims=True)
        + 2.0 * jnp.sum(whole[1] * whole[1], keepdims=True)
        + jnp.sum(whole[2] * whole[2], keepdims=True)
    )
    away, offset = [], []
    for g in range(2):
        mean = jnp.mean(means[g], axis=0, keepdims=True)
        gap = mean - par_ref[g, 2:3]
        loss = loss + jnp.sum(gap * gap, keepdims=True)
        away.append(2.0 * gap)
        own = mine[g:g + 1] + mine[2 + g:3 + g] + mine[4 + g:5 + g]
        offset.append(jnp.concatenate(list(split3(own - mean)) + [jnp.zeros((13, GW), F32)], axis=0).astype(BF16))
    tail = [jnp.broadcast_to(part, (1, LANES)) for part in split3(loss)]
    tail = jnp.concatenate(tail + [jnp.zeros((TAIL - 3, LANES), F32)], axis=0).astype(BF16)
    tail = jnp.broadcast_to(tail[None], (CHIPS, TAIL, LANES))
    plain, crossed = (((1,), (0,)), ((), ())), (((1,), (1,)), ((), ()))

    def product(side, at, dims):
        lhs = jnp.concatenate([zc_ref[side], offset[side]], axis=0)
        return lax.dot_general(lhs, mats[at], dims, preferred_element_type=F32)

    for g in range(2):
        pull = product(0, 0, plain) + product(1, 1, crossed) if g == 0 else product(0, 1, plain) + product(1, 2, plain)
        row = pull[HOME:HOME + 1] + pull[HOME + 1:HOME + 2] + pull[HOME + 2:HOME + 3] + away[g]
        pull = pull[0:HOME] + row
        pull = pull.astype(BF16).reshape(CHIPS, HALF, GW)
        out_ref[:, g, 0:HALF] = pull[:, :, 0:LANES]
        out_ref[:, g, HALF:2 * HALF] = pull[:, :, LANES:]
        out_ref[:, g, 2 * HALF:] = tail


def backward_kernel(j_ref, q_ref, slope_ref, own_ref, other_ref, out_ref):
    core = j_ref[0] % 2
    loss = jnp.zeros((1, LANES), F32)
    grad = None
    for layer in reversed(range(LAYERS)):
        rows = q_ref[layer, 0, 2 * HALF:].astype(F32)
        loss = loss + (rows[0:1] + rows[1:2] + rows[2:3])
        pull = jnp.concatenate(
            [q_ref[layer, :, 0:HALF].reshape(ROWS, LANES), q_ref[layer, :, HALF:2 * HALF].reshape(ROWS, LANES)], axis=1
        )
        if grad is not None:
            pull = (grad * slope_ref[layer].astype(F32) + pull.astype(F32)).astype(BF16)
        grad = lax.dot_general(
            pull, layer_weight(own_ref, other_ref, core, layer), (((1,), (1,)), ((), ())), preferred_element_type=F32
        ).astype(BF16).astype(F32)
    loss = jnp.concatenate([loss, loss], axis=1)
    tail = jnp.concatenate(list(split3(loss)) + [jnp.zeros((TAIL - 3, GW), F32)], axis=0).astype(BF16)
    grad = grad.astype(BF16)
    for strip in range(8):
        out_ref[strip, 0:16] = grad[strip * 16:strip * 16 + 16]
        out_ref[strip, 16:16 + TAIL] = tail


def output_kernel(r_ref, grad_ref, loss_ref):
    loss = jnp.zeros((1, 1), F32)
    for k in range(BLOCKS):
        for g in range(2):
            at = 2 * k + g
            grad_ref[0, :, at * GW:(at + 1) * GW] = r_ref[at, 0:16]
        loss = loss + jnp.sum(r_ref[2 * k, 16:16 + TAIL].astype(F32)[0:3, 0:1], axis=0, keepdims=True)
    loss_ref[...] = loss * (1.0 / (LAYERS * BLOCKS * 2 * GW))


LARGE = 1100000


def is_large(shape, dtype):
    return math.prod(shape) * jnp.dtype(dtype).itemsize > LARGE


def kernel_call(kernel, outs, name, *args, scalars=(), scratch=(), far=(), loose=()):
    vmem = pl.BlockSpec(memory_space=pltpu.VMEM)
    smem = pl.BlockSpec(memory_space=pltpu.SMEM)
    placed = [arg if is_large(arg.shape, arg.dtype) else pltpu.with_memory_space_constraint(arg, pltpu.VMEM) for arg in args]
    placed += [pltpu.with_memory_space_constraint(arg, pltpu.HBM) for arg in far]
    return pl.pallas_call(
        kernel,
        out_shape=[jax.ShapeDtypeStruct(*out) if is_large(*out) else pltpu.VMEM(*out) for out in outs] + list(loose),
        in_specs=[smem] * len(scalars) + [vmem] * len(placed),
        out_specs=[vmem] * (len(outs) + len(loose)),
        scratch_shapes=list(scratch),
        name=name,
    )(*scalars, *placed)


def shards(images, weights, bn_mean, bn_var, bn_gain, bn_bias):
    chip = lax.axis_index(("x", "y"))
    part = lax.axis_index(("h", "g", "c")).astype(jnp.int32).reshape(1)

    hbm, vmem = pl.BlockSpec(memory_space=pl.ANY), pl.BlockSpec(memory_space=pltpu.VMEM)
    message, rows = pl.pallas_call(
        pack_kernel,
        out_shape=[pltpu.VMEM((4, 2, 2, SLICE + PROWS, GW), BF16), pltpu.VMEM((ROWS, GW), BF16)],
        in_specs=[hbm, hbm] + [vmem] * 4,
        out_specs=[vmem, vmem],
        scratch_shapes=[pltpu.VMEM((2 * BLOCKS, SLICE, GW), BF16), pltpu.SemaphoreType.DMA((5,))],
        name="pack",
    )(weights, images, bn_mean, bn_var, bn_gain, bn_bias)
    message = message.reshape(LAYERS, SLICE + PROWS, GW)
    layer_parts = lax.all_to_all(message, ("k", "h", "g"), 0, 0, tiled=True)

    own = layer_parts[:, 0:SLICE]
    own = lax.all_to_all(jnp.broadcast_to(own[None], (CHIPS, LAYERS, SLICE, GW)), ("x", "y"), 0, 0, tiled=True)
    other = lax.ppermute(own, "c", [(0, 1), (1, 0)])

    xs, slope = kernel_call(
        forward_kernel,
        [],
        "fwd",
        rows,
        layer_parts,
        scalars=[part],
        far=[own, other],
        loose=[jax.ShapeDtypeStruct((LAYERS, ROWS, GW), BF16)] * 2,
    )

    home = lax.all_to_all(xs.reshape(2 * CHIPS, HALF, GW), ("x", "y", "g"), 0, 0, tiled=True)
    mine = jnp.concatenate(
        [
            lax.dynamic_index_in_dim(own, chip, 1, keepdims=False).reshape(GW // 2, GW),
            lax.dynamic_index_in_dim(other, chip, 1, keepdims=False).reshape(GW // 2, GW),
            lax.dynamic_index_in_dim(layer_parts, chip, 0, keepdims=False)[SLICE:],
        ],
        axis=0,
    )
    mine = lax.optimization_barrier((mine, xs))[0]
    theirs = lax.ppermute(mine, "g", [(0, 1), (1, 0)])
    keep, send, tail, params, centered = kernel_call(
        gram_kernel,
        [
            ((4 * 3 * PIECE, GW), F32),
            ((4 * 3 * PIECE + TAIL, GW), BF16),
            ((TAIL, GW), BF16),
            ((2, 4, GW), F32),
        ],
        "gram",
        home.reshape(CHIPS, 2, HALF, GW),
        mine,
        theirs,
        scalars=[part],
        loose=[jax.ShapeDtypeStruct((2, HOME, GW), BF16)],
    )
    got = lax.ppermute(send, "c", [(0, 1), (1, 0)])
    (pieces,) = kernel_call(
        chip_kernel, [((4, 3 * PIECE + 2 * TAIL, GW), BF16)], "chip", keep, tail, got, scalars=[part]
    )
    pieces = lax.all_to_all(pieces, ("h", "g"), 0, 0, tiled=True)
    (deviation,) = kernel_call(
        deviation_kernel,
        [((4, 3 * PIECE, GW), BF16)],
        "deviation",
        pieces,
        params,
        scalars=[part],
        scratch=[pltpu.VMEM((GW, GW), F32)],
    )
    deviation = lax.all_gather(lax.all_to_all(deviation, ("h", "g"), 0, 0, tiled=True), "c", axis=0)
    (pulls,) = kernel_call(
        pull_kernel,
        [((CHIPS, 2, 2 * HALF + TAIL, LANES), BF16)],
        "pull",
        deviation,
        pieces,
        tail,
        params,
        far=[centered],
    )
    pulls = lax.all_to_all(pulls.reshape(2 * CHIPS, 2 * HALF + TAIL, LANES), ("x", "y", "g"), 0, 0, tiled=True)

    (grads,) = kernel_call(
        backward_kernel,
        [((8, 16 + TAIL, GW), BF16)],
        "bwd",
        pulls.reshape(LAYERS, 2, 2 * HALF + TAIL, LANES),
        scalars=[part],
        far=[slope, own, other],
    )
    grads = lax.all_to_all(grads, ("k", "g"), 0, 0, tiled=True)
    image_grad, loss = pl.pallas_call(
        output_kernel,
        out_shape=[jax.ShapeDtypeStruct((1, 16, BLOCKS * 2 * GW), BF16), jax.ShapeDtypeStruct((1, 1), F32)],
        in_specs=[vmem],
        out_specs=[vmem, vmem],
        name="outputs",
    )(pltpu.with_memory_space_constraint(grads, pltpu.VMEM))
    return image_grad, loss.reshape(())


def solution(mesh):
    fine = Mesh(np.asarray(mesh.devices).reshape(4, 2, 2, 4, 4, 2), ("k", "h", "g", "x", "y", "c"))
    batch, section = ("x", "y", "c"), ("k", "h", "g")
    return jax.shard_map(
        shards,
        mesh=fine,
        in_specs=(
            P(batch, None, None),
            P(section, None, None, None),
            P(section, None),
            P(section, None),
            P(section, None),
            P(section, None),
        ),
        out_specs=(P(batch, section, None), P()),
        check_vma=False,
    )
```

time: 199 us -> 169 us (0.85)
  waiting for transfers between devices: 38 us -> 15.5 us
  blocking collectives: 94.5 us -> 112 us
  starting transfers between devices: 33.6 us -> 19.3 us
  local copies, waits for them, and re-layouts: 6.55 us -> 2.8 us
  Pallas kernels: 20.8 us -> 17.7 us
  other arithmetic: 2.22 us -> 0.01 us
    all_to_all x2 -> x5, blocking collectives: 41.7 us -> 87.5 us  [the longest x1 27.5 us: shards(): layer_parts = lax.all_to_all(message, ('k', 'h', 'g'), 0, 0, tiled=True)]
    all_to_all x4 -> x1, waiting for transfers between devices: 38 us -> 1.4 us  [shards(): lax.all_to_all(xs.reshape(2 * CHIPS, HALF, GW), ('x', 'y', 'g'), 0, 0, ti...]
    all_to_all x4 -> x1, starting transfers between devices: 33.6 us -> 4.49 us  [shards(): lax.all_to_all(xs.reshape(2 * CHIPS, HALF, GW), ('x', 'y', 'g'), 0, 0, ti...]
    ppermute x0 -> x3, starting transfers between devices: none -> 14.8 us  [the longest x1 6.91 us: shards(): other = lax.ppermute(own, 'c', [(0, 1), (1, 0)])]
    all_to_all x1, blocking collectives: 33.9 us -> 19.6 us  [shards(): lax.all_to_all(jnp.broadcast_to(own[None], (CHIPS, LAYERS, SLICE, GW)), (...]
    all_gather x2 -> x1, blocking collectives: 18.9 us -> 4.67 us  [shards(): lax.all_gather(lax.all_to_all(deviation, ('h', 'g'), 0, 0, tiled=True), '...]
    ppermute x0 -> x3, waiting for transfers between devices: none -> 14.1 us  [the longest x1 10.8 us: shards(): theirs = lax.ppermute(mine, 'g', [(0, 1), (1, 0)])]
    pallas_call x5 -> x8, Pallas kernels: 20.8 us -> 17.7 us  [the longest x6 15.5 us: kernel_call(): pl.pallas_call(kernel, out_shape=[jax.ShapeDtypeStruct(*out) if is_large(...]
where the time goes in v2:
time: 169 us; the launch traced here: 168 us
  blocking collectives  112 us (66%)
  starting transfers between devices  19.3 us (11%)
  Pallas kernels  17.7 us (10%)
  waiting for transfers between devices  15.5 us (9%)
  local copies, waits for them, and re-layouts  2.8 us (2%)
    all_to_all x1, blocking collectives, shards(): layer_parts = lax.all_to_all(message, ('k', 'h', 'g'), 0, 0, tiled=True)  27.5 us
    all_to_all x1, blocking collectives, shards(): lax.all_to_all(pulls.reshape(2 * CHIPS, 2 * HALF + TAIL, LANES), ('x', 'y...  22.6 us
    all_to_all x1, blocking collectives, shards(): lax.all_to_all(jnp.broadcast_to(own[None], (CHIPS, LAYERS, SLICE, GW)), (...  19.6 us
    all_to_all x1, blocking collectives, shards(): grads = lax.all_to_all(grads, ('k', 'g'), 0, 0, tiled=True)  18.2 us
    pallas_call x6, Pallas kernels, kernel_call(): pl.pallas_call(kernel, out_shape=[jax.ShapeDtypeStruct(*out) if is_large(...  15.5 us
    ppermute x1, waiting for transfers between devices, shards(): theirs = lax.ppermute(mine, 'g', [(0, 1), (1, 0)])  10.8 us
    all_to_all x1, blocking collectives, shards(): pieces = lax.all_to_all(pieces, ('h', 'g'), 0, 0, tiled=True)  9.72 us
    all_to_all x1, blocking collectives, shards(): lax.all_to_all(deviation, ('h', 'g'), 0, 0, tiled=True)  9.46 us
  transfers between devices with their start and end apart: 4, of which 4 were waited for; matrix products, arithmetic and copies ran while one was open for 1% of the time, Pallas kernels for 0%

profile of v2, /device:TPU:1, one launch (start us, length us, event | category | flops | bytes accessed | tf_op | source)
XLA Modules:
  0.0 167.8 jit_solution(1829106935478767685)
XLA Ops:
  0.6 1.6 pack.1
  2.2 27.5 %all_to_all.35.par_ref = bf16[16,16,256]{2,1,0:T(8,128)(2,1)S(1)} all-to-all(bf16[16,16,256]{2,1,0:T(8,128)(2,1)S(1)} %bitcast.16), channel_id=1, replica_groups=mesh['k'=4,'h'=2,'g'=2,'x'=4,'y'=4,'c'=2] {'k','h','g'}, dimensions={0} | all-to-all | bytes 262144 | tf_op jit(solution)/shard_map/all_to_all | solution.py:263
  29.8 0.1 broadcast_in_dim.2
  29.9 19.6 %all_to_all.36.own_ref = bf16[16,16,8,256]{3,2,1,0:T(8,128)(2,1)S(1)} all-to-all(bf16[16,16,8,256]{3,2,1,0:T(8,128)(2,1)S(1)} %broadcast_in_dim.2), channel_id=1, replica_groups=mesh['k'=4,'h'=2,'g'=2,'x'=4,'y'=4,'c'=2] {'x','y'}, dimensions={0} | all-to-all | bytes 2097152 | tf_op jit(solution)/shard_map/all_to_all | solution.py:266
  49.5 0.0 copy-start
  49.5 6.9 %collective-permute-start = (bf16[16,16,8,256]{3,2,1,0:T(8,128)(2,1)S(1)}, bf16[16,16,8,256]{3,2,1,0:T(8,128)(2,1)S(1)}, u32[]{:S(2)}, u32[]{:S(2)}) collective-permute-start(bf16[16,16,8,256]{3,2,1,0:T(8,128)(2,1)S(1)} %all_to_all.36.own_ref), channel_id=1, source_target_pairs={{0,1},{1,0},{2,3},{3,2},{4,5},{5,4},{6,7},{7,6},{8,9},{9,8},{10,11... | collective-permute-start | bytes 3145736 | tf_op jit(solution)/shard_map/ppermute | solution.py:267
  56.4 2.3 %collective-permute-done.other_ref = bf16[16,16,8,256]{3,2,1,0:T(8,128)(2,1)S(1)} collective-permute-done((bf16[16,16,8,256]{3,2,1,0:T(8,128)(2,1)S(1)}, bf16[16,16,8,256]{3,2,1,0:T(8,128)(2,1)S(1)}, u32[]{:S(2)}, u32[]{:S(2)}) %collective-permute-start) | collective-permute-done | bytes 1048608 | tf_op jit(solution)/shard_map/ppermute | solution.py:267
  58.6 0.0 copy-start.1
  58.6 0.0 copy-done
  58.6 1.0 copy-done.1
  59.6 5.2 %fwd.1 = (bf16[16,128,256]{2,1,0:T(8,128)(2,1)}, bf16[16,128,256]{2,1,0:T(8,128)(2,1)}) custom-call(s32[1]{0:T(128)} %bitcast.j_ref, bf16[128,256]{1,0:T(8,128)(2,1)S(1)} %get-tuple-element.14.x_ref, bf16[16,16,256]{2,1,0:T(8,128)(2,1)S(1)} %all_to_all.35.par_ref, bf16[16,16,8,256]{3,2,1,0:T(8,128)(2,1)} %copy-done, bf16[16,16,8,256]{3,2,1,0:T(8,128)(2,1)} %copy-done.1), custom_call_target="tpu_custom_call" | custom-call | tf_op jit(solution)/shard_map/fwd/pallas_call | solution.py:239
  64.8 4.5 %all-to-all-start.2 = ((bf16[32,64,256]{2,1,0:T(8,128)(2,1)}), bf16[32,64,256]{2,1,0:T(8,128)(2,1)S(1)}, u32[]{:S(2)}, u32[]{:S(2)}) async-start(bf16[32,64,256]{2,1,0:T(8,128)(2,1)} %bitcast.19), calls=%async_computation.2 | async-start | bytes 2097152 | tf_op jit(solution)/shard_map/all_to_all | solution.py:280
  69.4 0.9 dynamic-slice_bitcast_fusion.1
  70.2 0.8 dynamic-slice_bitcast_fusion
  71.1 3.1 %collective-permute-start.1 = (bf16[264,256]{1,0:T(8,128)(2,1)S(1)}, bf16[264,256]{1,0:T(8,128)(2,1)S(1)}, u32[]{:S(2)}, u32[]{:S(2)}) collective-permute-start(bf16[264,256]{1,0:T(8,128)(2,1)S(1)} %pad_maximum_fusion.mine_ref), channel_id=1, source_target_pairs={{0,32},{32,0},{1,33},{33,1},{2,34},{34,2},{3,35},{35,3},{4,36},{36... | collective-permute-start | bytes 405512 | tf_op jit(solution)/shard_map/ppermute | solution.py:290
  74.2 10.8 %collective-permute-done.1.theirs_ref = bf16[264,256]{1,0:T(8,128)(2,1)S(1)} collective-permute-done((bf16[264,256]{1,0:T(8,128)(2,1)S(1)}, bf16[264,256]{1,0:T(8,128)(2,1)S(1)}, u32[]{:S(2)}, u32[]{:S(2)}) %collective-permute-start.1) | collective-permute-done | bytes 135200 | tf_op jit(solution)/shard_map/ppermute | solution.py:290
  85.0 1.4 all-to-all-done.2
  86.4 1.8 %gram.1 = (f32[384,256]{1,0:T(8,128)S(1)}, bf16[392,256]{1,0:T(8,128)(2,1)S(1)}, bf16[8,256]{1,0:T(8,128)(2,1)S(1)}, f32[2,4,256]{2,1,0:T(4,128)S(1)}, bf16[2,1024,256]{2,1,0:T(8,128)(2,1)}) custom-call(s32[1]{0:T(128)} %bitcast.j_ref, bf16[16,2,64,256]{3,2,1,0:T(8,128)(2,1)S(1)} %bitcast.14, bf16[264,256]{1,0:T(8,128)(2,1)S(1)} %pad_maximum_fusion.mine_ref, ...), custom_call_target="tpu_custom_call" | custom-call | tf_op jit(solution)/shard_map/gram/pallas_call | solution.py:239
  88.2 4.8 %collective-permute-start.2 = (bf16[392,256]{1,0:T(8,128)(2,1)S(1)}, bf16[392,256]{1,0:T(8,128)(2,1)S(1)}, u32[]{:S(2)}, u32[]{:S(2)}) collective-permute-start(bf16[392,256]{1,0:T(8,128)(2,1)S(1)} %get-tuple-element.20), channel_id=1, source_target_pairs={{0,1},{1,0},{2,3},{3,2},{4,5},{5,4},{6,7},{7,6},{8,9},{9,8},{10,11... | collective-permute-start | bytes 602120 | tf_op jit(solution)/shard_map/ppermute | solution.py:306
  93.0 1.1 collective-permute-done.2.got_ref
  94.1 9.7 %all_to_all.37.r_ref = bf16[4,112,256]{2,1,0:T(8,128)(2,1)S(1)} all-to-all(bf16[4,112,256]{2,1,0:T(8,128)(2,1)S(1)} %chip.1), channel_id=1, replica_groups=mesh['k'=4,'h'=2,'g'=2,'x'=4,'y'=4,'c'=2] {'h','g'}, dimensions={0} | all-to-all | bytes 458752 | tf_op jit(solution)/shard_map/all_to_all | solution.py:310
  103.8 0.9 deviation.1
  104.7 9.5 %all_to_all.38 = bf16[4,96,256]{2,1,0:T(8,128)(2,1)S(1)} all-to-all(bf16[4,96,256]{2,1,0:T(8,128)(2,1)S(1)} %deviation.1), channel_id=1, replica_groups=mesh['k'=4,'h'=2,'g'=2,'x'=4,'y'=4,'c'=2] {'h','g'}, dimensions={0} | all-to-all | bytes 393216 | tf_op jit(solution)/shard_map/all_to_all | solution.py:320
  114.2 4.7 %all-gather = bf16[8,96,256]{2,1,0:T(8,128)(2,1)S(1)} all-gather(bf16[4,96,256]{2,1,0:T(8,128)(2,1)S(1)} %all_to_all.38), channel_id=2, replica_groups=mesh['k'=4,'h'=2,'g'=2,'x'=4,'y'=4,'c'=2] {'c'}, dimensions={0}, use_global_device_ids=true | all-gather | bytes 589824 | tf_op jit(solution)/shard_map/all_gather | solution.py:320
  118.9 3.3 %pull.1 = bf16[16,2,136,128]{3,2,1,0:T(8,128)(2,1)} custom-call(bf16[2,4,96,256]{3,2,1,0:T(8,128)(2,1)S(1)} %bitcast.15, bf16[4,112,256]{2,1,0:T(8,128)(2,1)S(1)} %all_to_all.37.r_ref, bf16[8,256]{1,0:T(8,128)(2,1)S(1)} %get-tuple-element.19.tail_ref, f32[2,4,256]{2,1,0:T(4,128)S(1)} %get-tuple-element.21.par_ref, bf16[2,1024,256]{2,1,0:T(8,128)(2,1)} %get-tuple-element.22.zc_ref), custom_call_target="tpu_custom_call" | custom-call | tf_op jit(solution)/shard_map/pull/pallas_call | solution.py:239
  122.1 22.6 %all_to_all.39 = bf16[32,136,128]{2,1,0:T(8,128)(2,1)} all-to-all(bf16[32,136,128]{2,1,0:T(8,128)(2,1)} %bitcast.18), channel_id=1, replica_groups=mesh['k'=4,'h'=2,'g'=2,'x'=4,'y'=4,'c'=2] {'x','y','g'}, dimensions={0} | all-to-all | bytes 2228224 | tf_op jit(solution)/shard_map/all_to_all | solution.py:331
  144.8 4.2 %bwd.1 = bf16[8,24,256]{2,1,0:T(8,128)(2,1)S(1)} custom-call(s32[1]{0:T(128)} %bitcast.j_ref, bf16[16,2,136,128]{3,2,1,0:T(8,128)(2,1)} %bitcast.17, bf16[16,128,256]{2,1,0:T(8,128)(2,1)} %get-tuple-element.23.slope_ref, bf16[16,16,8,256]{3,2,1,0:T(8,128)(2,1)} %copy-done, bf16[16,16,8,256]{3,2,1,0:T(8,128)(2,1)} %copy-done.1), custom_call_target="tpu_custom_call" | custom-call | tf_op jit(solution)/shard_map/bwd/pallas_call | solution.py:239
  149.0 18.2 %all_to_all.40.r_ref = bf16[8,24,256]{2,1,0:T(8,128)(2,1)S(1)} all-to-all(bf16[8,24,256]{2,1,0:T(8,128)(2,1)S(1)} %bwd.1), channel_id=1, replica_groups=mesh['k'=4,'h'=2,'g'=2,'x'=4,'y'=4,'c'=2] {'k','g'}, dimensions={0} | all-to-all | bytes 196608 | tf_op jit(solution)/shard_map/all_to_all | solution.py:341
  167.2 0.6 outputs.1
  (4 shorter events, 0.1 us)
Async XLA Ops:
  49.5 9.2 %copy-start = (bf16[16,16,8,256]{3,2,1,0:T(8,128)(2,1)}, bf16[16,16,8,256]{3,2,1,0:T(8,128)(2,1)S(1)}, u32[]{:S(2)}) copy-start(bf16[16,16,8,256]{3,2,1,0:T(8,128)(2,1)S(1)} %all_to_all.36.own_ref) | copy-start | bytes 3145732
  49.5 9.2 %collective-permute-start = (bf16[16,16,8,256]{3,2,1,0:T(8,128)(2,1)S(1)}, bf16[16,16,8,256]{3,2,1,0:T(8,128)(2,1)S(1)}, u32[]{:S(2)}, u32[]{:S(2)}) collective-permute-start(bf16[16,16,8,256]{3,2,1,0:T(8,128)(2,1)S(1)} %all_to_all.36.own_ref), channel_id=1, source_target_pairs={{0,1},{1,0},{2,3},{3,2},{4,5},{5,4},{6,7},{7,6},{8,9},{9,8},{10,11... | collective-permute-start | bytes 3145736 | tf_op jit(solution)/shard_map/ppermute | solution.py:267
  58.6 1.0 copy-start.1
  64.8 21.5 %all-to-all-start.2 = ((bf16[32,64,256]{2,1,0:T(8,128)(2,1)}), bf16[32,64,256]{2,1,0:T(8,128)(2,1)S(1)}, u32[]{:S(2)}, u32[]{:S(2)}) async-start(bf16[32,64,256]{2,1,0:T(8,128)(2,1)} %bitcast.19), calls=%async_computation.2 | async-start | bytes 2097152 | tf_op jit(solution)/shard_map/all_to_all | solution.py:280
  71.1 13.9 %collective-permute-start.1 = (bf16[264,256]{1,0:T(8,128)(2,1)S(1)}, bf16[264,256]{1,0:T(8,128)(2,1)S(1)}, u32[]{:S(2)}, u32[]{:S(2)}) collective-permute-start(bf16[264,256]{1,0:T(8,128)(2,1)S(1)} %pad_maximum_fusion.mine_ref), channel_id=1, source_target_pairs={{0,32},{32,0},{1,33},{33,1},{2,34},{34,2},{3,35},{35,3},{4,36},{36... | collective-permute-start | bytes 405512 | tf_op jit(solution)/shard_map/ppermute | solution.py:290
  88.2 5.9 %collective-permute-start.2 = (bf16[392,256]{1,0:T(8,128)(2,1)S(1)}, bf16[392,256]{1,0:T(8,128)(2,1)S(1)}, u32[]{:S(2)}, u32[]{:S(2)}) collective-permute-start(bf16[392,256]{1,0:T(8,128)(2,1)S(1)} %get-tuple-element.20), channel_id=1, source_target_pairs={{0,1},{1,0},{2,3},{3,2},{4,5},{5,4},{6,7},{7,6},{8,9},{9,8},{10,11... | collective-permute-start | bytes 602120 | tf_op jit(solution)/shard_map/ppermute | solution.py:306

commit v3 on v2

--- a/solution.py
+++ b/solution.py
@@ -9,6 +9,7 @@
 from jax.sharding import Mesh, PartitionSpec as P
 
 EPS = 1e-05
+LOG2E = math.log2(math.e)
 HIGHEST = lax.Precision.HIGHEST
 F32 = jnp.float32
 BF16 = jnp.bfloat16
@@ -36,8 +37,13 @@
     return high, middle, rest - middle
 
 
-def pack_kernel(w_ref, images_ref, mean_ref, var_ref, gain_ref, bias_ref, out_ref, x_ref, slab_ref, sems):
-    chip = lax.axis_index("x") * 4 + lax.axis_index("y")
+def pack_kernel(w_ref, images_ref, *refs):
+    inputs, (out_ref, x_ref, slab_ref), held, sems = refs[:4], refs[4:7], refs[7:11], refs[11]
+    reads = [pltpu.make_async_copy(source, target, sems.at[5 + at]) for at, (source, target) in enumerate(zip(inputs, held))]
+    for copy in reads:
+        copy.start()
+    mean_ref, var_ref, gain_ref, bias_ref = held
+    chip = lax.axis_index("y") * 4 + lax.axis_index("x")
     row = (lax.axis_index("c") * CHIPS + chip) * SLICE
     half = lax.axis_index("h")
     group = 2 * jnp.minimum(lax.axis_index("k"), BLOCKS - 1) + lax.axis_index("g")
@@ -50,6 +56,8 @@
         ]
         copies.append(pltpu.make_async_copy(source, x_ref.at[strip * 32:strip * 32 + 32], sems.at[1 + strip]))
         copies[-1].start()
+    for copy in reads:
+        copy.wait()
     scale = gain_ref[...] * lax.rsqrt(var_ref[...] + EPS)
     packed = [scale, bias_ref[...] - mean_ref[...] * scale, mean_ref[...], var_ref[...]]
     high = [value.astype(BF16).astype(F32) for value in packed]
@@ -69,37 +77,70 @@
     return jnp.concatenate([lax.select(core == 0, own, other), lax.select(core == 0, other, own)], axis=0)
 
 
-def layer_weight(own_ref, other_ref, core, layer):
-    return in_order(own_ref[:, layer].reshape(GW // 2, GW), other_ref[:, layer].reshape(GW // 2, GW), core)
-
-
-def forward_kernel(j_ref, x_ref, par_ref, own_ref, other_ref, xs_ref, slope_ref):
-    core = j_ref[0] % 2
+def forward_kernel(
+    x_ref, par_ref, own_in, other_in, out_ref, w_out, slope_out, w_ref, slope_ref, rows_ref, sems
+):
+    core = lax.axis_index("c")
+    chip = lax.axis_index("y") * 4 + lax.axis_index("x")
+    arrivals = []
+    for layer in range(LAYERS):
+        arrivals.append(
+            [
+                pltpu.make_async_copy(own_in.at[:, layer], w_ref.at[layer, core], sems.at[0, layer]),
+                pltpu.make_async_copy(other_in.at[:, layer], w_ref.at[layer, 1 - core], sems.at[1, layer]),
+            ]
+        )
+        for copy in arrivals[layer]:
+            copy.start()
+    for layer in range(LAYERS):
+        rows_ref[layer] = par_ref[layer, SLICE:SLICE + PROWS].astype(F32)
+    at_row = lax.broadcasted_iota(jnp.int32, (TAIL, LANES), 0)
+    copies = []
     x = x_ref[...]
     for layer in range(LAYERS):
-        xs_ref[layer] = x
-        weight = layer_weight(own_ref, other_ref, core, layer)
-        packed = par_ref[layer, SLICE:SLICE + PROWS].astype(F32)
-        scale = packed[0:1] + packed[4:5]
-        shift = packed[1:2] + packed[5:6]
-        active = jnp.dot(x, weight, preferred_element_type=F32) * scale + shift
-        gate = 1.0 / (1.0 + jnp.exp(-active))
-        x = (active * gate).astype(BF16)
-        slope_ref[layer] = (gate * (1.0 + active * (1.0 - gate)) * scale).astype(BF16)
-
-
-def gram_kernel(j_ref, x_ref, mine_ref, theirs_ref, keep_ref, send_ref, tail_ref, par_ref, zc_ref):
-    core, side = j_ref[0] % 2, j_ref[0] // 2 % 2
+        for copy in arrivals[layer]:
+            copy.wait()
+        copies.append(pltpu.make_async_copy(w_ref.at[layer], w_out.at[layer], sems.at[2, layer]))
+        copies[-1].start()
+        scale = rows_ref[layer, 0:1] + rows_ref[layer, 4:5]
+        shift = rows_ref[layer, 1:2] + rows_ref[layer, 5:6]
+        z = jnp.dot(x, w_ref[layer].reshape(GW, GW), preferred_element_type=F32)
+        active = z * scale + shift
+        gate = 1.0 / (1.0 + jnp.exp2(active * -LOG2E))
+        after = active * gate
+        x = after.astype(BF16)
+        slope_ref[layer] = (gate * ((active - after) + 1.0) * scale).astype(BF16)
+        copies.append(pltpu.make_async_copy(slope_ref.at[layer], slope_out.at[layer], sems.at[3, layer]))
+        copies[-1].start()
+        row = rows_ref[layer, pl.ds(chip // 2, 1), :]
+        row = jnp.broadcast_to(lax.select(chip % 2 == 0, row[:, 0:LANES], row[:, LANES:]), (TAIL, LANES))
+        for half in range(2):
+            rows = z[half * HALF:(half + 1) * HALF]
+            mean = jnp.sum(rows, axis=0, keepdims=True) * (1.0 / HALF)
+            rows = (rows - mean).astype(BF16)
+            out_ref[half, layer, 0:HALF] = rows[:, 0:LANES]
+            out_ref[half, layer, HALF:2 * HALF] = rows[:, LANES:]
+            high = mean.astype(BF16).astype(F32)
+            terms = [part[:, at:at + LANES] for part in (high, mean - high) for at in (0, LANES)]
+            tail = row
+            for at, term in enumerate(terms):
+                tail = jnp.where(at_row == at, term, tail)
+            out_ref[half, layer, 2 * HALF:] = tail.astype(BF16)
+    for copy in copies:
+        copy.wait()
+
+
+def gram_kernel(j_ref, x_ref, keep_ref, send_ref, tail_ref, par_ref, zc_ref):
+    core = j_ref[0] % 2
     means = []
     for g in range(2):
-        layer = lax.select(side == g, mine_ref[...], theirs_ref[...])
-        packed = layer[GW:].astype(F32)
-        par_ref[g] = packed[0:4] + packed[4:8]
-        weight = in_order(layer[0:GW // 2], layer[GW // 2:GW], core)
-        z = jnp.dot(x_ref[:, g].reshape(HOME, GW), weight, preferred_element_type=F32)
-        mean = jnp.sum(z, axis=0, keepdims=True) * (1.0 / HOME)
-        zc_ref[g] = (z - mean).astype(BF16)
-        means.append(mean)
+        tails = x_ref[g, :, 2 * HALF:].astype(F32)
+        mean = sum(jnp.concatenate([tails[:, at:at + 1], tails[:, at + 1:at + 2]], axis=2) for at in (0, 2))
+        means.append(jnp.mean(mean, axis=0))
+        rows = jnp.concatenate([x_ref[g, :, 0:HALF], x_ref[g, :, HALF:2 * HALF]], axis=2).astype(F32)
+        zc_ref[g] = (rows + (mean - means[g][None])).astype(BF16).reshape(HOME, GW)
+        packed = [jnp.concatenate([tails[2 * r, 6:7], tails[2 * r + 1, 6:7]], axis=1) for r in range(PROWS)]
+        par_ref[g] = jnp.concatenate([packed[r] + packed[r + 4] for r in range(4)], axis=0)
     parts = [split3(mean) for mean in means]
     tail = [parts[g][term] for term in range(3) for g in range(2)]
     tail = jnp.concatenate(tail + [jnp.zeros((2, GW), F32)], axis=0).astype(BF16)
@@ -186,32 +227,41 @@
         row = pull[HOME:HOME + 1] + pull[HOME + 1:HOME + 2] + pull[HOME + 2:HOME + 3] + away[g]
         pull = pull[0:HOME] + row
         pull = pull.astype(BF16).reshape(CHIPS, HALF, GW)
-        out_ref[:, g, 0:HALF] = pull[:, :, 0:LANES]
-        out_ref[:, g, HALF:2 * HALF] = pull[:, :, LANES:]
-        out_ref[:, g, 2 * HALF:] = tail
-
-
-def backward_kernel(j_ref, q_ref, slope_ref, own_ref, other_ref, out_ref):
-    core = j_ref[0] % 2
+        out_ref[g, :, 0:HALF] = pull[:, :, 0:LANES]
+        out_ref[g, :, HALF:2 * HALF] = pull[:, :, LANES:]
+        out_ref[g, :, 2 * HALF:] = tail
+
+
+def backward_kernel(q_ref, w_in, slope_in, out_ref, w_ref, slope_ref, sems):
+    copies = [None] * LAYERS
+    for layer in reversed(range(LAYERS)):
+        copies[layer] = [pltpu.make_async_copy(w_in.at[layer], w_ref.at[layer], sems.at[0, layer])]
+        if layer < LAYERS - 1:
+            copies[layer].append(pltpu.make_async_copy(slope_in.at[layer], slope_ref.at[layer], sems.at[1, layer]))
+        for copy in copies[layer]:
+            copy.start()
     loss = jnp.zeros((1, LANES), F32)
     grad = None
     for layer in reversed(range(LAYERS)):
-        rows = q_ref[layer, 0, 2 * HALF:].astype(F32)
+        rows = q_ref[0, layer, 2 * HALF:].astype(F32)
         loss = loss + (rows[0:1] + rows[1:2] + rows[2:3])
         pull = jnp.concatenate(
-            [q_ref[layer, :, 0:HALF].reshape(ROWS, LANES), q_ref[layer, :, HALF:2 * HALF].reshape(ROWS, LANES)], axis=1
+            [q_ref[:, layer, 0:HALF].reshape(ROWS, LANES), q_ref[:, layer, HALF:2 * HALF].reshape(ROWS, LANES)], axis=1
         )
+        for copy in copies[layer]:
+            copy.wait()
         if grad is not None:
             pull = (grad * slope_ref[layer].astype(F32) + pull.astype(F32)).astype(BF16)
         grad = lax.dot_general(
-            pull, layer_weight(own_ref, other_ref, core, layer), (((1,), (1,)), ((), ())), preferred_element_type=F32
+            pull, w_ref[layer].reshape(GW, GW), (((1,), (1,)), ((), ())), preferred_element_type=F32
         ).astype(BF16).astype(F32)
     loss = jnp.concatenate([loss, loss], axis=1)
     tail = jnp.concatenate(list(split3(loss)) + [jnp.zeros((TAIL - 3, GW), F32)], axis=0).astype(BF16)
     grad = grad.astype(BF16)
     for strip in range(8):
-        out_ref[strip, 0:16] = grad[strip * 16:strip * 16 + 16]
-        out_ref[strip, 16:16 + TAIL] = tail
+        slot = strip % 2 * 4 + strip // 2
+        out_ref[slot, 0:16] = grad[strip * 16:strip * 16 + 16]
+        out_ref[slot, 16:16 + TAIL] = tail
 
 
 def output_kernel(r_ref, grad_ref, loss_ref):
@@ -219,12 +269,12 @@
     for k in range(BLOCKS):
         for g in range(2):
             at = 2 * k + g
-            grad_ref[0, :, at * GW:(at + 1) * GW] = r_ref[at, 0:16]
-        loss = loss + jnp.sum(r_ref[2 * k, 16:16 + TAIL].astype(F32)[0:3, 0:1], axis=0, keepdims=True)
+            grad_ref[0, :, at * GW:(at + 1) * GW] = r_ref[4 * g + k, 0:16]
+        loss = loss + jnp.sum(r_ref[k, 16:16 + TAIL].astype(F32)[0:3, 0:1], axis=0, keepdims=True)
     loss_ref[...] = loss * (1.0 / (LAYERS * BLOCKS * 2 * GW))
 
 
-LARGE = 1100000
+LARGE = 1200000
 
 
 def is_large(shape, dtype):
@@ -247,47 +297,44 @@
 
 
 def shards(images, weights, bn_mean, bn_var, bn_gain, bn_bias):
-    chip = lax.axis_index(("x", "y"))
-    part = lax.axis_index(("h", "g", "c")).astype(jnp.int32).reshape(1)
+    part = lax.axis_index(("g", "h", "c")).astype(jnp.int32).reshape(1)
 
     hbm, vmem = pl.BlockSpec(memory_space=pl.ANY), pl.BlockSpec(memory_space=pltpu.VMEM)
     message, rows = pl.pallas_call(
         pack_kernel,
         out_shape=[pltpu.VMEM((4, 2, 2, SLICE + PROWS, GW), BF16), pltpu.VMEM((ROWS, GW), BF16)],
-        in_specs=[hbm, hbm] + [vmem] * 4,
+        in_specs=[hbm] * 6,
         out_specs=[vmem, vmem],
-        scratch_shapes=[pltpu.VMEM((2 * BLOCKS, SLICE, GW), BF16), pltpu.SemaphoreType.DMA((5,))],
+        scratch_shapes=[pltpu.VMEM((2 * BLOCKS, SLICE, GW), BF16)]
+        + [pltpu.VMEM((1, 2 * BLOCKS * GW), F32)] * 4
+        + [pltpu.SemaphoreType.DMA((9,))],
         name="pack",
     )(weights, images, bn_mean, bn_var, bn_gain, bn_bias)
     message = message.reshape(LAYERS, SLICE + PROWS, GW)
     layer_parts = lax.all_to_all(message, ("k", "h", "g"), 0, 0, tiled=True)
 
     own = layer_parts[:, 0:SLICE]
-    own = lax.all_to_all(jnp.broadcast_to(own[None], (CHIPS, LAYERS, SLICE, GW)), ("x", "y"), 0, 0, tiled=True)
+    own = lax.all_to_all(jnp.broadcast_to(own[None], (CHIPS, LAYERS, SLICE, GW)), ("y", "x"), 0, 0, tiled=True)
     other = lax.ppermute(own, "c", [(0, 1), (1, 0)])
 
-    xs, slope = kernel_call(
+    def near(array):
+        return pltpu.with_memory_space_constraint(array, pltpu.VMEM)
+
+    layers = [pltpu.VMEM((LAYERS, 2, CHIPS, SLICE, GW), BF16), pltpu.VMEM((LAYERS, ROWS, GW), BF16)]
+    xs, chain_weights, slope = pl.pallas_call(
         forward_kernel,
-        [],
-        "fwd",
-        rows,
-        layer_parts,
-        scalars=[part],
-        far=[own, other],
-        loose=[jax.ShapeDtypeStruct((LAYERS, ROWS, GW), BF16)] * 2,
-    )
-
-    home = lax.all_to_all(xs.reshape(2 * CHIPS, HALF, GW), ("x", "y", "g"), 0, 0, tiled=True)
-    mine = jnp.concatenate(
-        [
-            lax.dynamic_index_in_dim(own, chip, 1, keepdims=False).reshape(GW // 2, GW),
-            lax.dynamic_index_in_dim(other, chip, 1, keepdims=False).reshape(GW // 2, GW),
-            lax.dynamic_index_in_dim(layer_parts, chip, 0, keepdims=False)[SLICE:],
+        out_shape=[
+            pltpu.VMEM((2, LAYERS, 2 * HALF + TAIL, LANES), BF16),
+            jax.ShapeDtypeStruct((LAYERS, 2, CHIPS, SLICE, GW), BF16),
+            jax.ShapeDtypeStruct((LAYERS, ROWS, GW), BF16),
         ],
-        axis=0,
-    )
-    mine = lax.optimization_barrier((mine, xs))[0]
-    theirs = lax.ppermute(mine, "g", [(0, 1), (1, 0)])
+        in_specs=[vmem, vmem, hbm, vmem],
+        out_specs=[vmem, hbm, hbm],
+        scratch_shapes=layers + [pltpu.VMEM((LAYERS, PROWS, GW), F32), pltpu.SemaphoreType.DMA((4, LAYERS))],
+        name="fwd",
+    )(near(rows), near(layer_parts), own, near(other))
+
+    home = lax.all_to_all(xs.reshape(2 * CHIPS, 2 * HALF + TAIL, LANES), ("g", "y", "x"), 0, 0, tiled=True)
     keep, send, tail, params, centered = kernel_call(
         gram_kernel,
         [
@@ -297,9 +344,7 @@
             ((2, 4, GW), F32),
         ],
         "gram",
-        home.reshape(CHIPS, 2, HALF, GW),
-        mine,
-        theirs,
+        home.reshape(2, CHIPS, 2 * HALF + TAIL, LANES),
         scalars=[part],
         loose=[jax.ShapeDtypeStruct((2, HOME, GW), BF16)],
     )
@@ -307,7 +352,7 @@
     (pieces,) = kernel_call(
         chip_kernel, [((4, 3 * PIECE + 2 * TAIL, GW), BF16)], "chip", keep, tail, got, scalars=[part]
     )
-    pieces = lax.all_to_all(pieces, ("h", "g"), 0, 0, tiled=True)
+    pieces = lax.all_to_all(pieces, ("g", "h"), 0, 0, tiled=True)
     (deviation,) = kernel_call(
         deviation_kernel,
         [((4, 3 * PIECE, GW), BF16)],
@@ -317,10 +362,10 @@
         scalars=[part],
         scratch=[pltpu.VMEM((GW, GW), F32)],
     )
-    deviation = lax.all_gather(lax.all_to_all(deviation, ("h", "g"), 0, 0, tiled=True), "c", axis=0)
+    deviation = lax.all_gather(lax.all_to_all(deviation, ("g", "h"), 0, 0, tiled=True), "c", axis=0)
     (pulls,) = kernel_call(
         pull_kernel,
-        [((CHIPS, 2, 2 * HALF + TAIL, LANES), BF16)],
+        [((2, CHIPS, 2 * HALF + TAIL, LANES), BF16)],
         "pull",
         deviation,
         pieces,
@@ -328,24 +373,24 @@
         params,
         far=[centered],
     )
-    pulls = lax.all_to_all(pulls.reshape(2 * CHIPS, 2 * HALF + TAIL, LANES), ("x", "y", "g"), 0, 0, tiled=True)
-
-    (grads,) = kernel_call(
+    pulls = lax.all_to_all(pulls.reshape(2 * CHIPS, 2 * HALF + TAIL, LANES), ("g", "y", "x"), 0, 0, tiled=True)
+
+    grads = pl.pallas_call(
         backward_kernel,
-        [((8, 16 + TAIL, GW), BF16)],
-        "bwd",
-        pulls.reshape(LAYERS, 2, 2 * HALF + TAIL, LANES),
-        scalars=[part],
-        far=[slope, own, other],
-    )
-    grads = lax.all_to_all(grads, ("k", "g"), 0, 0, tiled=True)
+        out_shape=pltpu.VMEM((8, 16 + TAIL, GW), BF16),
+        in_specs=[vmem, hbm, hbm],
+        out_specs=vmem,
+        scratch_shapes=layers + [pltpu.SemaphoreType.DMA((2, LAYERS))],
+        name="bwd",
+    )(near(pulls.reshape(2, LAYERS, 2 * HALF + TAIL, LANES)), chain_weights, slope)
+    grads = lax.all_to_all(grads, ("g", "k"), 0, 0, tiled=True)
     image_grad, loss = pl.pallas_call(
         output_kernel,
         out_shape=[jax.ShapeDtypeStruct((1, 16, BLOCKS * 2 * GW), BF16), jax.ShapeDtypeStruct((1, 1), F32)],
         in_specs=[vmem],
         out_specs=[vmem, vmem],
         name="outputs",
-    )(pltpu.with_memory_space_constraint(grads, pltpu.VMEM))
+    )(near(grads))
     return image_grad, loss.reshape(())
 
 

time: 169 us -> 165 us (0.976)
  starting transfers between devices: 19.3 us -> 15.1 us
  waiting for transfers between devices: 15.5 us -> 19.1 us
  local copies, waits for them, and re-layouts: 2.8 us -> 0.1 us
  blocking collectives: 112 us -> 110 us
    all_to_all x1, waiting for transfers between devices: 1.4 us -> 15.8 us  [shards(): lax.all_to_all(xs.reshape(2 * CHIPS, 2 * HALF + TAIL, LANES), ('g', 'y',...]
    pallas_call x0 -> x2, Pallas kernels: none -> 11.5 us  [the longest x1 6.82 us: shards(): pl.pallas_call(forward_kernel, out_shape=[pltpu.VMEM((2, LAYERS, 2 * HALF...]
    pallas_call x6 -> x4, Pallas kernels: 15.5 us -> 4.56 us  [kernel_call(): pl.pallas_call(kernel, out_shape=[jax.ShapeDtypeStruct(*out) if is_large(...]
    ppermute x1 -> x0, waiting for transfers between devices: 10.8 us -> none  [shards(): theirs = lax.ppermute(mine, 'g', [(0, 1), (1, 0)])]
    ppermute x1 -> x0, starting transfers between devices: 3.14 us -> none  [shards(): theirs = lax.ppermute(mine, 'g', [(0, 1), (1, 0)])]
    all_to_all x4, blocking collectives: 60 us -> 57.5 us  [the longest x1 21.1 us: shards(): lax.all_to_all(pulls.reshape(2 * CHIPS, 2 * HALF + TAIL, LANES), ('g', 'y...]
    reshape x2 -> x0, local copies, waits for them, and re-layouts: 1.7 us -> none  [the longest x1 0.85 us: shards(): lax.dynamic_index_in_dim(own, chip, 1, keepdims=False).reshape(GW // 2, GW)]
  transfers between devices with their start and end apart: 4 -> 3, of which waited for: 4 -> 3; matrix products, arithmetic and copies ran while one was open for 1% -> 0% of each run, Pallas kernels for 0% -> 0%
where the time goes in v3:
time: 165 us; the launch traced here: 162 us
  blocking collectives  110 us (67%)
  waiting for transfers between devices  19.1 us (12%)
  Pallas kernels  17.6 us (11%)
  starting transfers between devices  15.1 us (9%)
    all_to_all x1, blocking collectives, shards(): layer_parts = lax.all_to_all(message, ('k', 'h', 'g'), 0, 0, tiled=True)  27.5 us
    all_to_all x1, blocking collectives, shards(): lax.all_to_all(pulls.reshape(2 * CHIPS, 2 * HALF + TAIL, LANES), ('g', 'y...  21.1 us
    all_to_all x1, blocking collectives, shards(): lax.all_to_all(jnp.broadcast_to(own[None], (CHIPS, LAYERS, SLICE, GW)), (...  19.9 us
    all_to_all x1, blocking collectives, shards(): grads = lax.all_to_all(grads, ('g', 'k'), 0, 0, tiled=True)  16.8 us
    all_to_all x1, waiting for transfers between devices, shards(): lax.all_to_all(xs.reshape(2 * CHIPS, 2 * HALF + TAIL, LANES), ('g', 'y',...  15.8 us
    all_to_all x1, blocking collectives, shards(): pieces = lax.all_to_all(pieces, ('g', 'h'), 0, 0, tiled=True)  11.2 us
    all_to_all x1, blocking collectives, shards(): lax.all_to_all(deviation, ('g', 'h'), 0, 0, tiled=True)  8.32 us
    pallas_call x1, Pallas kernels, shards(): pl.pallas_call(forward_kernel, out_shape=[pltpu.VMEM((2, LAYERS, 2 * HALF...  6.82 us
  transfers between devices with their start and end apart: 3, of which 3 were waited for; matrix products, arithmetic and copies ran while one was open for 0% of the time, Pallas kernels for 0%

profile of v3, /device:TPU:1, one launch (start us, length us, event | category | flops | bytes accessed | tf_op | source)
XLA Modules:
  0.0 162.3 jit_solution(10074594427516276131)
XLA Ops:
  0.6 0.9 pack.1
  1.6 27.5 %all_to_all.35.par_ref = bf16[16,16,256]{2,1,0:T(8,128)(2,1)S(1)} all-to-all(bf16[16,16,256]{2,1,0:T(8,128)(2,1)S(1)} %bitcast.12), channel_id=1, replica_groups=mesh['k'=4,'h'=2,'g'=2,'x'=4,'y'=4,'c'=2] {'k','h','g'}, dimensions={0} | all-to-all | bytes 262144 | tf_op jit(solution)/shard_map/all_to_all | solution.py:314
  29.1 0.1 broadcast_in_dim.2
  29.2 19.9 %all_to_all.36.own_in = bf16[16,16,8,256]{3,2,1,0:T(8,128)(2,1)S(1)} all-to-all(bf16[16,16,8,256]{3,2,1,0:T(8,128)(2,1)S(1)} %broadcast_in_dim.2), channel_id=1, replica_groups=mesh['k'=4,'h'=2,'g'=2,'x'=4,'y'=4,'c'=2] {'y','x'}, dimensions={0} | all-to-all | bytes 2097152 | tf_op jit(solution)/shard_map/all_to_all | solution.py:317
  49.1 0.0 copy-start
  49.1 6.8 %collective-permute-start = (bf16[16,16,8,256]{3,2,1,0:T(8,128)(2,1)S(1)}, bf16[16,16,8,256]{3,2,1,0:T(8,128)(2,1)S(1)}, u32[]{:S(2)}, u32[]{:S(2)}) collective-permute-start(bf16[16,16,8,256]{3,2,1,0:T(8,128)(2,1)S(1)} %all_to_all.36.own_in), channel_id=1, source_target_pairs={{0,1},{1,0},{2,3},{3,2},{4,5},{5,4},{6,7},{7,6},{8,9},{9,8},{10,11... | collective-permute-start | bytes 3145736 | tf_op jit(solution)/shard_map/ppermute | solution.py:318
  55.8 2.3 %collective-permute-done.other_in = bf16[16,16,8,256]{3,2,1,0:T(8,128)(2,1)S(1)} collective-permute-done((bf16[16,16,8,256]{3,2,1,0:T(8,128)(2,1)S(1)}, bf16[16,16,8,256]{3,2,1,0:T(8,128)(2,1)S(1)}, u32[]{:S(2)}, u32[]{:S(2)}) %collective-permute-start) | collective-permute-done | bytes 1048608 | tf_op jit(solution)/shard_map/ppermute | solution.py:318
  58.1 0.0 copy-done
  58.1 6.8 %fwd.1 = (bf16[2,16,136,128]{3,2,1,0:T(8,128)(2,1)}, bf16[16,2,16,8,256]{4,3,2,1,0:T(8,128)(2,1)}, bf16[16,128,256]{2,1,0:T(8,128)(2,1)}) custom-call(bf16[128,256]{1,0:T(8,128)(2,1)S(1)} %get-tuple-element.14.x_ref, bf16[16,16,256]{2,1,0:T(8,128)(2,1)S(1)} %all_to_all.35.par_ref, bf16[16,16,8,256]{3,2,1,0:T(8,128)(2,1)} %copy-done, ...), custom_call_target="tpu_custom_call" | custom-call | tf_op jit(solution)/shard_map/fwd/pallas_call | solution.py:324
  64.9 4.1 %all-to-all-start.2 = ((bf16[32,136,128]{2,1,0:T(8,128)(2,1)}), bf16[32,136,128]{2,1,0:T(8,128)(2,1)S(1)}, u32[]{:S(2)}, u32[]{:S(2)}) async-start(bf16[32,136,128]{2,1,0:T(8,128)(2,1)} %bitcast.2), calls=%async_computation.2 | async-start | bytes 2228224 | tf_op jit(solution)/shard_map/all_to_all | solution.py:337
  69.0 15.8 %all-to-all-done.2 = bf16[32,136,128]{2,1,0:T(8,128)(2,1)S(1)} async-done(((bf16[32,136,128]{2,1,0:T(8,128)(2,1)}), bf16[32,136,128]{2,1,0:T(8,128)(2,1)S(1)}, u32[]{:S(2)}, u32[]{:S(2)}) %all-to-all-start.2) | async-done | bytes 1114144 | tf_op jit(solution)/shard_map/all_to_all | solution.py:337
  84.8 1.4 gram.1
  86.2 4.2 %collective-permute-start.1 = (bf16[392,256]{1,0:T(8,128)(2,1)S(1)}, bf16[392,256]{1,0:T(8,128)(2,1)S(1)}, u32[]{:S(2)}, u32[]{:S(2)}) collective-permute-start(bf16[392,256]{1,0:T(8,128)(2,1)S(1)} %get-tuple-element.19), channel_id=1, source_target_pairs={{0,1},{1,0},{2,3},{3,2},{4,5},{5,4},{6,7},{7,6},{8,9},{9,8},{10,11... | collective-permute-start | bytes 602120 | tf_op jit(solution)/shard_map/ppermute | solution.py:351
  90.5 1.1 collective-permute-done.1.got_ref
  91.5 0.1 chip.1
  91.6 11.2 %all_to_all.37.r_ref = bf16[4,112,256]{2,1,0:T(8,128)(2,1)S(1)} all-to-all(bf16[4,112,256]{2,1,0:T(8,128)(2,1)S(1)} %chip.1), channel_id=1, replica_groups=mesh['k'=4,'h'=2,'g'=2,'x'=4,'y'=4,'c'=2] {'g','h'}, dimensions={0} | all-to-all | bytes 458752 | tf_op jit(solution)/shard_map/all_to_all | solution.py:355
  102.8 0.9 deviation.1
  103.7 8.3 %all_to_all.38 = bf16[4,96,256]{2,1,0:T(8,128)(2,1)S(1)} all-to-all(bf16[4,96,256]{2,1,0:T(8,128)(2,1)S(1)} %deviation.1), channel_id=1, replica_groups=mesh['k'=4,'h'=2,'g'=2,'x'=4,'y'=4,'c'=2] {'g','h'}, dimensions={0} | all-to-all | bytes 393216 | tf_op jit(solution)/shard_map/all_to_all | solution.py:365
  112.0 4.8 %all-gather = bf16[8,96,256]{2,1,0:T(8,128)(2,1)S(1)} all-gather(bf16[4,96,256]{2,1,0:T(8,128)(2,1)S(1)} %all_to_all.38), channel_id=2, replica_groups=mesh['k'=4,'h'=2,'g'=2,'x'=4,'y'=4,'c'=2] {'c'}, dimensions={0}, use_global_device_ids=true | all-gather | bytes 589824 | tf_op jit(solution)/shard_map/all_gather | solution.py:365
  116.8 2.2 %pull.1 = bf16[2,16,136,128]{3,2,1,0:T(8,128)(2,1)S(1)} custom-call(bf16[2,4,96,256]{3,2,1,0:T(8,128)(2,1)S(1)} %bitcast.11, bf16[4,112,256]{2,1,0:T(8,128)(2,1)S(1)} %all_to_all.37.r_ref, bf16[8,256]{1,0:T(8,128)(2,1)S(1)} %get-tuple-element.18.tail_ref, f32[2,4,256]{2,1,0:T(4,128)S(1)} %get-tuple-element.20.par_ref, ...), custom_call_target="tpu_custom_call" | custom-call | tf_op jit(solution)/shard_map/pull/pallas_call | solution.py:289
  119.0 21.1 %all_to_all.39 = bf16[32,136,128]{2,1,0:T(8,128)(2,1)S(1)} all-to-all(bf16[32,136,128]{2,1,0:T(8,128)(2,1)S(1)} %bitcast.10), channel_id=1, replica_groups=mesh['k'=4,'h'=2,'g'=2,'x'=4,'y'=4,'c'=2] {'g','y','x'}, dimensions={0} | all-to-all | bytes 2228224 | tf_op jit(solution)/shard_map/all_to_all | solution.py:376
  140.2 4.7 %bwd.1 = bf16[8,24,256]{2,1,0:T(8,128)(2,1)S(1)} custom-call(bf16[2,16,136,128]{3,2,1,0:T(8,128)(2,1)S(1)} %bitcast.9, bf16[16,2,16,8,256]{4,3,2,1,0:T(8,128)(2,1)} %get-tuple-element.22.w_in, bf16[16,128,256]{2,1,0:T(8,128)(2,1)} %get-tuple-element.23.slope_in), custom_call_target="tpu_custom_call" | custom-call | tf_op jit(solution)/shard_map/bwd/pallas_call | solution.py:378
  144.9 16.8 %all_to_all.40.r_ref = bf16[8,24,256]{2,1,0:T(8,128)(2,1)S(1)} all-to-all(bf16[8,24,256]{2,1,0:T(8,128)(2,1)S(1)} %bwd.1), channel_id=1, replica_groups=mesh['k'=4,'h'=2,'g'=2,'x'=4,'y'=4,'c'=2] {'g','k'}, dimensions={0} | all-to-all | bytes 196608 | tf_op jit(solution)/shard_map/all_to_all | solution.py:386
  161.7 0.6 outputs.1
  (1 shorter events, 0.0 us)
Async XLA Ops:
  49.1 9.0 %copy-start = (bf16[16,16,8,256]{3,2,1,0:T(8,128)(2,1)}, bf16[16,16,8,256]{3,2,1,0:T(8,128)(2,1)S(1)}, u32[]{:S(2)}) copy-start(bf16[16,16,8,256]{3,2,1,0:T(8,128)(2,1)S(1)} %all_to_all.36.own_in) | copy-start | bytes 3145732
  49.1 9.0 %collective-permute-start = (bf16[16,16,8,256]{3,2,1,0:T(8,128)(2,1)S(1)}, bf16[16,16,8,256]{3,2,1,0:T(8,128)(2,1)S(1)}, u32[]{:S(2)}, u32[]{:S(2)}) collective-permute-start(bf16[16,16,8,256]{3,2,1,0:T(8,128)(2,1)S(1)} %all_to_all.36.own_in), channel_id=1, source_target_pairs={{0,1},{1,0},{2,3},{3,2},{4,5},{5,4},{6,7},{7,6},{8,9},{9,8},{10,11... | collective-permute-start | bytes 3145736 | tf_op jit(solution)/shard_map/ppermute | solution.py:318
  64.9 19.9 %all-to-all-start.2 = ((bf16[32,136,128]{2,1,0:T(8,128)(2,1)}), bf16[32,136,128]{2,1,0:T(8,128)(2,1)S(1)}, u32[]{:S(2)}, u32[]{:S(2)}) async-start(bf16[32,136,128]{2,1,0:T(8,128)(2,1)} %bitcast.2), calls=%async_computation.2 | async-start | bytes 2228224 | tf_op jit(solution)/shard_map/all_to_all | solution.py:337
  86.2 5.3 %collective-permute-start.1 = (bf16[392,256]{1,0:T(8,128)(2,1)S(1)}, bf16[392,256]{1,0:T(8,128)(2,1)S(1)}, u32[]{:S(2)}, u32[]{:S(2)}) collective-permute-start(bf16[392,256]{1,0:T(8,128)(2,1)S(1)} %get-tuple-element.19), channel_id=1, source_target_pairs={{0,1},{1,0},{2,3},{3,2},{4,5},{5,4},{6,7},{7,6},{8,9},{9,8},{10,11... | collective-permute-start | bytes 602120 | tf_op jit(solution)/shard_map/ppermute | solution.py:351

commit v4 on v3

--- a/solution.py
+++ b/solution.py
@@ -10,7 +10,6 @@
 
 EPS = 1e-05
 LOG2E = math.log2(math.e)
-HIGHEST = lax.Precision.HIGHEST
 F32 = jnp.float32
 BF16 = jnp.bfloat16
 
@@ -77,56 +76,75 @@
     return jnp.concatenate([lax.select(core == 0, own, other), lax.select(core == 0, other, own)], axis=0)
 
 
+FIRST = 4
+
+
+def weight_reads(own_in, other_in, w_ref, core, sems, layer):
+    return [
+        pltpu.make_async_copy(own_in.at[:, layer], w_ref.at[layer, core], sems.at[0, layer]),
+        pltpu.make_async_copy(other_in.at[:, layer], w_ref.at[layer, 1 - core], sems.at[1, layer]),
+    ]
+
+
 def forward_kernel(
-    x_ref, par_ref, own_in, other_in, out_ref, w_out, slope_out, w_ref, slope_ref, rows_ref, sems
+    x_ref, par_ref, own_in, other_in, xs_out, slope_out, w_ref, slope_ref, rows_ref, z_ref, xs_ref, sems, out_sems
 ):
     core = lax.axis_index("c")
     chip = lax.axis_index("y") * 4 + lax.axis_index("x")
-    arrivals = []
-    for layer in range(LAYERS):
-        arrivals.append(
-            [
-                pltpu.make_async_copy(own_in.at[:, layer], w_ref.at[layer, core], sems.at[0, layer]),
-                pltpu.make_async_copy(other_in.at[:, layer], w_ref.at[layer, 1 - core], sems.at[1, layer]),
-            ]
-        )
-        for copy in arrivals[layer]:
-            copy.start()
+    arrivals = [weight_reads(own_in, other_in, w_ref, core, sems, layer) for layer in range(LAYERS)]
+    for copy in sum(arrivals, []):
+        copy.start()
     for layer in range(LAYERS):
         rows_ref[layer] = par_ref[layer, SLICE:SLICE + PROWS].astype(F32)
     at_row = lax.broadcasted_iota(jnp.int32, (TAIL, LANES), 0)
-    copies = []
+
+    def pack_layer(layer):
+        row = rows_ref[layer, pl.ds(chip // 2, 1), :]
+        row = jnp.broadcast_to(lax.select(chip % 2 == 0, row[:, 0:LANES], row[:, LANES:]), (TAIL, LANES))
+        for half in range(2):
+            rows = z_ref[layer, half * HALF:(half + 1) * HALF]
+            mean = jnp.sum(rows, axis=0, keepdims=True) * (1.0 / HALF)
+            rows = (rows - mean).astype(BF16)
+            xs_ref[half, layer, 0:HALF] = rows[:, 0:LANES]
+            xs_ref[half, layer, HALF:2 * HALF] = rows[:, LANES:]
+            high = mean.astype(BF16).astype(F32)
+            terms = [part[:, at:at + LANES] for part in (high, mean - high) for at in (0, LANES)]
+            tail = row
+            for at, term in enumerate(terms):
+                tail = jnp.where(at_row == at, term, tail)
+            xs_ref[half, layer, 2 * HALF:] = tail.astype(BF16)
+
+    writes = []
+
+    def write(first, last):
+        span = pl.ds(first, last - first)
+        at = len(writes)
+        writes.append(pltpu.make_async_copy(xs_ref.at[:, span], xs_out.at[:, span], out_sems.at[at]))
+        writes.append(pltpu.make_async_copy(slope_ref.at[span], slope_out.at[span], out_sems.at[at + 1]))
+        for copy in writes[-2:]:
+            copy.start()
+
     x = x_ref[...]
     for layer in range(LAYERS):
-        for copy in arrivals[layer]:
-            copy.wait()
-        copies.append(pltpu.make_async_copy(w_ref.at[layer], w_out.at[layer], sems.at[2, layer]))
-        copies[-1].start()
+        if layer in (0, FIRST):
+            for copy in sum(arrivals[0:FIRST] if layer == 0 else arrivals[FIRST:], []):
+                copy.wait()
+        z = jnp.dot(x, w_ref[layer].reshape(GW, GW), preferred_element_type=F32)
+        z_ref[layer] = z
+        if layer > 0:
+            pack_layer(layer - 1)
         scale = rows_ref[layer, 0:1] + rows_ref[layer, 4:5]
         shift = rows_ref[layer, 1:2] + rows_ref[layer, 5:6]
-        z = jnp.dot(x, w_ref[layer].reshape(GW, GW), preferred_element_type=F32)
         active = z * scale + shift
         gate = 1.0 / (1.0 + jnp.exp2(active * -LOG2E))
         after = active * gate
         x = after.astype(BF16)
         slope_ref[layer] = (gate * ((active - after) + 1.0) * scale).astype(BF16)
-        copies.append(pltpu.make_async_copy(slope_ref.at[layer], slope_out.at[layer], sems.at[3, layer]))
-        copies[-1].start()
-        row = rows_ref[layer, pl.ds(chip // 2, 1), :]
-        row = jnp.broadcast_to(lax.select(chip % 2 == 0, row[:, 0:LANES], row[:, LANES:]), (TAIL, LANES))
-        for half in range(2):
-            rows = z[half * HALF:(half + 1) * HALF]
-            mean = jnp.sum(rows, axis=0, keepdims=True) * (1.0 / HALF)
-            rows = (rows - mean).astype(BF16)
-            out_ref[half, layer, 0:HALF] = rows[:, 0:LANES]
-            out_ref[half, layer, HALF:2 * HALF] = rows[:, LANES:]
-            high = mean.astype(BF16).astype(F32)
-            terms = [part[:, at:at + LANES] for part in (high, mean - high) for at in (0, LANES)]
-            tail = row
-            for at, term in enumerate(terms):
-                tail = jnp.where(at_row == at, term, tail)
-            out_ref[half, layer, 2 * HALF:] = tail.astype(BF16)
-    for copy in copies:
+        if layer == LAYERS // 2:
+            write(0, LAYERS // 2)
+    pack_layer(LAYERS - 1)
+    write(LAYERS // 2, LAYERS)
+    for copy in writes:
         copy.wait()
 
 
@@ -179,6 +197,11 @@
     row_at = (j_ref[0] % 2 * 4 + j_ref[0] // 2) * PIECE
     means = all_means(r_ref)
     shifted = [m - jnp.mean(m, axis=0, keepdims=True) for m in means]
+    highs = [m.astype(BF16).astype(F32) for m in shifted]
+    lows = [m - high for m, high in zip(shifted, highs)]
+    spare = jnp.zeros((PARTS, GW), F32)
+    firsts = [jnp.concatenate([high, high, low, spare], axis=0).astype(BF16) for high, low in zip(highs, lows)]
+    seconds = [jnp.concatenate([high, low, high, spare], axis=0).astype(BF16) for high, low in zip(highs, lows)]
     total = jnp.sum(r_ref[:, 0:3 * PIECE].astype(F32), axis=0) * (1.0 / TOTAL)
     diagonal = (
         lax.broadcasted_iota(jnp.int32, (PIECE, GW), 0) + row_at
@@ -186,7 +209,7 @@
     )
     for at, (a, b) in enumerate(((0, 0), (0, 1), (1, 1))):
         scratch_ref[...] = lax.dot_general(
-            shifted[a], shifted[b], (((0,), (0,)), ((), ())), precision=HIGHEST, preferred_element_type=F32
+            firsts[a], seconds[b], (((0,), (0,)), ((), ())), preferred_element_type=F32
         )
         part = total[at * PIECE:(at + 1) * PIECE] + scratch_ref[pl.ds(row_at, PIECE), :] * (1.0 / PARTS)
         if a == b:
@@ -232,14 +255,14 @@
         out_ref[g, :, 2 * HALF:] = tail
 
 
-def backward_kernel(q_ref, w_in, slope_in, out_ref, w_ref, slope_ref, sems):
-    copies = [None] * LAYERS
-    for layer in reversed(range(LAYERS)):
-        copies[layer] = [pltpu.make_async_copy(w_in.at[layer], w_ref.at[layer], sems.at[0, layer])]
-        if layer < LAYERS - 1:
-            copies[layer].append(pltpu.make_async_copy(slope_in.at[layer], slope_ref.at[layer], sems.at[1, layer]))
-        for copy in copies[layer]:
-            copy.start()
+def backward_kernel(q_ref, own_in, other_in, slope_in, out_ref, w_ref, slope_ref, sems, slope_sem):
+    core = lax.axis_index("c")
+    arrivals = [weight_reads(own_in, other_in, w_ref, core, sems, layer) for layer in range(LAYERS)]
+    parts = [pl.ds(LAYERS - FIRST, FIRST), pl.ds(0, LAYERS - FIRST)]
+    slopes = [pltpu.make_async_copy(slope_in.at[at], slope_ref.at[at], slope_sem.at[n]) for n, at in enumerate(parts)]
+    arrivals = [sum(arrivals[LAYERS - FIRST:], []) + slopes[:1], sum(arrivals[:LAYERS - FIRST], []) + slopes[1:]]
+    for copy in arrivals[0] + arrivals[1]:
+        copy.start()
     loss = jnp.zeros((1, LANES), F32)
     grad = None
     for layer in reversed(range(LAYERS)):
@@ -248,8 +271,9 @@
         pull = jnp.concatenate(
             [q_ref[:, layer, 0:HALF].reshape(ROWS, LANES), q_ref[:, layer, HALF:2 * HALF].reshape(ROWS, LANES)], axis=1
         )
-        for copy in copies[layer]:
-            copy.wait()
+        if layer in (LAYERS - 1, LAYERS - 1 - FIRST):
+            for copy in arrivals[0 if layer == LAYERS - 1 else 1]:
+                copy.wait()
         if grad is not None:
             pull = (grad * slope_ref[layer].astype(F32) + pull.astype(F32)).astype(BF16)
         grad = lax.dot_general(
@@ -321,16 +345,16 @@
         return pltpu.with_memory_space_constraint(array, pltpu.VMEM)
 
     layers = [pltpu.VMEM((LAYERS, 2, CHIPS, SLICE, GW), BF16), pltpu.VMEM((LAYERS, ROWS, GW), BF16)]
-    xs, chain_weights, slope = pl.pallas_call(
+    sems = pltpu.SemaphoreType.DMA((2, LAYERS))
+    pieces_shape = (2, LAYERS, 2 * HALF + TAIL, LANES)
+    xs, slope = pl.pallas_call(
         forward_kernel,
-        out_shape=[
-            pltpu.VMEM((2, LAYERS, 2 * HALF + TAIL, LANES), BF16),
-            jax.ShapeDtypeStruct((LAYERS, 2, CHIPS, SLICE, GW), BF16),
-            jax.ShapeDtypeStruct((LAYERS, ROWS, GW), BF16),
-        ],
+        out_shape=[jax.ShapeDtypeStruct(pieces_shape, BF16), jax.ShapeDtypeStruct((LAYERS, ROWS, GW), BF16)],
         in_specs=[vmem, vmem, hbm, vmem],
-        out_specs=[vmem, hbm, hbm],
-        scratch_shapes=layers + [pltpu.VMEM((LAYERS, PROWS, GW), F32), pltpu.SemaphoreType.DMA((4, LAYERS))],
+        out_specs=[hbm, hbm],
+        scratch_shapes=layers
+        + [pltpu.VMEM((LAYERS, PROWS, GW), F32), pltpu.VMEM((LAYERS, ROWS, GW), F32), pltpu.VMEM(pieces_shape, BF16)]
+        + [sems, pltpu.SemaphoreType.DMA((4,))],
         name="fwd",
     )(near(rows), near(layer_parts), own, near(other))
 
@@ -378,11 +402,11 @@
     grads = pl.pallas_call(
         backward_kernel,
         out_shape=pltpu.VMEM((8, 16 + TAIL, GW), BF16),
-        in_specs=[vmem, hbm, hbm],
+        in_specs=[vmem, hbm, hbm, hbm],
         out_specs=vmem,
-        scratch_shapes=layers + [pltpu.SemaphoreType.DMA((2, LAYERS))],
+        scratch_shapes=layers + [sems, pltpu.SemaphoreType.DMA((2,))],
         name="bwd",
-    )(near(pulls.reshape(2, LAYERS, 2 * HALF + TAIL, LANES)), chain_weights, slope)
+    )(near(pulls.reshape(2, LAYERS, 2 * HALF + TAIL, LANES)), own, other, slope)
     grads = lax.all_to_all(grads, ("g", "k"), 0, 0, tiled=True)
     image_grad, loss = pl.pallas_call(
         output_kernel,

time: 165 us -> 162 us (0.982)
  Pallas kernels: 17.6 us -> 14.8 us
    pallas_call x1, Pallas kernels: 6.82 us -> 5.06 us  [shards(): pl.pallas_call(forward_kernel, out_shape=[jax.ShapeDtypeStruct(pieces_sha...]
where the time goes in v4:
time: 162 us; the launch traced here: 160 us
  blocking collectives  110 us (68%)
  waiting for transfers between devices  19.1 us (12%)
  starting transfers between devices  15.1 us (9%)
  Pallas kernels  14.8 us (9%)
    all_to_all x1, blocking collectives, shards(): layer_parts = lax.all_to_all(message, ('k', 'h', 'g'), 0, 0, tiled=True)  27.5 us
    all_to_all x1, blocking collectives, shards(): lax.all_to_all(pulls.reshape(2 * CHIPS, 2 * HALF + TAIL, LANES), ('g', 'y...  21.1 us
    all_to_all x1, blocking collectives, shards(): lax.all_to_all(jnp.broadcast_to(own[None], (CHIPS, LAYERS, SLICE, GW)), (...  19.9 us
    all_to_all x1, blocking collectives, shards(): grads = lax.all_to_all(grads, ('g', 'k'), 0, 0, tiled=True)  16.8 us
    all_to_all x1, waiting for transfers between devices, shards(): lax.all_to_all(xs.reshape(2 * CHIPS, 2 * HALF + TAIL, LANES), ('g', 'y',...  15.8 us
    all_to_all x1, blocking collectives, shards(): pieces = lax.all_to_all(pieces, ('g', 'h'), 0, 0, tiled=True)  11.2 us
    all_to_all x1, blocking collectives, shards(): lax.all_to_all(deviation, ('g', 'h'), 0, 0, tiled=True)  8.32 us
    ppermute x1, starting transfers between devices, shards(): other = lax.ppermute(own, 'c', [(0, 1), (1, 0)])  6.76 us
  transfers between devices with their start and end apart: 3, of which 3 were waited for; matrix products, arithmetic and copies ran while one was open for 0% of the time, Pallas kernels for 0%

profile of v4, /device:TPU:1, one launch (start us, length us, event | category | flops | bytes accessed | tf_op | source)
XLA Modules:
  0.0 159.5 jit_solution(1013627177404860225)
XLA Ops:
  0.6 0.9 pack.1
  1.6 27.5 %all_to_all.35.par_ref = bf16[16,16,256]{2,1,0:T(8,128)(2,1)S(1)} all-to-all(bf16[16,16,256]{2,1,0:T(8,128)(2,1)S(1)} %bitcast.12), channel_id=1, replica_groups=mesh['k'=4,'h'=2,'g'=2,'x'=4,'y'=4,'c'=2] {'k','h','g'}, dimensions={0} | all-to-all | bytes 262144 | tf_op jit(solution)/shard_map/all_to_all | solution.py:338
  29.1 0.1 broadcast_in_dim.2
  29.2 19.9 %all_to_all.36.own_in = bf16[16,16,8,256]{3,2,1,0:T(8,128)(2,1)S(1)} all-to-all(bf16[16,16,8,256]{3,2,1,0:T(8,128)(2,1)S(1)} %broadcast_in_dim.2), channel_id=1, replica_groups=mesh['k'=4,'h'=2,'g'=2,'x'=4,'y'=4,'c'=2] {'y','x'}, dimensions={0} | all-to-all | bytes 2097152 | tf_op jit(solution)/shard_map/all_to_all | solution.py:341
  49.1 0.0 copy-start.1
  49.1 6.8 %collective-permute-start = (bf16[16,16,8,256]{3,2,1,0:T(8,128)(2,1)S(1)}, bf16[16,16,8,256]{3,2,1,0:T(8,128)(2,1)S(1)}, u32[]{:S(2)}, u32[]{:S(2)}) collective-permute-start(bf16[16,16,8,256]{3,2,1,0:T(8,128)(2,1)S(1)} %all_to_all.36.own_in), channel_id=1, source_target_pairs={{0,1},{1,0},{2,3},{3,2},{4,5},{5,4},{6,7},{7,6},{8,9},{9,8},{10,11... | collective-permute-start | bytes 3145736 | tf_op jit(solution)/shard_map/ppermute | solution.py:342
  55.8 2.3 %collective-permute-done.other_in = bf16[16,16,8,256]{3,2,1,0:T(8,128)(2,1)S(1)} collective-permute-done((bf16[16,16,8,256]{3,2,1,0:T(8,128)(2,1)S(1)}, bf16[16,16,8,256]{3,2,1,0:T(8,128)(2,1)S(1)}, u32[]{:S(2)}, u32[]{:S(2)}) %collective-permute-start) | collective-permute-done | bytes 1048608 | tf_op jit(solution)/shard_map/ppermute | solution.py:342
  58.1 0.0 copy-start
  58.1 0.0 copy-done.1
  58.1 5.1 %fwd.1 = (bf16[2,16,136,128]{3,2,1,0:T(8,128)(2,1)}, bf16[16,128,256]{2,1,0:T(8,128)(2,1)}) custom-call(bf16[128,256]{1,0:T(8,128)(2,1)S(1)} %get-tuple-element.13.x_ref, bf16[16,16,256]{2,1,0:T(8,128)(2,1)S(1)} %all_to_all.35.par_ref, bf16[16,16,8,256]{3,2,1,0:T(8,128)(2,1)} %copy-done.1, bf16[16,16,8,256]{3,2,1,0:T(8,128)(2,1)S(1)} %collective-permute-done.other_in), custom_call_target="tpu_custom_call" | custom-call | tf_op jit(solution)/shard_map/fwd/pallas_call | solution.py:350
  63.2 0.0 copy-done
  63.2 4.1 %all-to-all-start.2 = ((bf16[32,136,128]{2,1,0:T(8,128)(2,1)}), bf16[32,136,128]{2,1,0:T(8,128)(2,1)S(1)}, u32[]{:S(2)}, u32[]{:S(2)}) async-start(bf16[32,136,128]{2,1,0:T(8,128)(2,1)} %bitcast.13), calls=%async_computation.2 | async-start | bytes 2228224 | tf_op jit(solution)/shard_map/all_to_all | solution.py:361
  67.3 15.8 %all-to-all-done.2 = bf16[32,136,128]{2,1,0:T(8,128)(2,1)S(1)} async-done(((bf16[32,136,128]{2,1,0:T(8,128)(2,1)}), bf16[32,136,128]{2,1,0:T(8,128)(2,1)S(1)}, u32[]{:S(2)}, u32[]{:S(2)}) %all-to-all-start.2) | async-done | bytes 1114144 | tf_op jit(solution)/shard_map/all_to_all | solution.py:361
  83.1 1.4 gram.1
  84.5 4.2 %collective-permute-start.1 = (bf16[392,256]{1,0:T(8,128)(2,1)S(1)}, bf16[392,256]{1,0:T(8,128)(2,1)S(1)}, u32[]{:S(2)}, u32[]{:S(2)}) collective-permute-start(bf16[392,256]{1,0:T(8,128)(2,1)S(1)} %get-tuple-element.18), channel_id=1, source_target_pairs={{0,1},{1,0},{2,3},{3,2},{4,5},{5,4},{6,7},{7,6},{8,9},{9,8},{10,11... | collective-permute-start | bytes 602120 | tf_op jit(solution)/shard_map/ppermute | solution.py:375
  88.7 1.1 collective-permute-done.1.got_ref
  89.8 0.1 chip.1
  89.8 11.2 %all_to_all.37.r_ref = bf16[4,112,256]{2,1,0:T(8,128)(2,1)S(1)} all-to-all(bf16[4,112,256]{2,1,0:T(8,128)(2,1)S(1)} %chip.1), channel_id=1, replica_groups=mesh['k'=4,'h'=2,'g'=2,'x'=4,'y'=4,'c'=2] {'g','h'}, dimensions={0} | all-to-all | bytes 458752 | tf_op jit(solution)/shard_map/all_to_all | solution.py:379
  101.0 0.3 deviation.1
  101.4 8.3 %all_to_all.38 = bf16[4,96,256]{2,1,0:T(8,128)(2,1)S(1)} all-to-all(bf16[4,96,256]{2,1,0:T(8,128)(2,1)S(1)} %deviation.1), channel_id=1, replica_groups=mesh['k'=4,'h'=2,'g'=2,'x'=4,'y'=4,'c'=2] {'g','h'}, dimensions={0} | all-to-all | bytes 393216 | tf_op jit(solution)/shard_map/all_to_all | solution.py:389
  109.7 4.8 %all-gather = bf16[8,96,256]{2,1,0:T(8,128)(2,1)S(1)} all-gather(bf16[4,96,256]{2,1,0:T(8,128)(2,1)S(1)} %all_to_all.38), channel_id=2, replica_groups=mesh['k'=4,'h'=2,'g'=2,'x'=4,'y'=4,'c'=2] {'c'}, dimensions={0}, use_global_device_ids=true | all-gather | bytes 589824 | tf_op jit(solution)/shard_map/all_gather | solution.py:389
  114.5 2.2 %pull.1 = bf16[2,16,136,128]{3,2,1,0:T(8,128)(2,1)S(1)} custom-call(bf16[2,4,96,256]{3,2,1,0:T(8,128)(2,1)S(1)} %bitcast.11, bf16[4,112,256]{2,1,0:T(8,128)(2,1)S(1)} %all_to_all.37.r_ref, bf16[8,256]{1,0:T(8,128)(2,1)S(1)} %get-tuple-element.17.tail_ref, f32[2,4,256]{2,1,0:T(4,128)S(1)} %get-tuple-element.19.par_ref, ...), custom_call_target="tpu_custom_call" | custom-call | tf_op jit(solution)/shard_map/pull/pallas_call | solution.py:313
  116.7 21.1 %all_to_all.39 = bf16[32,136,128]{2,1,0:T(8,128)(2,1)S(1)} all-to-all(bf16[32,136,128]{2,1,0:T(8,128)(2,1)S(1)} %bitcast.10), channel_id=1, replica_groups=mesh['k'=4,'h'=2,'g'=2,'x'=4,'y'=4,'c'=2] {'g','y','x'}, dimensions={0} | all-to-all | bytes 2228224 | tf_op jit(solution)/shard_map/all_to_all | solution.py:400
  137.9 4.2 %bwd.1 = bf16[8,24,256]{2,1,0:T(8,128)(2,1)S(1)} custom-call(bf16[2,16,136,128]{3,2,1,0:T(8,128)(2,1)S(1)} %bitcast.9, bf16[16,16,8,256]{3,2,1,0:T(8,128)(2,1)} %copy-done.1, bf16[16,16,8,256]{3,2,1,0:T(8,128)(2,1)} %copy-done, bf16[16,128,256]{2,1,0:T(8,128)(2,1)} %get-tuple-element.21.slope_in), custom_call_target="tpu_custom_call" | custom-call | tf_op jit(solution)/shard_map/bwd/pallas_call | solution.py:402
  142.1 16.8 %all_to_all.40.r_ref = bf16[8,24,256]{2,1,0:T(8,128)(2,1)S(1)} all-to-all(bf16[8,24,256]{2,1,0:T(8,128)(2,1)S(1)} %bwd.1), channel_id=1, replica_groups=mesh['k'=4,'h'=2,'g'=2,'x'=4,'y'=4,'c'=2] {'g','k'}, dimensions={0} | all-to-all | bytes 196608 | tf_op jit(solution)/shard_map/all_to_all | solution.py:410
  158.9 0.6 outputs.1
  (1 shorter events, 0.0 us)
Async XLA Ops:
  49.1 9.0 %copy-start.1 = (bf16[16,16,8,256]{3,2,1,0:T(8,128)(2,1)}, bf16[16,16,8,256]{3,2,1,0:T(8,128)(2,1)S(1)}, u32[]{:S(2)}) copy-start(bf16[16,16,8,256]{3,2,1,0:T(8,128)(2,1)S(1)} %all_to_all.36.own_in) | copy-start | bytes 3145732
  49.1 9.0 %collective-permute-start = (bf16[16,16,8,256]{3,2,1,0:T(8,128)(2,1)S(1)}, bf16[16,16,8,256]{3,2,1,0:T(8,128)(2,1)S(1)}, u32[]{:S(2)}, u32[]{:S(2)}) collective-permute-start(bf16[16,16,8,256]{3,2,1,0:T(8,128)(2,1)S(1)} %all_to_all.36.own_in), channel_id=1, source_target_pairs={{0,1},{1,0},{2,3},{3,2},{4,5},{5,4},{6,7},{7,6},{8,9},{9,8},{10,11... | collective-permute-start | bytes 3145736 | tf_op jit(solution)/shard_map/ppermute | solution.py:342
  58.1 5.1 %copy-start = (bf16[16,16,8,256]{3,2,1,0:T(8,128)(2,1)}, bf16[16,16,8,256]{3,2,1,0:T(8,128)(2,1)S(1)}, u32[]{:S(2)}) copy-start(bf16[16,16,8,256]{3,2,1,0:T(8,128)(2,1)S(1)} %collective-permute-done.other_in) | copy-start | bytes 3145732
  63.2 19.9 %all-to-all-start.2 = ((bf16[32,136,128]{2,1,0:T(8,128)(2,1)}), bf16[32,136,128]{2,1,0:T(8,128)(2,1)S(1)}, u32[]{:S(2)}, u32[]{:S(2)}) async-start(bf16[32,136,128]{2,1,0:T(8,128)(2,1)} %bitcast.13), calls=%async_computation.2 | async-start | bytes 2228224 | tf_op jit(solution)/shard_map/all_to_all | solution.py:361
  84.5 5.3 %collective-permute-start.1 = (bf16[392,256]{1,0:T(8,128)(2,1)S(1)}, bf16[392,256]{1,0:T(8,128)(2,1)S(1)}, u32[]{:S(2)}, u32[]{:S(2)}) collective-permute-start(bf16[392,256]{1,0:T(8,128)(2,1)S(1)} %get-tuple-element.18), channel_id=1, source_target_pairs={{0,1},{1,0},{2,3},{3,2},{4,5},{5,4},{6,7},{7,6},{8,9},{9,8},{10,11... | collective-permute-start | bytes 602120 | tf_op jit(solution)/shard_map/ppermute | solution.py:375

commit v5 on v4

--- a/solution.py
+++ b/solution.py
@@ -136,7 +136,7 @@
         scale = rows_ref[layer, 0:1] + rows_ref[layer, 4:5]
         shift = rows_ref[layer, 1:2] + rows_ref[layer, 5:6]
         active = z * scale + shift
-        gate = 1.0 / (1.0 + jnp.exp2(active * -LOG2E))
+        gate = 1.0 / (1.0 + jnp.exp2(z * (scale * -LOG2E) + shift * -LOG2E))
         after = active * gate
         x = after.astype(BF16)
         slope_ref[layer] = (gate * ((active - after) + 1.0) * scale).astype(BF16)
@@ -148,15 +148,17 @@
         copy.wait()
 
 
-def gram_kernel(j_ref, x_ref, keep_ref, send_ref, tail_ref, par_ref, zc_ref):
-    core = j_ref[0] % 2
-    means = []
+def gram_kernel(x_ref, keep_ref, send_ref, tail_ref, par_ref, zc_out, zc_ref, sems):
+    core = lax.axis_index("c")
+    means, writes = [], []
     for g in range(2):
         tails = x_ref[g, :, 2 * HALF:].astype(F32)
         mean = sum(jnp.concatenate([tails[:, at:at + 1], tails[:, at + 1:at + 2]], axis=2) for at in (0, 2))
         means.append(jnp.mean(mean, axis=0))
         rows = jnp.concatenate([x_ref[g, :, 0:HALF], x_ref[g, :, HALF:2 * HALF]], axis=2).astype(F32)
         zc_ref[g] = (rows + (mean - means[g][None])).astype(BF16).reshape(HOME, GW)
+        writes.append(pltpu.make_async_copy(zc_ref.at[g], zc_out.at[g], sems.at[g]))
+        writes[g].start()
         packed = [jnp.concatenate([tails[2 * r, 6:7], tails[2 * r + 1, 6:7]], axis=1) for r in range(PROWS)]
         par_ref[g] = jnp.concatenate([packed[r] + packed[r + 4] for r in range(4)], axis=0)
     parts = [split3(mean) for mean in means]
@@ -172,6 +174,8 @@
             rows = pl.ds((3 * j + at) * PIECE, PIECE)
             keep_ref[rows] = keep[j * PIECE:(j + 1) * PIECE]
             send_ref[rows] = send[j * PIECE:(j + 1) * PIECE]
+    for copy in writes:
+        copy.wait()
 
 
 def chip_kernel(j_ref, keep_ref, tail_ref, got_ref, out_ref):
@@ -218,7 +222,15 @@
             e_ref[j, at * PIECE:(at + 1) * PIECE] = part.astype(BF16)
 
 
-def pull_kernel(e_ref, r_ref, tail_ref, par_ref, zc_ref, out_ref):
+CHUNKS = 1
+
+
+def pull_kernel(e_ref, r_ref, tail_ref, par_ref, zc_in, out_ref, zc_ref, sems):
+    reads = []
+    for n in range(CHUNKS):
+        rows = pl.ds(n * (HOME // CHUNKS), HOME // CHUNKS)
+        reads.append(pltpu.make_async_copy(zc_in.at[:, rows], zc_ref.at[:, rows], sems.at[n]))
+        reads[n].start()
     means = all_means(r_ref)
     mine = tail_ref[...].astype(F32)
     mats = [e_ref[:, :, at * PIECE:(at + 1) * PIECE].reshape(GW, GW) for at in range(3)]
@@ -241,17 +253,27 @@
     tail = jnp.broadcast_to(tail[None], (CHIPS, TAIL, LANES))
     plain, crossed = (((1,), (0,)), ((), ())), (((1,), (1,)), ((), ()))
 
-    def product(side, at, dims):
-        lhs = jnp.concatenate([zc_ref[side], offset[side]], axis=0)
-        return lax.dot_general(lhs, mats[at], dims, preferred_element_type=F32)
-
+    def both(lhs, g):
+        (at, first), (bt, second) = ((0, plain), (1, crossed)) if g == 0 else ((1, plain), (2, plain))
+        return lax.dot_general(lhs[0], mats[at], first, preferred_element_type=F32) + lax.dot_general(
+            lhs[1], mats[bt], second, preferred_element_type=F32
+        )
+
+    rows = []
     for g in range(2):
-        pull = product(0, 0, plain) + product(1, 1, crossed) if g == 0 else product(0, 1, plain) + product(1, 2, plain)
-        row = pull[HOME:HOME + 1] + pull[HOME + 1:HOME + 2] + pull[HOME + 2:HOME + 3] + away[g]
-        pull = pull[0:HOME] + row
-        pull = pull.astype(BF16).reshape(CHIPS, HALF, GW)
-        out_ref[g, :, 0:HALF] = pull[:, :, 0:LANES]
-        out_ref[g, :, HALF:2 * HALF] = pull[:, :, LANES:]
+        row = both(offset, g)
+        rows.append(row[0:1] + row[1:2] + row[2:3] + away[g])
+    size = HOME // CHUNKS
+    chips = CHIPS // CHUNKS
+    for copy in reads:
+        copy.wait()
+    for n in range(CHUNKS):
+        for g in range(2):
+            pull = both([zc_ref[side, n * size:(n + 1) * size] for side in range(2)], g) + rows[g]
+            pull = pull.astype(BF16).reshape(chips, HALF, GW)
+            out_ref[g, n * chips:(n + 1) * chips, 0:HALF] = pull[:, :, 0:LANES]
+            out_ref[g, n * chips:(n + 1) * chips, HALF:2 * HALF] = pull[:, :, LANES:]
+    for g in range(2):
         out_ref[g, :, 2 * HALF:] = tail
 
 
@@ -278,7 +300,7 @@
             pull = (grad * slope_ref[layer].astype(F32) + pull.astype(F32)).astype(BF16)
         grad = lax.dot_general(
             pull, w_ref[layer].reshape(GW, GW), (((1,), (1,)), ((), ())), preferred_element_type=F32
-        ).astype(BF16).astype(F32)
+        )
     loss = jnp.concatenate([loss, loss], axis=1)
     tail = jnp.concatenate(list(split3(loss)) + [jnp.zeros((TAIL - 3, GW), F32)], axis=0).astype(BF16)
     grad = grad.astype(BF16)
@@ -298,26 +320,21 @@
     loss_ref[...] = loss * (1.0 / (LAYERS * BLOCKS * 2 * GW))
 
 
-LARGE = 1200000
-
-
-def is_large(shape, dtype):
-    return math.prod(shape) * jnp.dtype(dtype).itemsize > LARGE
-
-
-def kernel_call(kernel, outs, name, *args, scalars=(), scratch=(), far=(), loose=()):
+def near(array):
+    return pltpu.with_memory_space_constraint(array, pltpu.VMEM)
+
+
+def kernel_call(kernel, outs, name, *args, scalars=(), scratch=()):
     vmem = pl.BlockSpec(memory_space=pltpu.VMEM)
     smem = pl.BlockSpec(memory_space=pltpu.SMEM)
-    placed = [arg if is_large(arg.shape, arg.dtype) else pltpu.with_memory_space_constraint(arg, pltpu.VMEM) for arg in args]
-    placed += [pltpu.with_memory_space_constraint(arg, pltpu.HBM) for arg in far]
     return pl.pallas_call(
         kernel,
-        out_shape=[jax.ShapeDtypeStruct(*out) if is_large(*out) else pltpu.VMEM(*out) for out in outs] + list(loose),
-        in_specs=[smem] * len(scalars) + [vmem] * len(placed),
-        out_specs=[vmem] * (len(outs) + len(loose)),
+        out_shape=[pltpu.VMEM(*out) for out in outs],
+        in_specs=[smem] * len(scalars) + [vmem] * len(args),
+        out_specs=[vmem] * len(outs),
         scratch_shapes=list(scratch),
         name=name,
-    )(*scalars, *placed)
+    )(*scalars, *[near(arg) for arg in args])
 
 
 def shards(images, weights, bn_mean, bn_var, bn_gain, bn_bias):
@@ -341,9 +358,6 @@
     own = lax.all_to_all(jnp.broadcast_to(own[None], (CHIPS, LAYERS, SLICE, GW)), ("y", "x"), 0, 0, tiled=True)
     other = lax.ppermute(own, "c", [(0, 1), (1, 0)])
 
-    def near(array):
-        return pltpu.with_memory_space_constraint(array, pltpu.VMEM)
-
     layers = [pltpu.VMEM((LAYERS, 2, CHIPS, SLICE, GW), BF16), pltpu.VMEM((LAYERS, ROWS, GW), BF16)]
     sems = pltpu.SemaphoreType.DMA((2, LAYERS))
     pieces_shape = (2, LAYERS, 2 * HALF + TAIL, LANES)
@@ -359,19 +373,21 @@
     )(near(rows), near(layer_parts), own, near(other))
 
     home = lax.all_to_all(xs.reshape(2 * CHIPS, 2 * HALF + TAIL, LANES), ("g", "y", "x"), 0, 0, tiled=True)
-    keep, send, tail, params, centered = kernel_call(
+    held = pltpu.VMEM((2, HOME, GW), BF16)
+    keep, send, tail, params, centered = pl.pallas_call(
         gram_kernel,
-        [
-            ((4 * 3 * PIECE, GW), F32),
-            ((4 * 3 * PIECE + TAIL, GW), BF16),
-            ((TAIL, GW), BF16),
-            ((2, 4, GW), F32),
+        out_shape=[
+            pltpu.VMEM((4 * 3 * PIECE, GW), F32),
+            pltpu.VMEM((4 * 3 * PIECE + TAIL, GW), BF16),
+            pltpu.VMEM((TAIL, GW), BF16),
+            pltpu.VMEM((2, 4, GW), F32),
+            jax.ShapeDtypeStruct((2, HOME, GW), BF16),
         ],
-        "gram",
-        home.reshape(2, CHIPS, 2 * HALF + TAIL, LANES),
-        scalars=[part],
-        loose=[jax.ShapeDtypeStruct((2, HOME, GW), BF16)],
-    )
+        in_specs=[vmem],
+        out_specs=[vmem] * 4 + [hbm],
+        scratch_shapes=[held, pltpu.SemaphoreType.DMA((2,))],
+        name="gram",
+    )(near(home.reshape(2, CHIPS, 2 * HALF + TAIL, LANES)))
     got = lax.ppermute(send, "c", [(0, 1), (1, 0)])
     (pieces,) = kernel_call(
         chip_kernel, [((4, 3 * PIECE + 2 * TAIL, GW), BF16)], "chip", keep, tail, got, scalars=[part]
@@ -387,16 +403,14 @@
         scratch=[pltpu.VMEM((GW, GW), F32)],
     )
     deviation = lax.all_gather(lax.all_to_all(deviation, ("g", "h"), 0, 0, tiled=True), "c", axis=0)
-    (pulls,) = kernel_call(
+    pulls = pl.pallas_call(
         pull_kernel,
-        [((2, CHIPS, 2 * HALF + TAIL, LANES), BF16)],
-        "pull",
-        deviation,
-        pieces,
-        tail,
-        params,
-        far=[centered],
-    )
+        out_shape=pltpu.VMEM((2, CHIPS, 2 * HALF + TAIL, LANES), BF16),
+        in_specs=[vmem] * 4 + [hbm],
+        out_specs=vmem,
+        scratch_shapes=[held, pltpu.SemaphoreType.DMA((CHUNKS,))],
+        name="pull",
+    )(near(deviation), near(pieces), near(tail), near(params), centered)
     pulls = lax.all_to_all(pulls.reshape(2 * CHIPS, 2 * HALF + TAIL, LANES), ("g", "y", "x"), 0, 0, tiled=True)
 
     grads = pl.pallas_call(

time: 162 us -> 162 us (level)
  blocking collectives: 110 us -> 130 us
  waiting for transfers between devices: 19.1 us -> 3.31 us
  starting transfers between devices: 15.1 us -> 10.5 us
    all_to_all x0 -> x1, blocking collectives: none -> 21.7 us  [shards(): lax.all_to_all(xs.reshape(2 * CHIPS, 2 * HALF + TAIL, LANES), ('g', 'y',...]
    all_to_all x1 -> x0, waiting for transfers between devices: 15.8 us -> none  [shards(): lax.all_to_all(xs.reshape(2 * CHIPS, 2 * HALF + TAIL, LANES), ('g', 'y',...]
    all_to_all x1 -> x0, starting transfers between devices: 4.07 us -> none  [shards(): lax.all_to_all(xs.reshape(2 * CHIPS, 2 * HALF + TAIL, LANES), ('g', 'y',...]
  transfers between devices with their start and end apart: 3 -> 2, of which waited for: 3 -> 2; matrix products, arithmetic and copies ran while one was open for 0% -> 0% of each run, Pallas kernels for 0% -> 0%
where the time goes in v5:
time: 162 us; the launch traced here: 159 us
  blocking collectives  130 us (80%)
  Pallas kernels  14.5 us (9%)
  starting transfers between devices  10.5 us (6%)
  waiting for transfers between devices  3.31 us (2%)
    all_to_all x1, blocking collectives, shards(): layer_parts = lax.all_to_all(message, ('k', 'h', 'g'), 0, 0, tiled=True)  27.5 us
    all_to_all x1, blocking collectives, shards(): lax.all_to_all(xs.reshape(2 * CHIPS, 2 * HALF + TAIL, LANES), ('g', 'y',...  21.7 us
    all_to_all x1, blocking collectives, shards(): lax.all_to_all(pulls.reshape(2 * CHIPS, 2 * HALF + TAIL, LANES), ('g', 'y...  20.8 us
    all_to_all x1, blocking collectives, shards(): lax.all_to_all(jnp.broadcast_to(own[None], (CHIPS, LAYERS, SLICE, GW)), (...  19.9 us
    all_to_all x1, blocking collectives, shards(): grads = lax.all_to_all(grads, ('g', 'k'), 0, 0, tiled=True)  16.8 us
    all_to_all x1, blocking collectives, shards(): pieces = lax.all_to_all(pieces, ('g', 'h'), 0, 0, tiled=True)  10.2 us
    all_to_all x1, blocking collectives, shards(): lax.all_to_all(deviation, ('g', 'h'), 0, 0, tiled=True)  8.31 us
    ppermute x1, starting transfers between devices, shards(): other = lax.ppermute(own, 'c', [(0, 1), (1, 0)])  6.76 us
  transfers between devices with their start and end apart: 2, of which 2 were waited for; matrix products, arithmetic and copies ran while one was open for 0% of the time, Pallas kernels for 0%

profile of v5, /device:TPU:1, one launch (start us, length us, event | category | flops | bytes accessed | tf_op | source)
XLA Modules:
  0.0 159.3 jit_solution(8370893315749489188)
XLA Ops:
  0.6 0.9 pack.1
  1.6 27.5 %all_to_all.35.par_ref = bf16[16,16,256]{2,1,0:T(8,128)(2,1)S(1)} all-to-all(bf16[16,16,256]{2,1,0:T(8,128)(2,1)S(1)} %bitcast.12), channel_id=1, replica_groups=mesh['k'=4,'h'=2,'g'=2,'x'=4,'y'=4,'c'=2] {'k','h','g'}, dimensions={0} | all-to-all | bytes 262144 | tf_op jit(solution)/shard_map/all_to_all | solution.py:355
  29.1 0.1 broadcast_in_dim.2
  29.2 19.9 %all_to_all.36.own_in = bf16[16,16,8,256]{3,2,1,0:T(8,128)(2,1)S(1)} all-to-all(bf16[16,16,8,256]{3,2,1,0:T(8,128)(2,1)S(1)} %broadcast_in_dim.2), channel_id=1, replica_groups=mesh['k'=4,'h'=2,'g'=2,'x'=4,'y'=4,'c'=2] {'y','x'}, dimensions={0} | all-to-all | bytes 2097152 | tf_op jit(solution)/shard_map/all_to_all | solution.py:358
  49.1 0.0 copy-start.1
  49.1 6.8 %collective-permute-start = (bf16[16,16,8,256]{3,2,1,0:T(8,128)(2,1)S(1)}, bf16[16,16,8,256]{3,2,1,0:T(8,128)(2,1)S(1)}, u32[]{:S(2)}, u32[]{:S(2)}) collective-permute-start(bf16[16,16,8,256]{3,2,1,0:T(8,128)(2,1)S(1)} %all_to_all.36.own_in), channel_id=1, source_target_pairs={{0,1},{1,0},{2,3},{3,2},{4,5},{5,4},{6,7},{7,6},{8,9},{9,8},{10,11... | collective-permute-start | bytes 3145736 | tf_op jit(solution)/shard_map/ppermute | solution.py:359
  55.8 2.3 %collective-permute-done.other_in = bf16[16,16,8,256]{3,2,1,0:T(8,128)(2,1)S(1)} collective-permute-done((bf16[16,16,8,256]{3,2,1,0:T(8,128)(2,1)S(1)}, bf16[16,16,8,256]{3,2,1,0:T(8,128)(2,1)S(1)}, u32[]{:S(2)}, u32[]{:S(2)}) %collective-permute-start) | collective-permute-done | bytes 1048608 | tf_op jit(solution)/shard_map/ppermute | solution.py:359
  58.1 0.0 copy-start
  58.1 0.0 copy-done.1
  58.1 5.1 %fwd.1 = (bf16[2,16,136,128]{3,2,1,0:T(8,128)(2,1)}, bf16[16,128,256]{2,1,0:T(8,128)(2,1)}) custom-call(bf16[128,256]{1,0:T(8,128)(2,1)S(1)} %get-tuple-element.13.x_ref, bf16[16,16,256]{2,1,0:T(8,128)(2,1)S(1)} %all_to_all.35.par_ref, bf16[16,16,8,256]{3,2,1,0:T(8,128)(2,1)} %copy-done.1, bf16[16,16,8,256]{3,2,1,0:T(8,128)(2,1)S(1)} %collective-permute-done.other_in), custom_call_target="tpu_custom_call" | custom-call | tf_op jit(solution)/shard_map/fwd/pallas_call | solution.py:364
  63.2 0.0 copy-done
  63.2 21.7 %all_to_all.37 = bf16[32,136,128]{2,1,0:T(8,128)(2,1)S(1)} all-to-all(bf16[32,136,128]{2,1,0:T(8,128)(2,1)} %bitcast.13), channel_id=1, replica_groups=mesh['k'=4,'h'=2,'g'=2,'x'=4,'y'=4,'c'=2] {'g','y','x'}, dimensions={0} | all-to-all | bytes 2228224 | tf_op jit(solution)/shard_map/all_to_all | solution.py:375
  84.9 1.2 gram.1
  86.1 3.8 %collective-permute-start.1 = (bf16[392,256]{1,0:T(8,128)(2,1)S(1)}, bf16[392,256]{1,0:T(8,128)(2,1)S(1)}, u32[]{:S(2)}, u32[]{:S(2)}) collective-permute-start(bf16[392,256]{1,0:T(8,128)(2,1)S(1)} %get-tuple-element.18), channel_id=1, source_target_pairs={{0,1},{1,0},{2,3},{3,2},{4,5},{5,4},{6,7},{7,6},{8,9},{9,8},{10,11... | collective-permute-start | bytes 602120 | tf_op jit(solution)/shard_map/ppermute | solution.py:391
  89.9 1.0 collective-permute-done.1.got_ref
  91.0 10.2 %all_to_all.38.r_ref = bf16[4,112,256]{2,1,0:T(8,128)(2,1)S(1)} all-to-all(bf16[4,112,256]{2,1,0:T(8,128)(2,1)S(1)} %chip.1), channel_id=1, replica_groups=mesh['k'=4,'h'=2,'g'=2,'x'=4,'y'=4,'c'=2] {'g','h'}, dimensions={0} | all-to-all | bytes 458752 | tf_op jit(solution)/shard_map/all_to_all | solution.py:395
  101.2 0.3 deviation.1
  101.6 8.3 %all_to_all.39 = bf16[4,96,256]{2,1,0:T(8,128)(2,1)S(1)} all-to-all(bf16[4,96,256]{2,1,0:T(8,128)(2,1)S(1)} %deviation.1), channel_id=1, replica_groups=mesh['k'=4,'h'=2,'g'=2,'x'=4,'y'=4,'c'=2] {'g','h'}, dimensions={0} | all-to-all | bytes 393216 | tf_op jit(solution)/shard_map/all_to_all | solution.py:405
  109.9 4.8 %all-gather = bf16[8,96,256]{2,1,0:T(8,128)(2,1)S(1)} all-gather(bf16[4,96,256]{2,1,0:T(8,128)(2,1)S(1)} %all_to_all.39), channel_id=2, replica_groups=mesh['k'=4,'h'=2,'g'=2,'x'=4,'y'=4,'c'=2] {'c'}, dimensions={0}, use_global_device_ids=true | all-gather | bytes 589824 | tf_op jit(solution)/shard_map/all_gather | solution.py:405
  114.7 2.1 %pull.1 = bf16[2,16,136,128]{3,2,1,0:T(8,128)(2,1)S(1)} custom-call(bf16[2,4,96,256]{3,2,1,0:T(8,128)(2,1)S(1)} %bitcast.11, bf16[4,112,256]{2,1,0:T(8,128)(2,1)S(1)} %all_to_all.38.r_ref, bf16[8,256]{1,0:T(8,128)(2,1)S(1)} %get-tuple-element.17.tail_ref, f32[2,4,256]{2,1,0:T(4,128)S(1)} %get-tuple-element.19.par_ref, ...), custom_call_target="tpu_custom_call" | custom-call | tf_op jit(solution)/shard_map/pull/pallas_call | solution.py:406
  116.8 20.8 %all_to_all.40 = bf16[32,136,128]{2,1,0:T(8,128)(2,1)S(1)} all-to-all(bf16[32,136,128]{2,1,0:T(8,128)(2,1)S(1)} %bitcast.10), channel_id=1, replica_groups=mesh['k'=4,'h'=2,'g'=2,'x'=4,'y'=4,'c'=2] {'g','y','x'}, dimensions={0} | all-to-all | bytes 2228224 | tf_op jit(solution)/shard_map/all_to_all | solution.py:414
  137.7 4.1 %bwd.1 = bf16[8,24,256]{2,1,0:T(8,128)(2,1)S(1)} custom-call(bf16[2,16,136,128]{3,2,1,0:T(8,128)(2,1)S(1)} %bitcast.9, bf16[16,16,8,256]{3,2,1,0:T(8,128)(2,1)} %copy-done.1, bf16[16,16,8,256]{3,2,1,0:T(8,128)(2,1)} %copy-done, bf16[16,128,256]{2,1,0:T(8,128)(2,1)} %get-tuple-element.21.slope_in), custom_call_target="tpu_custom_call" | custom-call | tf_op jit(solution)/shard_map/bwd/pallas_call | solution.py:416
  141.8 16.8 %all_to_all.41.r_ref = bf16[8,24,256]{2,1,0:T(8,128)(2,1)S(1)} all-to-all(bf16[8,24,256]{2,1,0:T(8,128)(2,1)S(1)} %bwd.1), channel_id=1, replica_groups=mesh['k'=4,'h'=2,'g'=2,'x'=4,'y'=4,'c'=2] {'g','k'}, dimensions={0} | all-to-all | bytes 196608 | tf_op jit(solution)/shard_map/all_to_all | solution.py:424
  158.7 0.6 outputs.1
  (2 shorter events, 0.0 us)
Async XLA Ops:
  49.1 9.0 %copy-start.1 = (bf16[16,16,8,256]{3,2,1,0:T(8,128)(2,1)}, bf16[16,16,8,256]{3,2,1,0:T(8,128)(2,1)S(1)}, u32[]{:S(2)}) copy-start(bf16[16,16,8,256]{3,2,1,0:T(8,128)(2,1)S(1)} %all_to_all.36.own_in) | copy-start | bytes 3145732
  49.1 9.0 %collective-permute-start = (bf16[16,16,8,256]{3,2,1,0:T(8,128)(2,1)S(1)}, bf16[16,16,8,256]{3,2,1,0:T(8,128)(2,1)S(1)}, u32[]{:S(2)}, u32[]{:S(2)}) collective-permute-start(bf16[16,16,8,256]{3,2,1,0:T(8,128)(2,1)S(1)} %all_to_all.36.own_in), channel_id=1, source_target_pairs={{0,1},{1,0},{2,3},{3,2},{4,5},{5,4},{6,7},{7,6},{8,9},{9,8},{10,11... | collective-permute-start | bytes 3145736 | tf_op jit(solution)/shard_map/ppermute | solution.py:359
  58.1 5.1 %copy-start = (bf16[16,16,8,256]{3,2,1,0:T(8,128)(2,1)}, bf16[16,16,8,256]{3,2,1,0:T(8,128)(2,1)S(1)}, u32[]{:S(2)}) copy-start(bf16[16,16,8,256]{3,2,1,0:T(8,128)(2,1)S(1)} %collective-permute-done.other_in) | copy-start | bytes 3145732
  86.1 4.8 %collective-permute-start.1 = (bf16[392,256]{1,0:T(8,128)(2,1)S(1)}, bf16[392,256]{1,0:T(8,128)(2,1)S(1)}, u32[]{:S(2)}, u32[]{:S(2)}) collective-permute-start(bf16[392,256]{1,0:T(8,128)(2,1)S(1)} %get-tuple-element.18), channel_id=1, source_target_pairs={{0,1},{1,0},{2,3},{3,2},{4,5},{5,4},{6,7},{7,6},{8,9},{9,8},{10,11... | collective-permute-start | bytes 602120 | tf_op jit(solution)/shard_map/ppermute | solution.py:391

commit v6 on v5

--- a/solution.py
+++ b/solution.py
@@ -76,7 +76,7 @@
     return jnp.concatenate([lax.select(core == 0, own, other), lax.select(core == 0, other, own)], axis=0)
 
 
-FIRST = 4
+GROUPS = (0, 2, 4, 8, LAYERS)
 
 
 def weight_reads(own_in, other_in, w_ref, core, sems, layer):
@@ -126,8 +126,8 @@
 
     x = x_ref[...]
     for layer in range(LAYERS):
-        if layer in (0, FIRST):
-            for copy in sum(arrivals[0:FIRST] if layer == 0 else arrivals[FIRST:], []):
+        if layer in GROUPS:
+            for copy in sum(arrivals[layer:GROUPS[GROUPS.index(layer) + 1]], []):
                 copy.wait()
         z = jnp.dot(x, w_ref[layer].reshape(GW, GW), preferred_element_type=F32)
         z_ref[layer] = z
@@ -279,12 +279,15 @@
 
 def backward_kernel(q_ref, own_in, other_in, slope_in, out_ref, w_ref, slope_ref, sems, slope_sem):
     core = lax.axis_index("c")
-    arrivals = [weight_reads(own_in, other_in, w_ref, core, sems, layer) for layer in range(LAYERS)]
-    parts = [pl.ds(LAYERS - FIRST, FIRST), pl.ds(0, LAYERS - FIRST)]
-    slopes = [pltpu.make_async_copy(slope_in.at[at], slope_ref.at[at], slope_sem.at[n]) for n, at in enumerate(parts)]
-    arrivals = [sum(arrivals[LAYERS - FIRST:], []) + slopes[:1], sum(arrivals[:LAYERS - FIRST], []) + slopes[1:]]
-    for copy in arrivals[0] + arrivals[1]:
-        copy.start()
+    arrivals = []
+    for n, (first, last) in enumerate(zip(GROUPS, GROUPS[1:])):
+        span = pl.ds(LAYERS - last, last - first)
+        group = [pltpu.make_async_copy(slope_in.at[span], slope_ref.at[span], slope_sem.at[n])]
+        for layer in range(LAYERS - last, LAYERS - first):
+            group += weight_reads(own_in, other_in, w_ref, core, sems, layer)
+        for copy in group:
+            copy.start()
+        arrivals.append(group)
     loss = jnp.zeros((1, LANES), F32)
     grad = None
     for layer in reversed(range(LAYERS)):
@@ -293,8 +296,8 @@
         pull = jnp.concatenate(
             [q_ref[:, layer, 0:HALF].reshape(ROWS, LANES), q_ref[:, layer, HALF:2 * HALF].reshape(ROWS, LANES)], axis=1
         )
-        if layer in (LAYERS - 1, LAYERS - 1 - FIRST):
-            for copy in arrivals[0 if layer == LAYERS - 1 else 1]:
+        if LAYERS - 1 - layer in GROUPS:
+            for copy in arrivals[GROUPS.index(LAYERS - 1 - layer)]:
                 copy.wait()
         if grad is not None:
             pull = (grad * slope_ref[layer].astype(F32) + pull.astype(F32)).astype(BF16)
@@ -418,7 +421,7 @@
         out_shape=pltpu.VMEM((8, 16 + TAIL, GW), BF16),
         in_specs=[vmem, hbm, hbm, hbm],
         out_specs=vmem,
-        scratch_shapes=layers + [sems, pltpu.SemaphoreType.DMA((2,))],
+        scratch_shapes=layers + [sems, pltpu.SemaphoreType.DMA((4,))],
         name="bwd",
     )(near(pulls.reshape(2, LAYERS, 2 * HALF + TAIL, LANES)), own, other, slope)
     grads = lax.all_to_all(grads, ("g", "k"), 0, 0, tiled=True)

time: 162 us -> 162 us (level)
  no operation moved by 1% of the time
where the time goes in v6:
time: 162 us; the launch traced here: 159 us
  blocking collectives  130 us (80%)
  Pallas kernels  14.6 us (9%)
  starting transfers between devices  10.5 us (6%)
  waiting for transfers between devices  3.31 us (2%)
    all_to_all x1, blocking collectives, shards(): layer_parts = lax.all_to_all(message, ('k', 'h', 'g'), 0, 0, tiled=True)  27.5 us
    all_to_all x1, blocking collectives, shards(): lax.all_to_all(xs.reshape(2 * CHIPS, 2 * HALF + TAIL, LANES), ('g', 'y',...  21.7 us
    all_to_all x1, blocking collectives, shards(): lax.all_to_all(pulls.reshape(2 * CHIPS, 2 * HALF + TAIL, LANES), ('g', 'y...  20.8 us
    all_to_all x1, blocking collectives, shards(): lax.all_to_all(jnp.broadcast_to(own[None], (CHIPS, LAYERS, SLICE, GW)), (...  19.9 us
    all_to_all x1, blocking collectives, shards(): grads = lax.all_to_all(grads, ('g', 'k'), 0, 0, tiled=True)  16.8 us
    all_to_all x1, blocking collectives, shards(): pieces = lax.all_to_all(pieces, ('g', 'h'), 0, 0, tiled=True)  10.2 us
    all_to_all x1, blocking collectives, shards(): lax.all_to_all(deviation, ('g', 'h'), 0, 0, tiled=True)  8.32 us
    ppermute x1, starting transfers between devices, shards(): other = lax.ppermute(own, 'c', [(0, 1), (1, 0)])  6.76 us
  transfers between devices with their start and end apart: 2, of which 2 were waited for; matrix products, arithmetic and copies ran while one was open for 0% of the time, Pallas kernels for 0%

profile of v6, /device:TPU:1, one launch (start us, length us, event | category | flops | bytes accessed | tf_op | source)
XLA Modules:
  0.0 159.4 jit_solution(7884362635797054305)
XLA Ops:
  0.6 0.9 pack.1
  1.6 27.5 %all_to_all.35.par_ref = bf16[16,16,256]{2,1,0:T(8,128)(2,1)S(1)} all-to-all(bf16[16,16,256]{2,1,0:T(8,128)(2,1)S(1)} %bitcast.12), channel_id=1, replica_groups=mesh['k'=4,'h'=2,'g'=2,'x'=4,'y'=4,'c'=2] {'k','h','g'}, dimensions={0} | all-to-all | bytes 262144 | tf_op jit(solution)/shard_map/all_to_all | solution.py:358
  29.1 0.1 broadcast_in_dim.2
  29.2 19.9 %all_to_all.36.own_in = bf16[16,16,8,256]{3,2,1,0:T(8,128)(2,1)S(1)} all-to-all(bf16[16,16,8,256]{3,2,1,0:T(8,128)(2,1)S(1)} %broadcast_in_dim.2), channel_id=1, replica_groups=mesh['k'=4,'h'=2,'g'=2,'x'=4,'y'=4,'c'=2] {'y','x'}, dimensions={0} | all-to-all | bytes 2097152 | tf_op jit(solution)/shard_map/all_to_all | solution.py:361
  49.1 0.0 copy-start.1
  49.1 6.8 %collective-permute-start = (bf16[16,16,8,256]{3,2,1,0:T(8,128)(2,1)S(1)}, bf16[16,16,8,256]{3,2,1,0:T(8,128)(2,1)S(1)}, u32[]{:S(2)}, u32[]{:S(2)}) collective-permute-start(bf16[16,16,8,256]{3,2,1,0:T(8,128)(2,1)S(1)} %all_to_all.36.own_in), channel_id=1, source_target_pairs={{0,1},{1,0},{2,3},{3,2},{4,5},{5,4},{6,7},{7,6},{8,9},{9,8},{10,11... | collective-permute-start | bytes 3145736 | tf_op jit(solution)/shard_map/ppermute | solution.py:362
  55.8 2.3 %collective-permute-done.other_in = bf16[16,16,8,256]{3,2,1,0:T(8,128)(2,1)S(1)} collective-permute-done((bf16[16,16,8,256]{3,2,1,0:T(8,128)(2,1)S(1)}, bf16[16,16,8,256]{3,2,1,0:T(8,128)(2,1)S(1)}, u32[]{:S(2)}, u32[]{:S(2)}) %collective-permute-start) | collective-permute-done | bytes 1048608 | tf_op jit(solution)/shard_map/ppermute | solution.py:362
  58.1 0.0 copy-start
  58.1 0.0 copy-done.1
  58.1 5.0 %fwd.1 = (bf16[2,16,136,128]{3,2,1,0:T(8,128)(2,1)}, bf16[16,128,256]{2,1,0:T(8,128)(2,1)}) custom-call(bf16[128,256]{1,0:T(8,128)(2,1)S(1)} %get-tuple-element.13.x_ref, bf16[16,16,256]{2,1,0:T(8,128)(2,1)S(1)} %all_to_all.35.par_ref, bf16[16,16,8,256]{3,2,1,0:T(8,128)(2,1)} %copy-done.1, bf16[16,16,8,256]{3,2,1,0:T(8,128)(2,1)S(1)} %collective-permute-done.other_in), custom_call_target="tpu_custom_call" | custom-call | tf_op jit(solution)/shard_map/fwd/pallas_call | solution.py:367
  63.1 0.0 copy-done
  63.2 21.7 %all_to_all.37 = bf16[32,136,128]{2,1,0:T(8,128)(2,1)S(1)} all-to-all(bf16[32,136,128]{2,1,0:T(8,128)(2,1)} %bitcast.13), channel_id=1, replica_groups=mesh['k'=4,'h'=2,'g'=2,'x'=4,'y'=4,'c'=2] {'g','y','x'}, dimensions={0} | all-to-all | bytes 2228224 | tf_op jit(solution)/shard_map/all_to_all | solution.py:378
  84.8 1.2 gram.1
  86.1 3.8 %collective-permute-start.1 = (bf16[392,256]{1,0:T(8,128)(2,1)S(1)}, bf16[392,256]{1,0:T(8,128)(2,1)S(1)}, u32[]{:S(2)}, u32[]{:S(2)}) collective-permute-start(bf16[392,256]{1,0:T(8,128)(2,1)S(1)} %get-tuple-element.18), channel_id=1, source_target_pairs={{0,1},{1,0},{2,3},{3,2},{4,5},{5,4},{6,7},{7,6},{8,9},{9,8},{10,11... | collective-permute-start | bytes 602120 | tf_op jit(solution)/shard_map/ppermute | solution.py:394
  89.9 1.0 collective-permute-done.1.got_ref
  90.9 10.2 %all_to_all.38.r_ref = bf16[4,112,256]{2,1,0:T(8,128)(2,1)S(1)} all-to-all(bf16[4,112,256]{2,1,0:T(8,128)(2,1)S(1)} %chip.1), channel_id=1, replica_groups=mesh['k'=4,'h'=2,'g'=2,'x'=4,'y'=4,'c'=2] {'g','h'}, dimensions={0} | all-to-all | bytes 458752 | tf_op jit(solution)/shard_map/all_to_all | solution.py:398
  101.2 0.3 deviation.1
  101.5 8.3 %all_to_all.39 = bf16[4,96,256]{2,1,0:T(8,128)(2,1)S(1)} all-to-all(bf16[4,96,256]{2,1,0:T(8,128)(2,1)S(1)} %deviation.1), channel_id=1, replica_groups=mesh['k'=4,'h'=2,'g'=2,'x'=4,'y'=4,'c'=2] {'g','h'}, dimensions={0} | all-to-all | bytes 393216 | tf_op jit(solution)/shard_map/all_to_all | solution.py:408
  109.8 4.8 %all-gather = bf16[8,96,256]{2,1,0:T(8,128)(2,1)S(1)} all-gather(bf16[4,96,256]{2,1,0:T(8,128)(2,1)S(1)} %all_to_all.39), channel_id=2, replica_groups=mesh['k'=4,'h'=2,'g'=2,'x'=4,'y'=4,'c'=2] {'c'}, dimensions={0}, use_global_device_ids=true | all-gather | bytes 589824 | tf_op jit(solution)/shard_map/all_gather | solution.py:408
  114.7 2.1 %pull.1 = bf16[2,16,136,128]{3,2,1,0:T(8,128)(2,1)S(1)} custom-call(bf16[2,4,96,256]{3,2,1,0:T(8,128)(2,1)S(1)} %bitcast.11, bf16[4,112,256]{2,1,0:T(8,128)(2,1)S(1)} %all_to_all.38.r_ref, bf16[8,256]{1,0:T(8,128)(2,1)S(1)} %get-tuple-element.17.tail_ref, f32[2,4,256]{2,1,0:T(4,128)S(1)} %get-tuple-element.19.par_ref, ...), custom_call_target="tpu_custom_call" | custom-call | tf_op jit(solution)/shard_map/pull/pallas_call | solution.py:409
  116.8 20.8 %all_to_all.40 = bf16[32,136,128]{2,1,0:T(8,128)(2,1)S(1)} all-to-all(bf16[32,136,128]{2,1,0:T(8,128)(2,1)S(1)} %bitcast.10), channel_id=1, replica_groups=mesh['k'=4,'h'=2,'g'=2,'x'=4,'y'=4,'c'=2] {'g','y','x'}, dimensions={0} | all-to-all | bytes 2228224 | tf_op jit(solution)/shard_map/all_to_all | solution.py:417
  137.6 4.3 %bwd.1 = bf16[8,24,256]{2,1,0:T(8,128)(2,1)S(1)} custom-call(bf16[2,16,136,128]{3,2,1,0:T(8,128)(2,1)S(1)} %bitcast.9, bf16[16,16,8,256]{3,2,1,0:T(8,128)(2,1)} %copy-done.1, bf16[16,16,8,256]{3,2,1,0:T(8,128)(2,1)} %copy-done, bf16[16,128,256]{2,1,0:T(8,128)(2,1)} %get-tuple-element.21.slope_in), custom_call_target="tpu_custom_call" | custom-call | tf_op jit(solution)/shard_map/bwd/pallas_call | solution.py:419
  141.9 16.8 %all_to_all.41.r_ref = bf16[8,24,256]{2,1,0:T(8,128)(2,1)S(1)} all-to-all(bf16[8,24,256]{2,1,0:T(8,128)(2,1)S(1)} %bwd.1), channel_id=1, replica_groups=mesh['k'=4,'h'=2,'g'=2,'x'=4,'y'=4,'c'=2] {'g','k'}, dimensions={0} | all-to-all | bytes 196608 | tf_op jit(solution)/shard_map/all_to_all | solution.py:427
  158.7 0.6 outputs.1
  (2 shorter events, 0.0 us)
Async XLA Ops:
  49.1 9.0 %copy-start.1 = (bf16[16,16,8,256]{3,2,1,0:T(8,128)(2,1)}, bf16[16,16,8,256]{3,2,1,0:T(8,128)(2,1)S(1)}, u32[]{:S(2)}) copy-start(bf16[16,16,8,256]{3,2,1,0:T(8,128)(2,1)S(1)} %all_to_all.36.own_in) | copy-start | bytes 3145732
  49.1 9.0 %collective-permute-start = (bf16[16,16,8,256]{3,2,1,0:T(8,128)(2,1)S(1)}, bf16[16,16,8,256]{3,2,1,0:T(8,128)(2,1)S(1)}, u32[]{:S(2)}, u32[]{:S(2)}) collective-permute-start(bf16[16,16,8,256]{3,2,1,0:T(8,128)(2,1)S(1)} %all_to_all.36.own_in), channel_id=1, source_target_pairs={{0,1},{1,0},{2,3},{3,2},{4,5},{5,4},{6,7},{7,6},{8,9},{9,8},{10,11... | collective-permute-start | bytes 3145736 | tf_op jit(solution)/shard_map/ppermute | solution.py:362
  58.1 5.0 %copy-start = (bf16[16,16,8,256]{3,2,1,0:T(8,128)(2,1)}, bf16[16,16,8,256]{3,2,1,0:T(8,128)(2,1)S(1)}, u32[]{:S(2)}) copy-start(bf16[16,16,8,256]{3,2,1,0:T(8,128)(2,1)S(1)} %collective-permute-done.other_in) | copy-start | bytes 3145732
  86.1 4.8 %collective-permute-start.1 = (bf16[392,256]{1,0:T(8,128)(2,1)S(1)}, bf16[392,256]{1,0:T(8,128)(2,1)S(1)}, u32[]{:S(2)}, u32[]{:S(2)}) collective-permute-start(bf16[392,256]{1,0:T(8,128)(2,1)S(1)} %get-tuple-element.18), channel_id=1, source_target_pairs={{0,1},{1,0},{2,3},{3,2},{4,5},{5,4},{6,7},{7,6},{8,9},{9,8},{10,11... | collective-permute-start | bytes 602120 | tf_op jit(solution)/shard_map/ppermute | solution.py:394

commit v7 on v5

--- a/solution.py
+++ b/solution.py
@@ -87,33 +87,15 @@
 
 
 def forward_kernel(
-    x_ref, par_ref, own_in, other_in, xs_out, slope_out, w_ref, slope_ref, rows_ref, z_ref, xs_ref, sems, out_sems
+    x_ref, par_ref, own_in, other_in, xs_out, slope_out, w_ref, slope_ref, rows_ref, xs_ref, sems, out_sems
 ):
     core = lax.axis_index("c")
-    chip = lax.axis_index("y") * 4 + lax.axis_index("x")
     arrivals = [weight_reads(own_in, other_in, w_ref, core, sems, layer) for layer in range(LAYERS)]
     for copy in sum(arrivals, []):
         copy.start()
     for layer in range(LAYERS):
-        rows_ref[layer] = par_ref[layer, SLICE:SLICE + PROWS].astype(F32)
-    at_row = lax.broadcasted_iota(jnp.int32, (TAIL, LANES), 0)
-
-    def pack_layer(layer):
-        row = rows_ref[layer, pl.ds(chip // 2, 1), :]
-        row = jnp.broadcast_to(lax.select(chip % 2 == 0, row[:, 0:LANES], row[:, LANES:]), (TAIL, LANES))
-        for half in range(2):
-            rows = z_ref[layer, half * HALF:(half + 1) * HALF]
-            mean = jnp.sum(rows, axis=0, keepdims=True) * (1.0 / HALF)
-            rows = (rows - mean).astype(BF16)
-            xs_ref[half, layer, 0:HALF] = rows[:, 0:LANES]
-            xs_ref[half, layer, HALF:2 * HALF] = rows[:, LANES:]
-            high = mean.astype(BF16).astype(F32)
-            terms = [part[:, at:at + LANES] for part in (high, mean - high) for at in (0, LANES)]
-            tail = row
-            for at, term in enumerate(terms):
-                tail = jnp.where(at_row == at, term, tail)
-            xs_ref[half, layer, 2 * HALF:] = tail.astype(BF16)
-
+        packed = par_ref[layer, SLICE:SLICE + PROWS].astype(F32)
+        rows_ref[layer] = packed[0:4] + packed[4:8]
     writes = []
 
     def write(first, last):
@@ -130,37 +112,33 @@
             for copy in sum(arrivals[0:FIRST] if layer == 0 else arrivals[FIRST:], []):
                 copy.wait()
         z = jnp.dot(x, w_ref[layer].reshape(GW, GW), preferred_element_type=F32)
-        z_ref[layer] = z
-        if layer > 0:
-            pack_layer(layer - 1)
-        scale = rows_ref[layer, 0:1] + rows_ref[layer, 4:5]
-        shift = rows_ref[layer, 1:2] + rows_ref[layer, 5:6]
+        scale, shift = rows_ref[layer, 0:1], rows_ref[layer, 1:2]
         active = z * scale + shift
         gate = 1.0 / (1.0 + jnp.exp2(z * (scale * -LOG2E) + shift * -LOG2E))
         after = active * gate
         x = after.astype(BF16)
         slope_ref[layer] = (gate * ((active - after) + 1.0) * scale).astype(BF16)
+        away = (z - rows_ref[layer, 2:3]).astype(BF16)
+        for half in range(2):
+            xs_ref[half, layer] = away[half * HALF:(half + 1) * HALF]
         if layer == LAYERS // 2:
             write(0, LAYERS // 2)
-    pack_layer(LAYERS - 1)
     write(LAYERS // 2, LAYERS)
     for copy in writes:
         copy.wait()
 
 
-def gram_kernel(x_ref, keep_ref, send_ref, tail_ref, par_ref, zc_out, zc_ref, sems):
-    core = lax.axis_index("c")
+def gram_kernel(x_ref, mine_ref, theirs_ref, keep_ref, send_ref, tail_ref, par_ref, zc_out, zc_ref, sems):
+    core, side = lax.axis_index("c"), lax.axis_index("g")
     means, writes = [], []
     for g in range(2):
-        tails = x_ref[g, :, 2 * HALF:].astype(F32)
-        mean = sum(jnp.concatenate([tails[:, at:at + 1], tails[:, at + 1:at + 2]], axis=2) for at in (0, 2))
-        means.append(jnp.mean(mean, axis=0))
-        rows = jnp.concatenate([x_ref[g, :, 0:HALF], x_ref[g, :, HALF:2 * HALF]], axis=2).astype(F32)
-        zc_ref[g] = (rows + (mean - means[g][None])).astype(BF16).reshape(HOME, GW)
+        rows = x_ref[g].reshape(HOME, GW).astype(F32)
+        means.append(jnp.sum(rows, axis=0, keepdims=True) * (1.0 / HOME))
+        zc_ref[g] = (rows - means[g]).astype(BF16)
         writes.append(pltpu.make_async_copy(zc_ref.at[g], zc_out.at[g], sems.at[g]))
         writes[g].start()
-        packed = [jnp.concatenate([tails[2 * r, 6:7], tails[2 * r + 1, 6:7]], axis=1) for r in range(PROWS)]
-        par_ref[g] = jnp.concatenate([packed[r] + packed[r + 4] for r in range(4)], axis=0)
+        packed = lax.select(side == g, mine_ref[...], theirs_ref[...]).astype(F32)
+        par_ref[g] = packed[0:4] + packed[4:8]
     parts = [split3(mean) for mean in means]
     tail = [parts[g][term] for term in range(3) for g in range(2)]
     tail = jnp.concatenate(tail + [jnp.zeros((2, GW), F32)], axis=0).astype(BF16)
@@ -225,7 +203,7 @@
 CHUNKS = 1
 
 
-def pull_kernel(e_ref, r_ref, tail_ref, par_ref, zc_in, out_ref, zc_ref, sems):
+def pull_kernel(e_ref, r_ref, tail_ref, zc_in, out_ref, zc_ref, sems):
     reads = []
     for n in range(CHUNKS):
         rows = pl.ds(n * (HOME // CHUNKS), HOME // CHUNKS)
@@ -243,9 +221,8 @@
     away, offset = [], []
     for g in range(2):
         mean = jnp.mean(means[g], axis=0, keepdims=True)
-        gap = mean - par_ref[g, 2:3]
-        loss = loss + jnp.sum(gap * gap, keepdims=True)
-        away.append(2.0 * gap)
+        loss = loss + jnp.sum(mean * mean, keepdims=True)
+        away.append(2.0 * mean)
         own = mine[g:g + 1] + mine[2 + g:3 + g] + mine[4 + g:5 + g]
         offset.append(jnp.concatenate(list(split3(own - mean)) + [jnp.zeros((13, GW), F32)], axis=0).astype(BF16))
     tail = [jnp.broadcast_to(part, (1, LANES)) for part in split3(loss)]
@@ -360,19 +337,22 @@
 
     layers = [pltpu.VMEM((LAYERS, 2, CHIPS, SLICE, GW), BF16), pltpu.VMEM((LAYERS, ROWS, GW), BF16)]
     sems = pltpu.SemaphoreType.DMA((2, LAYERS))
-    pieces_shape = (2, LAYERS, 2 * HALF + TAIL, LANES)
+    pieces_shape = (2, LAYERS, HALF, GW)
     xs, slope = pl.pallas_call(
         forward_kernel,
         out_shape=[jax.ShapeDtypeStruct(pieces_shape, BF16), jax.ShapeDtypeStruct((LAYERS, ROWS, GW), BF16)],
         in_specs=[vmem, vmem, hbm, vmem],
         out_specs=[hbm, hbm],
         scratch_shapes=layers
-        + [pltpu.VMEM((LAYERS, PROWS, GW), F32), pltpu.VMEM((LAYERS, ROWS, GW), F32), pltpu.VMEM(pieces_shape, BF16)]
+        + [pltpu.VMEM((LAYERS, 4, GW), F32), pltpu.VMEM(pieces_shape, BF16)]
         + [sems, pltpu.SemaphoreType.DMA((4,))],
         name="fwd",
     )(near(rows), near(layer_parts), own, near(other))
 
-    home = lax.all_to_all(xs.reshape(2 * CHIPS, 2 * HALF + TAIL, LANES), ("g", "y", "x"), 0, 0, tiled=True)
+    home = lax.all_to_all(xs.reshape(2 * CHIPS, HALF, GW), ("g", "x", "y"), 0, 0, tiled=True)
+    mine = lax.dynamic_index_in_dim(layer_parts, lax.axis_index(("x", "y")), 0, keepdims=False)[SLICE:]
+    mine = lax.optimization_barrier((mine, xs))[0]
+    theirs = lax.ppermute(mine, "g", [(0, 1), (1, 0)])
     held = pltpu.VMEM((2, HOME, GW), BF16)
     keep, send, tail, params, centered = pl.pallas_call(
         gram_kernel,
@@ -383,11 +363,11 @@
             pltpu.VMEM((2, 4, GW), F32),
             jax.ShapeDtypeStruct((2, HOME, GW), BF16),
         ],
-        in_specs=[vmem],
+        in_specs=[vmem] * 3,
         out_specs=[vmem] * 4 + [hbm],
         scratch_shapes=[held, pltpu.SemaphoreType.DMA((2,))],
         name="gram",
-    )(near(home.reshape(2, CHIPS, 2 * HALF + TAIL, LANES)))
+    )(near(home.reshape(2, CHIPS, HALF, GW)), near(mine), near(theirs))
     got = lax.ppermute(send, "c", [(0, 1), (1, 0)])
     (pieces,) = kernel_call(
         chip_kernel, [((4, 3 * PIECE + 2 * TAIL, GW), BF16)], "chip", keep, tail, got, scalars=[part]
@@ -406,12 +386,12 @@
     pulls = pl.pallas_call(
         pull_kernel,
         out_shape=pltpu.VMEM((2, CHIPS, 2 * HALF + TAIL, LANES), BF16),
-        in_specs=[vmem] * 4 + [hbm],
+        in_specs=[vmem] * 3 + [hbm],
         out_specs=vmem,
         scratch_shapes=[held, pltpu.SemaphoreType.DMA((CHUNKS,))],
         name="pull",
-    )(near(deviation), near(pieces), near(tail), near(params), centered)
-    pulls = lax.all_to_all(pulls.reshape(2 * CHIPS, 2 * HALF + TAIL, LANES), ("g", "y", "x"), 0, 0, tiled=True)
+    )(near(deviation), near(pieces), near(tail), centered)
+    pulls = lax.all_to_all(pulls.reshape(2 * CHIPS, 2 * HALF + TAIL, LANES), ("g", "x", "y"), 0, 0, tiled=True)
 
     grads = pl.pallas_call(
         backward_kernel,

time: 162 us -> 161 us (level)
  blocking collectives: 130 us -> 110 us
  waiting for transfers between devices: 3.31 us -> 15.3 us
  starting transfers between devices: 10.5 us -> 17.9 us
    all_to_all x2 -> x1, blocking collectives: 42.5 us -> 20.8 us  [shards(): lax.all_to_all(pulls.reshape(2 * CHIPS, 2 * HALF + TAIL, LANES), ('g', 'x...]
    ppermute x0 -> x1, waiting for transfers between devices: none -> 9.6 us  [shards(): theirs = lax.ppermute(mine, 'g', [(0, 1), (1, 0)])]
    all_to_all x0 -> x1, starting transfers between devices: none -> 4.07 us  [shards(): lax.all_to_all(xs.reshape(2 * CHIPS, HALF, GW), ('g', 'x', 'y'), 0, 0, ti...]
    ppermute x0 -> x1, starting transfers between devices: none -> 3.15 us  [shards(): theirs = lax.ppermute(mine, 'g', [(0, 1), (1, 0)])]
    all_to_all x0 -> x1, waiting for transfers between devices: none -> 2.43 us  [shards(): lax.all_to_all(xs.reshape(2 * CHIPS, HALF, GW), ('g', 'x', 'y'), 0, 0, ti...]
  transfers between devices with their start and end apart: 2 -> 4, of which waited for: 2 -> 4; matrix products, arithmetic and copies ran while one was open for 0% -> 0% of each run, Pallas kernels for 0% -> 0%
where the time goes in v7:
time: 161 us; the launch traced here: 158 us
  blocking collectives  110 us (68%)
  starting transfers between devices  17.9 us (11%)
  waiting for transfers between devices  15.3 us (10%)
  Pallas kernels  14.6 us (9%)
    all_to_all x1, blocking collectives, shards(): layer_parts = lax.all_to_all(message, ('k', 'h', 'g'), 0, 0, tiled=True)  27.5 us
    all_to_all x1, blocking collectives, shards(): lax.all_to_all(pulls.reshape(2 * CHIPS, 2 * HALF + TAIL, LANES), ('g', 'x...  20.8 us
    all_to_all x1, blocking collectives, shards(): lax.all_to_all(jnp.broadcast_to(own[None], (CHIPS, LAYERS, SLICE, GW)), (...  19.9 us
    all_to_all x1, blocking collectives, shards(): grads = lax.all_to_all(grads, ('g', 'k'), 0, 0, tiled=True)  16.9 us
    all_to_all x1, blocking collectives, shards(): pieces = lax.all_to_all(pieces, ('g', 'h'), 0, 0, tiled=True)  11.5 us
    ppermute x1, waiting for transfers between devices, shards(): theirs = lax.ppermute(mine, 'g', [(0, 1), (1, 0)])  9.6 us
    all_to_all x1, blocking collectives, shards(): lax.all_to_all(deviation, ('g', 'h'), 0, 0, tiled=True)  8.32 us
    ppermute x1, starting transfers between devices, shards(): other = lax.ppermute(own, 'c', [(0, 1), (1, 0)])  6.76 us
  transfers between devices with their start and end apart: 4, of which 4 were waited for; matrix products, arithmetic and copies ran while one was open for 0% of the time, Pallas kernels for 0%

profile of v7, /device:TPU:1, one launch (start us, length us, event | category | flops | bytes accessed | tf_op | source)
XLA Modules:
  0.0 158.5 jit_solution(16577883502560420395)
XLA Ops:
  0.6 0.9 pack.1
  1.6 27.5 %all_to_all.35.par_ref = bf16[16,16,256]{2,1,0:T(8,128)(2,1)S(1)} all-to-all(bf16[16,16,256]{2,1,0:T(8,128)(2,1)S(1)} %bitcast.14), channel_id=1, replica_groups=mesh['k'=4,'h'=2,'g'=2,'x'=4,'y'=4,'c'=2] {'k','h','g'}, dimensions={0} | all-to-all | bytes 262144 | tf_op jit(solution)/shard_map/all_to_all | solution.py:332
  29.1 0.1 broadcast_in_dim.2
  29.2 19.9 %all_to_all.36.own_in = bf16[16,16,8,256]{3,2,1,0:T(8,128)(2,1)S(1)} all-to-all(bf16[16,16,8,256]{3,2,1,0:T(8,128)(2,1)S(1)} %broadcast_in_dim.2), channel_id=1, replica_groups=mesh['k'=4,'h'=2,'g'=2,'x'=4,'y'=4,'c'=2] {'y','x'}, dimensions={0} | all-to-all | bytes 2097152 | tf_op jit(solution)/shard_map/all_to_all | solution.py:335
  49.1 0.0 copy-start.1
  49.1 6.8 %collective-permute-start = (bf16[16,16,8,256]{3,2,1,0:T(8,128)(2,1)S(1)}, bf16[16,16,8,256]{3,2,1,0:T(8,128)(2,1)S(1)}, u32[]{:S(2)}, u32[]{:S(2)}) collective-permute-start(bf16[16,16,8,256]{3,2,1,0:T(8,128)(2,1)S(1)} %all_to_all.36.own_in), channel_id=1, source_target_pairs={{0,1},{1,0},{2,3},{3,2},{4,5},{5,4},{6,7},{7,6},{8,9},{9,8},{10,11... | collective-permute-start | bytes 3145736 | tf_op jit(solution)/shard_map/ppermute | solution.py:336
  55.8 2.3 %collective-permute-done.other_in = bf16[16,16,8,256]{3,2,1,0:T(8,128)(2,1)S(1)} collective-permute-done((bf16[16,16,8,256]{3,2,1,0:T(8,128)(2,1)S(1)}, bf16[16,16,8,256]{3,2,1,0:T(8,128)(2,1)S(1)}, u32[]{:S(2)}, u32[]{:S(2)}) %collective-permute-start) | collective-permute-done | bytes 1048608 | tf_op jit(solution)/shard_map/ppermute | solution.py:336
  58.1 0.0 copy-start
  58.1 0.0 copy-done.1
  58.1 5.0 %fwd.1 = (bf16[2,16,64,256]{3,2,1,0:T(8,128)(2,1)}, bf16[16,128,256]{2,1,0:T(8,128)(2,1)}) custom-call(bf16[128,256]{1,0:T(8,128)(2,1)S(1)} %get-tuple-element.14.x_ref, bf16[16,16,256]{2,1,0:T(8,128)(2,1)S(1)} %all_to_all.35.par_ref, bf16[16,16,8,256]{3,2,1,0:T(8,128)(2,1)} %copy-done.1, bf16[16,16,8,256]{3,2,1,0:T(8,128)(2,1)S(1)} %collective-permute-done.other_in), custom_call_target="tpu_custom_call" | custom-call | tf_op jit(solution)/shard_map/fwd/pallas_call | solution.py:341
  63.1 0.0 copy-done
  63.1 4.1 %all-to-all-start.2 = ((bf16[32,64,256]{2,1,0:T(8,128)(2,1)}), bf16[32,64,256]{2,1,0:T(8,128)(2,1)S(1)}, u32[]{:S(2)}, u32[]{:S(2)}) async-start(bf16[32,64,256]{2,1,0:T(8,128)(2,1)} %bitcast.15), calls=%async_computation.2 | async-start | bytes 2097152 | tf_op jit(solution)/shard_map/all_to_all | solution.py:352
  67.2 3.1 %collective-permute-start.1 = (bf16[8,256]{1,0:T(8,128)(2,1)S(1)}, bf16[8,256]{1,0:T(8,128)(2,1)S(1)}, u32[]{:S(2)}, u32[]{:S(2)}) collective-permute-start(bf16[8,256]{1,0:T(8,128)(2,1)S(1)} %dynamic-slice_bitcast_fusion.mine_ref), channel_id=1, source_target_pairs={{0,32},{32,0},{1,33},{33,1},{2,34},{34,2},{3,35},{35,3},{4,36},{36... | collective-permute-start | bytes 12296 | tf_op jit(solution)/shard_map/ppermute | solution.py:355
  70.4 9.6 %collective-permute-done.1.theirs_ref = bf16[8,256]{1,0:T(8,128)(2,1)S(1)} collective-permute-done((bf16[8,256]{1,0:T(8,128)(2,1)S(1)}, bf16[8,256]{1,0:T(8,128)(2,1)S(1)}, u32[]{:S(2)}, u32[]{:S(2)}) %collective-permute-start.1) | collective-permute-done | bytes 4128 | tf_op jit(solution)/shard_map/ppermute | solution.py:355
  80.0 2.4 %all-to-all-done.2 = bf16[32,64,256]{2,1,0:T(8,128)(2,1)S(1)} async-done(((bf16[32,64,256]{2,1,0:T(8,128)(2,1)}), bf16[32,64,256]{2,1,0:T(8,128)(2,1)S(1)}, u32[]{:S(2)}, u32[]{:S(2)}) %all-to-all-start.2) | async-done | bytes 1048608 | tf_op jit(solution)/shard_map/all_to_all | solution.py:352
  82.4 1.4 gram.1
  83.8 3.9 %collective-permute-start.2 = (bf16[392,256]{1,0:T(8,128)(2,1)S(1)}, bf16[392,256]{1,0:T(8,128)(2,1)S(1)}, u32[]{:S(2)}, u32[]{:S(2)}) collective-permute-start(bf16[392,256]{1,0:T(8,128)(2,1)S(1)} %get-tuple-element.20), channel_id=1, source_target_pairs={{0,1},{1,0},{2,3},{3,2},{4,5},{5,4},{6,7},{7,6},{8,9},{9,8},{10,11... | collective-permute-start | bytes 602120 | tf_op jit(solution)/shard_map/ppermute | solution.py:371
  87.8 1.0 collective-permute-done.2.got_ref
  88.9 11.5 %all_to_all.37.r_ref = bf16[4,112,256]{2,1,0:T(8,128)(2,1)S(1)} all-to-all(bf16[4,112,256]{2,1,0:T(8,128)(2,1)S(1)} %chip.1), channel_id=1, replica_groups=mesh['k'=4,'h'=2,'g'=2,'x'=4,'y'=4,'c'=2] {'g','h'}, dimensions={0} | all-to-all | bytes 458752 | tf_op jit(solution)/shard_map/all_to_all | solution.py:375
  100.4 0.3 deviation.1
  100.8 8.3 %all_to_all.38 = bf16[4,96,256]{2,1,0:T(8,128)(2,1)S(1)} all-to-all(bf16[4,96,256]{2,1,0:T(8,128)(2,1)S(1)} %deviation.1), channel_id=1, replica_groups=mesh['k'=4,'h'=2,'g'=2,'x'=4,'y'=4,'c'=2] {'g','h'}, dimensions={0} | all-to-all | bytes 393216 | tf_op jit(solution)/shard_map/all_to_all | solution.py:385
  109.1 4.8 %all-gather = bf16[8,96,256]{2,1,0:T(8,128)(2,1)S(1)} all-gather(bf16[4,96,256]{2,1,0:T(8,128)(2,1)S(1)} %all_to_all.38), channel_id=2, replica_groups=mesh['k'=4,'h'=2,'g'=2,'x'=4,'y'=4,'c'=2] {'c'}, dimensions={0}, use_global_device_ids=true | all-gather | bytes 589824 | tf_op jit(solution)/shard_map/all_gather | solution.py:385
  113.9 2.1 %pull.1 = bf16[2,16,136,128]{3,2,1,0:T(8,128)(2,1)S(1)} custom-call(bf16[2,4,96,256]{3,2,1,0:T(8,128)(2,1)S(1)} %bitcast.13, bf16[4,112,256]{2,1,0:T(8,128)(2,1)S(1)} %all_to_all.37.r_ref, bf16[8,256]{1,0:T(8,128)(2,1)S(1)} %get-tuple-element.19.tail_ref, bf16[2,1024,256]{2,1,0:T(8,128)(2,1)} %get-tuple-element.22.zc_in), custom_call_target="tpu_custom_call" | custom-call | tf_op jit(solution)/shard_map/pull/pallas_call | solution.py:386
  116.0 20.8 %all_to_all.39 = bf16[32,136,128]{2,1,0:T(8,128)(2,1)S(1)} all-to-all(bf16[32,136,128]{2,1,0:T(8,128)(2,1)S(1)} %bitcast.11), channel_id=1, replica_groups=mesh['k'=4,'h'=2,'g'=2,'x'=4,'y'=4,'c'=2] {'g','x','y'}, dimensions={0} | all-to-all | bytes 2228224 | tf_op jit(solution)/shard_map/all_to_all | solution.py:394
  136.8 4.1 %bwd.1 = bf16[8,24,256]{2,1,0:T(8,128)(2,1)S(1)} custom-call(bf16[2,16,136,128]{3,2,1,0:T(8,128)(2,1)S(1)} %bitcast.10, bf16[16,16,8,256]{3,2,1,0:T(8,128)(2,1)} %copy-done.1, bf16[16,16,8,256]{3,2,1,0:T(8,128)(2,1)} %copy-done, bf16[16,128,256]{2,1,0:T(8,128)(2,1)} %get-tuple-element.23.slope_in), custom_call_target="tpu_custom_call" | custom-call | tf_op jit(solution)/shard_map/bwd/pallas_call | solution.py:396
  140.9 16.9 %all_to_all.40.r_ref = bf16[8,24,256]{2,1,0:T(8,128)(2,1)S(1)} all-to-all(bf16[8,24,256]{2,1,0:T(8,128)(2,1)S(1)} %bwd.1), channel_id=1, replica_groups=mesh['k'=4,'h'=2,'g'=2,'x'=4,'y'=4,'c'=2] {'g','k'}, dimensions={0} | all-to-all | bytes 196608 | tf_op jit(solution)/shard_map/all_to_all | solution.py:404
  157.8 0.6 outputs.1
  (3 shorter events, 0.1 us)
Async XLA Ops:
  49.1 9.0 %copy-start.1 = (bf16[16,16,8,256]{3,2,1,0:T(8,128)(2,1)}, bf16[16,16,8,256]{3,2,1,0:T(8,128)(2,1)S(1)}, u32[]{:S(2)}) copy-start(bf16[16,16,8,256]{3,2,1,0:T(8,128)(2,1)S(1)} %all_to_all.36.own_in) | copy-start | bytes 3145732
  49.1 9.0 %collective-permute-start = (bf16[16,16,8,256]{3,2,1,0:T(8,128)(2,1)S(1)}, bf16[16,16,8,256]{3,2,1,0:T(8,128)(2,1)S(1)}, u32[]{:S(2)}, u32[]{:S(2)}) collective-permute-start(bf16[16,16,8,256]{3,2,1,0:T(8,128)(2,1)S(1)} %all_to_all.36.own_in), channel_id=1, source_target_pairs={{0,1},{1,0},{2,3},{3,2},{4,5},{5,4},{6,7},{7,6},{8,9},{9,8},{10,11... | collective-permute-start | bytes 3145736 | tf_op jit(solution)/shard_map/ppermute | solution.py:336
  58.1 5.0 %copy-start = (bf16[16,16,8,256]{3,2,1,0:T(8,128)(2,1)}, bf16[16,16,8,256]{3,2,1,0:T(8,128)(2,1)S(1)}, u32[]{:S(2)}) copy-start(bf16[16,16,8,256]{3,2,1,0:T(8,128)(2,1)S(1)} %collective-permute-done.other_in) | copy-start | bytes 3145732
  63.1 19.3 %all-to-all-start.2 = ((bf16[32,64,256]{2,1,0:T(8,128)(2,1)}), bf16[32,64,256]{2,1,0:T(8,128)(2,1)S(1)}, u32[]{:S(2)}, u32[]{:S(2)}) async-start(bf16[32,64,256]{2,1,0:T(8,128)(2,1)} %bitcast.15), calls=%async_computation.2 | async-start | bytes 2097152 | tf_op jit(solution)/shard_map/all_to_all | solution.py:352
  67.2 12.8 %collective-permute-start.1 = (bf16[8,256]{1,0:T(8,128)(2,1)S(1)}, bf16[8,256]{1,0:T(8,128)(2,1)S(1)}, u32[]{:S(2)}, u32[]{:S(2)}) collective-permute-start(bf16[8,256]{1,0:T(8,128)(2,1)S(1)} %dynamic-slice_bitcast_fusion.mine_ref), channel_id=1, source_target_pairs={{0,32},{32,0},{1,33},{33,1},{2,34},{34,2},{3,35},{35,3},{4,36},{36... | collective-permute-start | bytes 12296 | tf_op jit(solution)/shard_map/ppermute | solution.py:355
  83.8 5.0 %collective-permute-start.2 = (bf16[392,256]{1,0:T(8,128)(2,1)S(1)}, bf16[392,256]{1,0:T(8,128)(2,1)S(1)}, u32[]{:S(2)}, u32[]{:S(2)}) collective-permute-start(bf16[392,256]{1,0:T(8,128)(2,1)S(1)} %get-tuple-element.20), channel_id=1, source_target_pairs={{0,1},{1,0},{2,3},{3,2},{4,5},{5,4},{6,7},{7,6},{8,9},{9,8},{10,11... | collective-permute-start | bytes 602120 | tf_op jit(solution)/shard_map/ppermute | solution.py:371

commit v8 on v7

--- a/solution.py
+++ b/solution.py
@@ -67,7 +67,9 @@
             at = 2 * min(k, BLOCKS - 1) + g
             for h in range(2):
                 out_ref[k, h, g, 0:SLICE] = slab_ref[at]
-                out_ref[k, h, g, SLICE:] = packed[:, at * GW:(at + 1) * GW]
+                out_ref[k, h, g, SLICE:SLICE + PROWS] = packed[:, at * GW:(at + 1) * GW]
+                beside = at + 1 - 2 * g
+                out_ref[k, h, g, SLICE + PROWS:] = packed[:, beside * GW:(beside + 1) * GW]
     for copy in copies:
         copy.wait()
 
@@ -87,7 +89,7 @@
 
 
 def forward_kernel(
-    x_ref, par_ref, own_in, other_in, xs_out, slope_out, w_ref, slope_ref, rows_ref, xs_ref, sems, out_sems
+    x_ref, par_ref, own_in, other_in, xs_ref, slope_out, w_ref, slope_ref, rows_ref, sems, out_sems
 ):
     core = lax.axis_index("c")
     arrivals = [weight_reads(own_in, other_in, w_ref, core, sems, layer) for layer in range(LAYERS)]
@@ -100,11 +102,8 @@
 
     def write(first, last):
         span = pl.ds(first, last - first)
-        at = len(writes)
-        writes.append(pltpu.make_async_copy(xs_ref.at[:, span], xs_out.at[:, span], out_sems.at[at]))
-        writes.append(pltpu.make_async_copy(slope_ref.at[span], slope_out.at[span], out_sems.at[at + 1]))
-        for copy in writes[-2:]:
-            copy.start()
+        writes.append(pltpu.make_async_copy(slope_ref.at[span], slope_out.at[span], out_sems.at[len(writes)]))
+        writes[-1].start()
 
     x = x_ref[...]
     for layer in range(LAYERS):
@@ -128,8 +127,10 @@
         copy.wait()
 
 
-def gram_kernel(x_ref, mine_ref, theirs_ref, keep_ref, send_ref, tail_ref, par_ref, zc_out, zc_ref, sems):
+def gram_kernel(x_ref, parts_ref, keep_ref, send_ref, tail_ref, par_ref, zc_out, zc_ref, sems):
     core, side = lax.axis_index("c"), lax.axis_index("g")
+    layer = lax.axis_index("x") * 4 + lax.axis_index("y")
+    own, beside = parts_ref[layer, SLICE:SLICE + PROWS], parts_ref[layer, SLICE + PROWS:]
     means, writes = [], []
     for g in range(2):
         rows = x_ref[g].reshape(HOME, GW).astype(F32)
@@ -137,7 +138,7 @@
         zc_ref[g] = (rows - means[g]).astype(BF16)
         writes.append(pltpu.make_async_copy(zc_ref.at[g], zc_out.at[g], sems.at[g]))
         writes[g].start()
-        packed = lax.select(side == g, mine_ref[...], theirs_ref[...]).astype(F32)
+        packed = lax.select(side == g, own, beside).astype(F32)
         par_ref[g] = packed[0:4] + packed[4:8]
     parts = [split3(mean) for mean in means]
     tail = [parts[g][term] for term in range(3) for g in range(2)]
@@ -320,7 +321,7 @@
     hbm, vmem = pl.BlockSpec(memory_space=pl.ANY), pl.BlockSpec(memory_space=pltpu.VMEM)
     message, rows = pl.pallas_call(
         pack_kernel,
-        out_shape=[pltpu.VMEM((4, 2, 2, SLICE + PROWS, GW), BF16), pltpu.VMEM((ROWS, GW), BF16)],
+        out_shape=[pltpu.VMEM((4, 2, 2, SLICE + 2 * PROWS, GW), BF16), pltpu.VMEM((ROWS, GW), BF16)],
         in_specs=[hbm] * 6,
         out_specs=[vmem, vmem],
         scratch_shapes=[pltpu.VMEM((2 * BLOCKS, SLICE, GW), BF16)]
@@ -328,7 +329,7 @@
         + [pltpu.SemaphoreType.DMA((9,))],
         name="pack",
     )(weights, images, bn_mean, bn_var, bn_gain, bn_bias)
-    message = message.reshape(LAYERS, SLICE + PROWS, GW)
+    message = message.reshape(LAYERS, SLICE + 2 * PROWS, GW)
     layer_parts = lax.all_to_all(message, ("k", "h", "g"), 0, 0, tiled=True)
 
     own = layer_parts[:, 0:SLICE]
@@ -340,19 +341,15 @@
     pieces_shape = (2, LAYERS, HALF, GW)
     xs, slope = pl.pallas_call(
         forward_kernel,
-        out_shape=[jax.ShapeDtypeStruct(pieces_shape, BF16), jax.ShapeDtypeStruct((LAYERS, ROWS, GW), BF16)],
+        out_shape=[pltpu.VMEM(pieces_shape, BF16), jax.ShapeDtypeStruct((LAYERS, ROWS, GW), BF16)],
         in_specs=[vmem, vmem, hbm, vmem],
-        out_specs=[hbm, hbm],
+        out_specs=[vmem, hbm],
         scratch_shapes=layers
-        + [pltpu.VMEM((LAYERS, 4, GW), F32), pltpu.VMEM(pieces_shape, BF16)]
-        + [sems, pltpu.SemaphoreType.DMA((4,))],
+        + [pltpu.VMEM((LAYERS, 4, GW), F32), sems, pltpu.SemaphoreType.DMA((2,))],
         name="fwd",
     )(near(rows), near(layer_parts), own, near(other))
 
     home = lax.all_to_all(xs.reshape(2 * CHIPS, HALF, GW), ("g", "x", "y"), 0, 0, tiled=True)
-    mine = lax.dynamic_index_in_dim(layer_parts, lax.axis_index(("x", "y")), 0, keepdims=False)[SLICE:]
-    mine = lax.optimization_barrier((mine, xs))[0]
-    theirs = lax.ppermute(mine, "g", [(0, 1), (1, 0)])
     held = pltpu.VMEM((2, HOME, GW), BF16)
     keep, send, tail, params, centered = pl.pallas_call(
         gram_kernel,
@@ -363,11 +360,11 @@
             pltpu.VMEM((2, 4, GW), F32),
             jax.ShapeDtypeStruct((2, HOME, GW), BF16),
         ],
-        in_specs=[vmem] * 3,
+        in_specs=[vmem] * 2,
         out_specs=[vmem] * 4 + [hbm],
         scratch_shapes=[held, pltpu.SemaphoreType.DMA((2,))],
         name="gram",
-    )(near(home.reshape(2, CHIPS, HALF, GW)), near(mine), near(theirs))
+    )(near(home.reshape(2, CHIPS, HALF, GW)), near(layer_parts))
     got = lax.ppermute(send, "c", [(0, 1), (1, 0)])
     (pieces,) = kernel_call(
         chip_kernel, [((4, 3 * PIECE + 2 * TAIL, GW), BF16)], "chip", keep, tail, got, scalars=[part]

time: 161 us -> 164 us (1.019)
  blocking collectives: 110 us -> 131 us
  waiting for transfers between devices: 15.3 us -> 3.31 us
  starting transfers between devices: 17.9 us -> 11.7 us
    all_to_all x0 -> x1, blocking collectives: none -> 22.7 us  [shards(): lax.all_to_all(xs.reshape(2 * CHIPS, HALF, GW), ('g', 'x', 'y'), 0, 0, ti...]
    ppermute x1 -> x0, waiting for transfers between devices: 9.6 us -> none  [shards(): theirs = lax.ppermute(mine, 'g', [(0, 1), (1, 0)])]
    all_to_all x1 -> x0, starting transfers between devices: 4.07 us -> none  [shards(): lax.all_to_all(xs.reshape(2 * CHIPS, HALF, GW), ('g', 'x', 'y'), 0, 0, ti...]
    ppermute x1 -> x0, starting transfers between devices: 3.15 us -> none  [shards(): theirs = lax.ppermute(mine, 'g', [(0, 1), (1, 0)])]
    all_to_all x1 -> x0, waiting for transfers between devices: 2.43 us -> none  [shards(): lax.all_to_all(xs.reshape(2 * CHIPS, HALF, GW), ('g', 'x', 'y'), 0, 0, ti...]
  transfers between devices with their start and end apart: 4 -> 2, of which waited for: 4 -> 2; matrix products, arithmetic and copies ran while one was open for 0% -> 0% of each run, Pallas kernels for 0% -> 0%
where the time goes in v8:
time: 164 us; the launch traced here: 161 us
  blocking collectives  131 us (80%)
  Pallas kernels  14.4 us (9%)
  starting transfers between devices  11.7 us (7%)
  waiting for transfers between devices  3.31 us (2%)
    all_to_all x1, blocking collectives, shards(): layer_parts = lax.all_to_all(message, ('k', 'h', 'g'), 0, 0, tiled=True)  28 us
    all_to_all x1, blocking collectives, shards(): lax.all_to_all(xs.reshape(2 * CHIPS, HALF, GW), ('g', 'x', 'y'), 0, 0, ti...  22.7 us
    all_to_all x1, blocking collectives, shards(): lax.all_to_all(pulls.reshape(2 * CHIPS, 2 * HALF + TAIL, LANES), ('g', 'x...  20.8 us
    all_to_all x1, blocking collectives, shards(): lax.all_to_all(jnp.broadcast_to(own[None], (CHIPS, LAYERS, SLICE, GW)), (...  18.9 us
    all_to_all x1, blocking collectives, shards(): grads = lax.all_to_all(grads, ('g', 'k'), 0, 0, tiled=True)  16.6 us
    all_to_all x1, blocking collectives, shards(): pieces = lax.all_to_all(pieces, ('g', 'h'), 0, 0, tiled=True)  10.5 us
    all_to_all x1, blocking collectives, shards(): lax.all_to_all(deviation, ('g', 'h'), 0, 0, tiled=True)  8.31 us
    ppermute x1, starting transfers between devices, shards(): other = lax.ppermute(own, 'c', [(0, 1), (1, 0)])  7.78 us
  transfers between devices with their start and end apart: 2, of which 2 were waited for; matrix products, arithmetic and copies ran while one was open for 0% of the time, Pallas kernels for 0%

profile of v8, /device:TPU:1, one launch (start us, length us, event | category | flops | bytes accessed | tf_op | source)
XLA Modules:
  0.0 160.9 jit_solution(11180653590745938808)
XLA Ops:
  0.6 0.9 pack.1
  1.6 28.0 %all_to_all.35.par_ref.parts_ref = bf16[16,24,256]{2,1,0:T(8,128)(2,1)S(1)} all-to-all(bf16[16,24,256]{2,1,0:T(8,128)(2,1)S(1)} %bitcast.13), channel_id=1, replica_groups=mesh['k'=4,'h'=2,'g'=2,'x'=4,'y'=4,'c'=2] {'k','h','g'}, dimensions={0} | all-to-all | bytes 393216 | tf_op jit(solution)/shard_map/all_to_all | solution.py:333
  29.6 0.0 copy-start.1
  29.6 0.1 broadcast_in_dim.2
  29.7 18.9 %all_to_all.36.own_in = bf16[16,16,8,256]{3,2,1,0:T(8,128)(2,1)S(1)} all-to-all(bf16[16,16,8,256]{3,2,1,0:T(8,128)(2,1)S(1)} %broadcast_in_dim.2), channel_id=1, replica_groups=mesh['k'=4,'h'=2,'g'=2,'x'=4,'y'=4,'c'=2] {'y','x'}, dimensions={0} | all-to-all | bytes 2097152 | tf_op jit(solution)/shard_map/all_to_all | solution.py:336
  48.6 0.0 copy-start.3
  48.6 7.8 %collective-permute-start = (bf16[16,16,8,256]{3,2,1,0:T(8,128)(2,1)S(1)}, bf16[16,16,8,256]{3,2,1,0:T(8,128)(2,1)S(1)}, u32[]{:S(2)}, u32[]{:S(2)}) collective-permute-start(bf16[16,16,8,256]{3,2,1,0:T(8,128)(2,1)S(1)} %all_to_all.36.own_in), channel_id=1, source_target_pairs={{0,1},{1,0},{2,3},{3,2},{4,5},{5,4},{6,7},{7,6},{8,9},{9,8},{10,11... | collective-permute-start | bytes 3145736 | tf_op jit(solution)/shard_map/ppermute | solution.py:337
  56.4 2.3 %collective-permute-done.other_in = bf16[16,16,8,256]{3,2,1,0:T(8,128)(2,1)S(1)} collective-permute-done((bf16[16,16,8,256]{3,2,1,0:T(8,128)(2,1)S(1)}, bf16[16,16,8,256]{3,2,1,0:T(8,128)(2,1)S(1)}, u32[]{:S(2)}, u32[]{:S(2)}) %collective-permute-start) | collective-permute-done | bytes 1048608 | tf_op jit(solution)/shard_map/ppermute | solution.py:337
  58.7 0.0 copy-done.3
  58.7 0.0 copy-start
  58.7 0.0 copy-done.1
  58.7 4.8 %fwd.1 = (bf16[2,16,64,256]{3,2,1,0:T(8,128)(2,1)S(1)}, bf16[16,128,256]{2,1,0:T(8,128)(2,1)}) custom-call(bf16[128,256]{1,0:T(8,128)(2,1)S(1)} %get-tuple-element.13.x_ref, bf16[16,24,256]{2,1,0:T(8,128)(2,1)S(1)} %all_to_all.35.par_ref.parts_ref, bf16[16,16,8,256]{3,2,1,0:T(8,128)(2,1)} %copy-done.3, bf16[16,16,8,256]{3,2,1,0:T(8,128)(2,1)S(1)} %collective-permute-done.other_in), custom_call_target="tpu_custom_call" | custom-call | tf_op jit(solution)/shard_map/fwd/pallas_call | solution.py:342
  63.5 0.0 copy-done
  63.5 0.0 copy-start.2
  63.5 22.7 %all_to_all.37 = bf16[32,64,256]{2,1,0:T(8,128)(2,1)S(1)} all-to-all(bf16[32,64,256]{2,1,0:T(8,128)(2,1)S(1)} %bitcast.12), channel_id=1, replica_groups=mesh['k'=4,'h'=2,'g'=2,'x'=4,'y'=4,'c'=2] {'g','x','y'}, dimensions={0} | all-to-all | bytes 2097152 | tf_op jit(solution)/shard_map/all_to_all | solution.py:352
  86.2 0.0 copy-done.2
  86.2 1.4 gram.1
  87.6 3.9 %collective-permute-start.1 = (bf16[392,256]{1,0:T(8,128)(2,1)S(1)}, bf16[392,256]{1,0:T(8,128)(2,1)S(1)}, u32[]{:S(2)}, u32[]{:S(2)}) collective-permute-start(bf16[392,256]{1,0:T(8,128)(2,1)S(1)} %get-tuple-element.18), channel_id=1, source_target_pairs={{0,1},{1,0},{2,3},{3,2},{4,5},{5,4},{6,7},{7,6},{8,9},{9,8},{10,11... | collective-permute-start | bytes 602120 | tf_op jit(solution)/shard_map/ppermute | solution.py:368
  91.5 1.0 collective-permute-done.1.got_ref
  92.6 0.1 chip.1
  92.6 10.5 %all_to_all.38.r_ref = bf16[4,112,256]{2,1,0:T(8,128)(2,1)S(1)} all-to-all(bf16[4,112,256]{2,1,0:T(8,128)(2,1)S(1)} %chip.1), channel_id=1, replica_groups=mesh['k'=4,'h'=2,'g'=2,'x'=4,'y'=4,'c'=2] {'g','h'}, dimensions={0} | all-to-all | bytes 458752 | tf_op jit(solution)/shard_map/all_to_all | solution.py:372
  103.2 0.3 deviation.1
  103.5 8.3 %all_to_all.39 = bf16[4,96,256]{2,1,0:T(8,128)(2,1)S(1)} all-to-all(bf16[4,96,256]{2,1,0:T(8,128)(2,1)S(1)} %deviation.1), channel_id=1, replica_groups=mesh['k'=4,'h'=2,'g'=2,'x'=4,'y'=4,'c'=2] {'g','h'}, dimensions={0} | all-to-all | bytes 393216 | tf_op jit(solution)/shard_map/all_to_all | solution.py:382
  111.8 4.8 %all-gather = bf16[8,96,256]{2,1,0:T(8,128)(2,1)S(1)} all-gather(bf16[4,96,256]{2,1,0:T(8,128)(2,1)S(1)} %all_to_all.39), channel_id=2, replica_groups=mesh['k'=4,'h'=2,'g'=2,'x'=4,'y'=4,'c'=2] {'c'}, dimensions={0}, use_global_device_ids=true | all-gather | bytes 589824 | tf_op jit(solution)/shard_map/all_gather | solution.py:382
  116.6 2.1 %pull.1 = bf16[2,16,136,128]{3,2,1,0:T(8,128)(2,1)S(1)} custom-call(bf16[2,4,96,256]{3,2,1,0:T(8,128)(2,1)S(1)} %bitcast.11, bf16[4,112,256]{2,1,0:T(8,128)(2,1)S(1)} %all_to_all.38.r_ref, bf16[8,256]{1,0:T(8,128)(2,1)S(1)} %get-tuple-element.17.tail_ref, bf16[2,1024,256]{2,1,0:T(8,128)(2,1)} %get-tuple-element.20.zc_in), custom_call_target="tpu_custom_call" | custom-call | tf_op jit(solution)/shard_map/pull/pallas_call | solution.py:383
  118.7 20.8 %all_to_all.40 = bf16[32,136,128]{2,1,0:T(8,128)(2,1)S(1)} all-to-all(bf16[32,136,128]{2,1,0:T(8,128)(2,1)S(1)} %bitcast.9), channel_id=1, replica_groups=mesh['k'=4,'h'=2,'g'=2,'x'=4,'y'=4,'c'=2] {'g','x','y'}, dimensions={0} | all-to-all | bytes 2228224 | tf_op jit(solution)/shard_map/all_to_all | solution.py:391
  139.6 4.1 %bwd.1 = bf16[8,24,256]{2,1,0:T(8,128)(2,1)S(1)} custom-call(bf16[2,16,136,128]{3,2,1,0:T(8,128)(2,1)S(1)} %bitcast.8, bf16[16,16,8,256]{3,2,1,0:T(8,128)(2,1)} %copy-done.3, bf16[16,16,8,256]{3,2,1,0:T(8,128)(2,1)} %copy-done, bf16[16,128,256]{2,1,0:T(8,128)(2,1)} %get-tuple-element.21.slope_in), custom_call_target="tpu_custom_call" | custom-call | tf_op jit(solution)/shard_map/bwd/pallas_call | solution.py:393
  143.7 16.6 %all_to_all.41.r_ref = bf16[8,24,256]{2,1,0:T(8,128)(2,1)S(1)} all-to-all(bf16[8,24,256]{2,1,0:T(8,128)(2,1)S(1)} %bwd.1), channel_id=1, replica_groups=mesh['k'=4,'h'=2,'g'=2,'x'=4,'y'=4,'c'=2] {'g','k'}, dimensions={0} | all-to-all | bytes 196608 | tf_op jit(solution)/shard_map/all_to_all | solution.py:401
  160.3 0.6 outputs.1
  (1 shorter events, 0.0 us)
Async XLA Ops:
  29.6 29.1 %copy-start.1 = (bf16[16,24,256]{2,1,0:T(8,128)(2,1)}, bf16[16,24,256]{2,1,0:T(8,128)(2,1)S(1)}, u32[]{:S(2)}) copy-start(bf16[16,24,256]{2,1,0:T(8,128)(2,1)S(1)} %all_to_all.35.par_ref.parts_ref) | copy-start | bytes 589828
  48.6 10.1 %copy-start.3 = (bf16[16,16,8,256]{3,2,1,0:T(8,128)(2,1)}, bf16[16,16,8,256]{3,2,1,0:T(8,128)(2,1)S(1)}, u32[]{:S(2)}) copy-start(bf16[16,16,8,256]{3,2,1,0:T(8,128)(2,1)S(1)} %all_to_all.36.own_in) | copy-start | bytes 3145732
  48.6 10.1 %collective-permute-start = (bf16[16,16,8,256]{3,2,1,0:T(8,128)(2,1)S(1)}, bf16[16,16,8,256]{3,2,1,0:T(8,128)(2,1)S(1)}, u32[]{:S(2)}, u32[]{:S(2)}) collective-permute-start(bf16[16,16,8,256]{3,2,1,0:T(8,128)(2,1)S(1)} %all_to_all.36.own_in), channel_id=1, source_target_pairs={{0,1},{1,0},{2,3},{3,2},{4,5},{5,4},{6,7},{7,6},{8,9},{9,8},{10,11... | collective-permute-start | bytes 3145736 | tf_op jit(solution)/shard_map/ppermute | solution.py:337
  58.7 4.8 %copy-start = (bf16[16,16,8,256]{3,2,1,0:T(8,128)(2,1)}, bf16[16,16,8,256]{3,2,1,0:T(8,128)(2,1)S(1)}, u32[]{:S(2)}) copy-start(bf16[16,16,8,256]{3,2,1,0:T(8,128)(2,1)S(1)} %collective-permute-done.other_in) | copy-start | bytes 3145732
  63.5 22.7 %copy-start.2 = (bf16[16,24,256]{2,1,0:T(8,128)(2,1)S(1)}, bf16[16,24,256]{2,1,0:T(8,128)(2,1)}, u32[]{:S(2)}) copy-start(bf16[16,24,256]{2,1,0:T(8,128)(2,1)} %copy-done.1) | copy-start | bytes 589828
  87.6 5.0 %collective-permute-start.1 = (bf16[392,256]{1,0:T(8,128)(2,1)S(1)}, bf16[392,256]{1,0:T(8,128)(2,1)S(1)}, u32[]{:S(2)}, u32[]{:S(2)}) collective-permute-start(bf16[392,256]{1,0:T(8,128)(2,1)S(1)} %get-tuple-element.18), channel_id=1, source_target_pairs={{0,1},{1,0},{2,3},{3,2},{4,5},{5,4},{6,7},{7,6},{8,9},{9,8},{10,11... | collective-permute-start | bytes 602120 | tf_op jit(solution)/shard_map/ppermute | solution.py:368

commit v9 on v7

--- a/solution.py
+++ b/solution.py
@@ -66,8 +66,8 @@
         for g in range(2):
             at = 2 * min(k, BLOCKS - 1) + g
             for h in range(2):
-                out_ref[k, h, g, 0:SLICE] = slab_ref[at]
-                out_ref[k, h, g, SLICE:] = packed[:, at * GW:(at + 1) * GW]
+                out_ref[h, k, g, 0:SLICE] = slab_ref[at]
+                out_ref[h, k, g, SLICE:] = packed[:, at * GW:(at + 1) * GW]
     for copy in copies:
         copy.wait()
 
@@ -79,10 +79,14 @@
 FIRST = 4
 
 
+def slot(layer):
+    return layer // 2 % 2 * 8 + layer // 4 * 2 + layer % 2
+
+
 def weight_reads(own_in, other_in, w_ref, core, sems, layer):
     return [
-        pltpu.make_async_copy(own_in.at[:, layer], w_ref.at[layer, core], sems.at[0, layer]),
-        pltpu.make_async_copy(other_in.at[:, layer], w_ref.at[layer, 1 - core], sems.at[1, layer]),
+        pltpu.make_async_copy(own_in.at[:, slot(layer)], w_ref.at[layer, core], sems.at[0, layer]),
+        pltpu.make_async_copy(other_in.at[:, slot(layer)], w_ref.at[layer, 1 - core], sems.at[1, layer]),
     ]
 
 
@@ -94,7 +98,7 @@
     for copy in sum(arrivals, []):
         copy.start()
     for layer in range(LAYERS):
-        packed = par_ref[layer, SLICE:SLICE + PROWS].astype(F32)
+        packed = par_ref[slot(layer), SLICE:SLICE + PROWS].astype(F32)
         rows_ref[layer] = packed[0:4] + packed[4:8]
     writes = []
 
@@ -320,7 +324,7 @@
     hbm, vmem = pl.BlockSpec(memory_space=pl.ANY), pl.BlockSpec(memory_space=pltpu.VMEM)
     message, rows = pl.pallas_call(
         pack_kernel,
-        out_shape=[pltpu.VMEM((4, 2, 2, SLICE + PROWS, GW), BF16), pltpu.VMEM((ROWS, GW), BF16)],
+        out_shape=[pltpu.VMEM((2, 4, 2, SLICE + PROWS, GW), BF16), pltpu.VMEM((ROWS, GW), BF16)],
         in_specs=[hbm] * 6,
         out_specs=[vmem, vmem],
         scratch_shapes=[pltpu.VMEM((2 * BLOCKS, SLICE, GW), BF16)]
@@ -329,7 +333,7 @@
         name="pack",
     )(weights, images, bn_mean, bn_var, bn_gain, bn_bias)
     message = message.reshape(LAYERS, SLICE + PROWS, GW)
-    layer_parts = lax.all_to_all(message, ("k", "h", "g"), 0, 0, tiled=True)
+    layer_parts = lax.all_to_all(message, ("h", "k", "g"), 0, 0, tiled=True)
 
     own = layer_parts[:, 0:SLICE]
     own = lax.all_to_all(jnp.broadcast_to(own[None], (CHIPS, LAYERS, SLICE, GW)), ("y", "x"), 0, 0, tiled=True)
@@ -350,7 +354,7 @@
     )(near(rows), near(layer_parts), own, near(other))
 
     home = lax.all_to_all(xs.reshape(2 * CHIPS, HALF, GW), ("g", "x", "y"), 0, 0, tiled=True)
-    mine = lax.dynamic_index_in_dim(layer_parts, lax.axis_index(("x", "y")), 0, keepdims=False)[SLICE:]
+    mine = lax.dynamic_index_in_dim(layer_parts, slot(lax.axis_index(("x", "y"))), 0, keepdims=False)[SLICE:]
     mine = lax.optimization_barrier((mine, xs))[0]
     theirs = lax.ppermute(mine, "g", [(0, 1), (1, 0)])
     held = pltpu.VMEM((2, HOME, GW), BF16)

time: 161 us -> 161 us (level)
  blocking collectives: 110 us -> 108 us
    all_to_all x1, starting transfers between devices: 4.07 us -> 5.72 us  [shards(): lax.all_to_all(xs.reshape(2 * CHIPS, HALF, GW), ('g', 'x', 'y'), 0, 0, ti...]
where the time goes in v9:
time: 161 us; the launch traced here: 158 us
  blocking collectives  108 us (67%)
  starting transfers between devices  19.2 us (12%)
  waiting for transfers between devices  15.3 us (10%)
  Pallas kernels  14.6 us (9%)
    all_to_all x1, blocking collectives, shards(): layer_parts = lax.all_to_all(message, ('h', 'k', 'g'), 0, 0, tiled=True)  27.9 us
    all_to_all x1, blocking collectives, shards(): lax.all_to_all(pulls.reshape(2 * CHIPS, 2 * HALF + TAIL, LANES), ('g', 'x...  21 us
    all_to_all x1, blocking collectives, shards(): lax.all_to_all(jnp.broadcast_to(own[None], (CHIPS, LAYERS, SLICE, GW)), (...  20.2 us
    all_to_all x1, blocking collectives, shards(): grads = lax.all_to_all(grads, ('g', 'k'), 0, 0, tiled=True)  15.9 us
    all_to_all x1, blocking collectives, shards(): pieces = lax.all_to_all(pieces, ('g', 'h'), 0, 0, tiled=True)  10.1 us
    ppermute x1, waiting for transfers between devices, shards(): theirs = lax.ppermute(mine, 'g', [(0, 1), (1, 0)])  9.56 us
    all_to_all x1, blocking collectives, shards(): lax.all_to_all(deviation, ('g', 'h'), 0, 0, tiled=True)  8.32 us
    ppermute x1, starting transfers between devices, shards(): other = lax.ppermute(own, 'c', [(0, 1), (1, 0)])  6.41 us
  transfers between devices with their start and end apart: 4, of which 4 were waited for; matrix products, arithmetic and copies ran while one was open for 0% of the time, Pallas kernels for 0%

profile of v9, /device:TPU:1, one launch (start us, length us, event | category | flops | bytes accessed | tf_op | source)
XLA Modules:
  0.0 158.2 jit_solution(11712793046139279722)
XLA Ops:
  0.6 0.9 pack.1
  1.6 27.9 %all_to_all.35.par_ref = bf16[16,16,256]{2,1,0:T(8,128)(2,1)S(1)} all-to-all(bf16[16,16,256]{2,1,0:T(8,128)(2,1)S(1)} %bitcast.14), channel_id=1, replica_groups=mesh['k'=4,'h'=2,'g'=2,'x'=4,'y'=4,'c'=2] {'h','k','g'}, dimensions={0} | all-to-all | bytes 262144 | tf_op jit(solution)/shard_map/all_to_all | solution.py:336
  29.4 0.1 broadcast_in_dim.2
  29.6 20.2 %all_to_all.36.own_in = bf16[16,16,8,256]{3,2,1,0:T(8,128)(2,1)S(1)} all-to-all(bf16[16,16,8,256]{3,2,1,0:T(8,128)(2,1)S(1)} %broadcast_in_dim.2), channel_id=1, replica_groups=mesh['k'=4,'h'=2,'g'=2,'x'=4,'y'=4,'c'=2] {'y','x'}, dimensions={0} | all-to-all | bytes 2097152 | tf_op jit(solution)/shard_map/all_to_all | solution.py:339
  49.7 0.0 copy-start.1
  49.7 6.4 %collective-permute-start = (bf16[16,16,8,256]{3,2,1,0:T(8,128)(2,1)S(1)}, bf16[16,16,8,256]{3,2,1,0:T(8,128)(2,1)S(1)}, u32[]{:S(2)}, u32[]{:S(2)}) collective-permute-start(bf16[16,16,8,256]{3,2,1,0:T(8,128)(2,1)S(1)} %all_to_all.36.own_in), channel_id=1, source_target_pairs={{0,1},{1,0},{2,3},{3,2},{4,5},{5,4},{6,7},{7,6},{8,9},{9,8},{10,11... | collective-permute-start | bytes 3145736 | tf_op jit(solution)/shard_map/ppermute | solution.py:340
  56.2 2.3 %collective-permute-done.other_in = bf16[16,16,8,256]{3,2,1,0:T(8,128)(2,1)S(1)} collective-permute-done((bf16[16,16,8,256]{3,2,1,0:T(8,128)(2,1)S(1)}, bf16[16,16,8,256]{3,2,1,0:T(8,128)(2,1)S(1)}, u32[]{:S(2)}, u32[]{:S(2)}) %collective-permute-start) | collective-permute-done | bytes 1048608 | tf_op jit(solution)/shard_map/ppermute | solution.py:340
  58.4 0.0 copy-start
  58.4 0.0 copy-done.1
  58.4 5.0 %fwd.1 = (bf16[2,16,64,256]{3,2,1,0:T(8,128)(2,1)}, bf16[16,128,256]{2,1,0:T(8,128)(2,1)}) custom-call(bf16[128,256]{1,0:T(8,128)(2,1)S(1)} %get-tuple-element.14.x_ref, bf16[16,16,256]{2,1,0:T(8,128)(2,1)S(1)} %all_to_all.35.par_ref, bf16[16,16,8,256]{3,2,1,0:T(8,128)(2,1)} %copy-done.1, bf16[16,16,8,256]{3,2,1,0:T(8,128)(2,1)S(1)} %collective-permute-done.other_in), custom_call_target="tpu_custom_call" | custom-call | tf_op jit(solution)/shard_map/fwd/pallas_call | solution.py:345
  63.4 0.0 copy-done
  63.4 5.7 %all-to-all-start.2 = ((bf16[32,64,256]{2,1,0:T(8,128)(2,1)}), bf16[32,64,256]{2,1,0:T(8,128)(2,1)S(1)}, u32[]{:S(2)}, u32[]{:S(2)}) async-start(bf16[32,64,256]{2,1,0:T(8,128)(2,1)} %bitcast.15), calls=%async_computation.2 | async-start | bytes 2097152 | tf_op jit(solution)/shard_map/all_to_all | solution.py:356
  69.2 3.1 %collective-permute-start.1 = (bf16[8,256]{1,0:T(8,128)(2,1)S(1)}, bf16[8,256]{1,0:T(8,128)(2,1)S(1)}, u32[]{:S(2)}, u32[]{:S(2)}) collective-permute-start(bf16[8,256]{1,0:T(8,128)(2,1)S(1)} %dynamic-slice_bitcast_fusion.mine_ref), channel_id=1, source_target_pairs={{0,32},{32,0},{1,33},{33,1},{2,34},{34,2},{3,35},{35,3},{4,36},{36... | collective-permute-start | bytes 12296 | tf_op jit(solution)/shard_map/ppermute | solution.py:359
  72.4 9.6 %collective-permute-done.1.theirs_ref = bf16[8,256]{1,0:T(8,128)(2,1)S(1)} collective-permute-done((bf16[8,256]{1,0:T(8,128)(2,1)S(1)}, bf16[8,256]{1,0:T(8,128)(2,1)S(1)}, u32[]{:S(2)}, u32[]{:S(2)}) %collective-permute-start.1) | collective-permute-done | bytes 4128 | tf_op jit(solution)/shard_map/ppermute | solution.py:359
  81.9 2.4 %all-to-all-done.2 = bf16[32,64,256]{2,1,0:T(8,128)(2,1)S(1)} async-done(((bf16[32,64,256]{2,1,0:T(8,128)(2,1)}), bf16[32,64,256]{2,1,0:T(8,128)(2,1)S(1)}, u32[]{:S(2)}, u32[]{:S(2)}) %all-to-all-start.2) | async-done | bytes 1048608 | tf_op jit(solution)/shard_map/all_to_all | solution.py:356
  84.4 1.4 gram.1
  85.8 3.9 %collective-permute-start.2 = (bf16[392,256]{1,0:T(8,128)(2,1)S(1)}, bf16[392,256]{1,0:T(8,128)(2,1)S(1)}, u32[]{:S(2)}, u32[]{:S(2)}) collective-permute-start(bf16[392,256]{1,0:T(8,128)(2,1)S(1)} %get-tuple-element.20), channel_id=1, source_target_pairs={{0,1},{1,0},{2,3},{3,2},{4,5},{5,4},{6,7},{7,6},{8,9},{9,8},{10,11... | collective-permute-start | bytes 602120 | tf_op jit(solution)/shard_map/ppermute | solution.py:375
  89.8 1.0 collective-permute-done.2.got_ref
  90.8 10.1 %all_to_all.37.r_ref = bf16[4,112,256]{2,1,0:T(8,128)(2,1)S(1)} all-to-all(bf16[4,112,256]{2,1,0:T(8,128)(2,1)S(1)} %chip.1), channel_id=1, replica_groups=mesh['k'=4,'h'=2,'g'=2,'x'=4,'y'=4,'c'=2] {'g','h'}, dimensions={0} | all-to-all | bytes 458752 | tf_op jit(solution)/shard_map/all_to_all | solution.py:379
  100.9 0.3 deviation.1
  101.3 8.3 %all_to_all.38 = bf16[4,96,256]{2,1,0:T(8,128)(2,1)S(1)} all-to-all(bf16[4,96,256]{2,1,0:T(8,128)(2,1)S(1)} %deviation.1), channel_id=1, replica_groups=mesh['k'=4,'h'=2,'g'=2,'x'=4,'y'=4,'c'=2] {'g','h'}, dimensions={0} | all-to-all | bytes 393216 | tf_op jit(solution)/shard_map/all_to_all | solution.py:389
  109.6 4.8 %all-gather = bf16[8,96,256]{2,1,0:T(8,128)(2,1)S(1)} all-gather(bf16[4,96,256]{2,1,0:T(8,128)(2,1)S(1)} %all_to_all.38), channel_id=2, replica_groups=mesh['k'=4,'h'=2,'g'=2,'x'=4,'y'=4,'c'=2] {'c'}, dimensions={0}, use_global_device_ids=true | all-gather | bytes 589824 | tf_op jit(solution)/shard_map/all_gather | solution.py:389
  114.4 2.1 %pull.1 = bf16[2,16,136,128]{3,2,1,0:T(8,128)(2,1)S(1)} custom-call(bf16[2,4,96,256]{3,2,1,0:T(8,128)(2,1)S(1)} %bitcast.13, bf16[4,112,256]{2,1,0:T(8,128)(2,1)S(1)} %all_to_all.37.r_ref, bf16[8,256]{1,0:T(8,128)(2,1)S(1)} %get-tuple-element.19.tail_ref, bf16[2,1024,256]{2,1,0:T(8,128)(2,1)} %get-tuple-element.22.zc_in), custom_call_target="tpu_custom_call" | custom-call | tf_op jit(solution)/shard_map/pull/pallas_call | solution.py:390
  116.5 21.0 %all_to_all.39 = bf16[32,136,128]{2,1,0:T(8,128)(2,1)S(1)} all-to-all(bf16[32,136,128]{2,1,0:T(8,128)(2,1)S(1)} %bitcast.11), channel_id=1, replica_groups=mesh['k'=4,'h'=2,'g'=2,'x'=4,'y'=4,'c'=2] {'g','x','y'}, dimensions={0} | all-to-all | bytes 2228224 | tf_op jit(solution)/shard_map/all_to_all | solution.py:398
  137.5 4.1 %bwd.1 = bf16[8,24,256]{2,1,0:T(8,128)(2,1)S(1)} custom-call(bf16[2,16,136,128]{3,2,1,0:T(8,128)(2,1)S(1)} %bitcast.10, bf16[16,16,8,256]{3,2,1,0:T(8,128)(2,1)} %copy-done.1, bf16[16,16,8,256]{3,2,1,0:T(8,128)(2,1)} %copy-done, bf16[16,128,256]{2,1,0:T(8,128)(2,1)} %get-tuple-element.23.slope_in), custom_call_target="tpu_custom_call" | custom-call | tf_op jit(solution)/shard_map/bwd/pallas_call | solution.py:400
  141.7 15.9 %all_to_all.40.r_ref = bf16[8,24,256]{2,1,0:T(8,128)(2,1)S(1)} all-to-all(bf16[8,24,256]{2,1,0:T(8,128)(2,1)S(1)} %bwd.1), channel_id=1, replica_groups=mesh['k'=4,'h'=2,'g'=2,'x'=4,'y'=4,'c'=2] {'g','k'}, dimensions={0} | all-to-all | bytes 196608 | tf_op jit(solution)/shard_map/all_to_all | solution.py:408
  157.6 0.6 outputs.1
  (3 shorter events, 0.1 us)
Async XLA Ops:
  49.7 8.7 %copy-start.1 = (bf16[16,16,8,256]{3,2,1,0:T(8,128)(2,1)}, bf16[16,16,8,256]{3,2,1,0:T(8,128)(2,1)S(1)}, u32[]{:S(2)}) copy-start(bf16[16,16,8,256]{3,2,1,0:T(8,128)(2,1)S(1)} %all_to_all.36.own_in) | copy-start | bytes 3145732
  49.7 8.7 %collective-permute-start = (bf16[16,16,8,256]{3,2,1,0:T(8,128)(2,1)S(1)}, bf16[16,16,8,256]{3,2,1,0:T(8,128)(2,1)S(1)}, u32[]{:S(2)}, u32[]{:S(2)}) collective-permute-start(bf16[16,16,8,256]{3,2,1,0:T(8,128)(2,1)S(1)} %all_to_all.36.own_in), channel_id=1, source_target_pairs={{0,1},{1,0},{2,3},{3,2},{4,5},{5,4},{6,7},{7,6},{8,9},{9,8},{10,11... | collective-permute-start | bytes 3145736 | tf_op jit(solution)/shard_map/ppermute | solution.py:340
  58.4 5.0 %copy-start = (bf16[16,16,8,256]{3,2,1,0:T(8,128)(2,1)}, bf16[16,16,8,256]{3,2,1,0:T(8,128)(2,1)S(1)}, u32[]{:S(2)}) copy-start(bf16[16,16,8,256]{3,2,1,0:T(8,128)(2,1)S(1)} %collective-permute-done.other_in) | copy-start | bytes 3145732
  63.4 20.9 %all-to-all-start.2 = ((bf16[32,64,256]{2,1,0:T(8,128)(2,1)}), bf16[32,64,256]{2,1,0:T(8,128)(2,1)S(1)}, u32[]{:S(2)}, u32[]{:S(2)}) async-start(bf16[32,64,256]{2,1,0:T(8,128)(2,1)} %bitcast.15), calls=%async_computation.2 | async-start | bytes 2097152 | tf_op jit(solution)/shard_map/all_to_all | solution.py:356
  69.2 12.7 %collective-permute-start.1 = (bf16[8,256]{1,0:T(8,128)(2,1)S(1)}, bf16[8,256]{1,0:T(8,128)(2,1)S(1)}, u32[]{:S(2)}, u32[]{:S(2)}) collective-permute-start(bf16[8,256]{1,0:T(8,128)(2,1)S(1)} %dynamic-slice_bitcast_fusion.mine_ref), channel_id=1, source_target_pairs={{0,32},{32,0},{1,33},{33,1},{2,34},{34,2},{3,35},{35,3},{4,36},{36... | collective-permute-start | bytes 12296 | tf_op jit(solution)/shard_map/ppermute | solution.py:359
  85.8 5.0 %collective-permute-start.2 = (bf16[392,256]{1,0:T(8,128)(2,1)S(1)}, bf16[392,256]{1,0:T(8,128)(2,1)S(1)}, u32[]{:S(2)}, u32[]{:S(2)}) collective-permute-start(bf16[392,256]{1,0:T(8,128)(2,1)S(1)} %get-tuple-element.20), channel_id=1, source_target_pairs={{0,1},{1,0},{2,3},{3,2},{4,5},{5,4},{6,7},{7,6},{8,9},{9,8},{10,11... | collective-permute-start | bytes 602120 | tf_op jit(solution)/shard_map/ppermute | solution.py:375

commit v10 on v9

--- a/solution.py
+++ b/solution.py
@@ -42,7 +42,7 @@
     for copy in reads:
         copy.start()
     mean_ref, var_ref, gain_ref, bias_ref = held
-    chip = lax.axis_index("y") * 4 + lax.axis_index("x")
+    chip = lax.axis_index("x") * 4 + lax.axis_index("y")
     row = (lax.axis_index("c") * CHIPS + chip) * SLICE
     half = lax.axis_index("h")
     group = 2 * jnp.minimum(lax.axis_index("k"), BLOCKS - 1) + lax.axis_index("g")
@@ -336,7 +336,7 @@
     layer_parts = lax.all_to_all(message, ("h", "k", "g"), 0, 0, tiled=True)
 
     own = layer_parts[:, 0:SLICE]
-    own = lax.all_to_all(jnp.broadcast_to(own[None], (CHIPS, LAYERS, SLICE, GW)), ("y", "x"), 0, 0, tiled=True)
+    own = lax.all_to_all(jnp.broadcast_to(own[None], (CHIPS, LAYERS, SLICE, GW)), ("x", "y"), 0, 0, tiled=True)
     other = lax.ppermute(own, "c", [(0, 1), (1, 0)])
 
     layers = [pltpu.VMEM((LAYERS, 2, CHIPS, SLICE, GW), BF16), pltpu.VMEM((LAYERS, ROWS, GW), BF16)]

time: 161 us -> 161 us (level)
  no operation moved by 1% of the time
where the time goes in v10:
time: 161 us; the launch traced here: 158 us
  blocking collectives  108 us (67%)
  starting transfers between devices  19.7 us (12%)
  waiting for transfers between devices  15.3 us (10%)
  Pallas kernels  14.6 us (9%)
    all_to_all x1, blocking collectives, shards(): layer_parts = lax.all_to_all(message, ('h', 'k', 'g'), 0, 0, tiled=True)  27.9 us
    all_to_all x1, blocking collectives, shards(): lax.all_to_all(pulls.reshape(2 * CHIPS, 2 * HALF + TAIL, LANES), ('g', 'x...  21.1 us
    all_to_all x1, blocking collectives, shards(): lax.all_to_all(jnp.broadcast_to(own[None], (CHIPS, LAYERS, SLICE, GW)), (...  19.9 us
    all_to_all x1, blocking collectives, shards(): grads = lax.all_to_all(grads, ('g', 'k'), 0, 0, tiled=True)  15.8 us
    all_to_all x1, blocking collectives, shards(): pieces = lax.all_to_all(pieces, ('g', 'h'), 0, 0, tiled=True)  10 us
    ppermute x1, waiting for transfers between devices, shards(): theirs = lax.ppermute(mine, 'g', [(0, 1), (1, 0)])  9.56 us
    all_to_all x1, blocking collectives, shards(): lax.all_to_all(deviation, ('g', 'h'), 0, 0, tiled=True)  8.32 us
    ppermute x1, starting transfers between devices, shards(): other = lax.ppermute(own, 'c', [(0, 1), (1, 0)])  6.57 us
  transfers between devices with their start and end apart: 4, of which 4 were waited for; matrix products, arithmetic and copies ran while one was open for 0% of the time, Pallas kernels for 0%

profile of v10, /device:TPU:1, one launch (start us, length us, event | category | flops | bytes accessed | tf_op | source)
XLA Modules:
  0.0 158.4 jit_solution(6771559353859447703)
XLA Ops:
  0.6 0.9 pack.1
  1.6 27.9 %all_to_all.35.par_ref = bf16[16,16,256]{2,1,0:T(8,128)(2,1)S(1)} all-to-all(bf16[16,16,256]{2,1,0:T(8,128)(2,1)S(1)} %bitcast.14), channel_id=1, replica_groups=mesh['k'=4,'h'=2,'g'=2,'x'=4,'y'=4,'c'=2] {'h','k','g'}, dimensions={0} | all-to-all | bytes 262144 | tf_op jit(solution)/shard_map/all_to_all | solution.py:336
  29.4 0.1 broadcast_in_dim.2
  29.6 19.9 %all_to_all.36.own_in = bf16[16,16,8,256]{3,2,1,0:T(8,128)(2,1)S(1)} all-to-all(bf16[16,16,8,256]{3,2,1,0:T(8,128)(2,1)S(1)} %broadcast_in_dim.2), channel_id=1, replica_groups=mesh['k'=4,'h'=2,'g'=2,'x'=4,'y'=4,'c'=2] {'x','y'}, dimensions={0} | all-to-all | bytes 2097152 | tf_op jit(solution)/shard_map/all_to_all | solution.py:339
  49.5 0.0 copy-start.1
  49.5 6.6 %collective-permute-start = (bf16[16,16,8,256]{3,2,1,0:T(8,128)(2,1)S(1)}, bf16[16,16,8,256]{3,2,1,0:T(8,128)(2,1)S(1)}, u32[]{:S(2)}, u32[]{:S(2)}) collective-permute-start(bf16[16,16,8,256]{3,2,1,0:T(8,128)(2,1)S(1)} %all_to_all.36.own_in), channel_id=1, source_target_pairs={{0,1},{1,0},{2,3},{3,2},{4,5},{5,4},{6,7},{7,6},{8,9},{9,8},{10,11... | collective-permute-start | bytes 3145736 | tf_op jit(solution)/shard_map/ppermute | solution.py:340
  56.1 2.3 %collective-permute-done.other_in = bf16[16,16,8,256]{3,2,1,0:T(8,128)(2,1)S(1)} collective-permute-done((bf16[16,16,8,256]{3,2,1,0:T(8,128)(2,1)S(1)}, bf16[16,16,8,256]{3,2,1,0:T(8,128)(2,1)S(1)}, u32[]{:S(2)}, u32[]{:S(2)}) %collective-permute-start) | collective-permute-done | bytes 1048608 | tf_op jit(solution)/shard_map/ppermute | solution.py:340
  58.3 0.0 copy-start
  58.3 0.0 copy-done.1
  58.3 5.0 %fwd.1 = (bf16[2,16,64,256]{3,2,1,0:T(8,128)(2,1)}, bf16[16,128,256]{2,1,0:T(8,128)(2,1)}) custom-call(bf16[128,256]{1,0:T(8,128)(2,1)S(1)} %get-tuple-element.14.x_ref, bf16[16,16,256]{2,1,0:T(8,128)(2,1)S(1)} %all_to_all.35.par_ref, bf16[16,16,8,256]{3,2,1,0:T(8,128)(2,1)} %copy-done.1, bf16[16,16,8,256]{3,2,1,0:T(8,128)(2,1)S(1)} %collective-permute-done.other_in), custom_call_target="tpu_custom_call" | custom-call | tf_op jit(solution)/shard_map/fwd/pallas_call | solution.py:345
  63.3 0.0 copy-done
  63.3 6.1 %all-to-all-start.2 = ((bf16[32,64,256]{2,1,0:T(8,128)(2,1)}), bf16[32,64,256]{2,1,0:T(8,128)(2,1)S(1)}, u32[]{:S(2)}, u32[]{:S(2)}) async-start(bf16[32,64,256]{2,1,0:T(8,128)(2,1)} %bitcast.15), calls=%async_computation.2 | async-start | bytes 2097152 | tf_op jit(solution)/shard_map/all_to_all | solution.py:356
  69.5 3.1 %collective-permute-start.1 = (bf16[8,256]{1,0:T(8,128)(2,1)S(1)}, bf16[8,256]{1,0:T(8,128)(2,1)S(1)}, u32[]{:S(2)}, u32[]{:S(2)}) collective-permute-start(bf16[8,256]{1,0:T(8,128)(2,1)S(1)} %dynamic-slice_bitcast_fusion.mine_ref), channel_id=1, source_target_pairs={{0,32},{32,0},{1,33},{33,1},{2,34},{34,2},{3,35},{35,3},{4,36},{36... | collective-permute-start | bytes 12296 | tf_op jit(solution)/shard_map/ppermute | solution.py:359
  72.6 9.6 %collective-permute-done.1.theirs_ref = bf16[8,256]{1,0:T(8,128)(2,1)S(1)} collective-permute-done((bf16[8,256]{1,0:T(8,128)(2,1)S(1)}, bf16[8,256]{1,0:T(8,128)(2,1)S(1)}, u32[]{:S(2)}, u32[]{:S(2)}) %collective-permute-start.1) | collective-permute-done | bytes 4128 | tf_op jit(solution)/shard_map/ppermute | solution.py:359
  82.2 2.4 %all-to-all-done.2 = bf16[32,64,256]{2,1,0:T(8,128)(2,1)S(1)} async-done(((bf16[32,64,256]{2,1,0:T(8,128)(2,1)}), bf16[32,64,256]{2,1,0:T(8,128)(2,1)S(1)}, u32[]{:S(2)}, u32[]{:S(2)}) %all-to-all-start.2) | async-done | bytes 1048608 | tf_op jit(solution)/shard_map/all_to_all | solution.py:356
  84.6 1.4 gram.1
  86.0 3.9 %collective-permute-start.2 = (bf16[392,256]{1,0:T(8,128)(2,1)S(1)}, bf16[392,256]{1,0:T(8,128)(2,1)S(1)}, u32[]{:S(2)}, u32[]{:S(2)}) collective-permute-start(bf16[392,256]{1,0:T(8,128)(2,1)S(1)} %get-tuple-element.20), channel_id=1, source_target_pairs={{0,1},{1,0},{2,3},{3,2},{4,5},{5,4},{6,7},{7,6},{8,9},{9,8},{10,11... | collective-permute-start | bytes 602120 | tf_op jit(solution)/shard_map/ppermute | solution.py:375
  90.0 1.0 collective-permute-done.2.got_ref
  91.1 10.0 %all_to_all.37.r_ref = bf16[4,112,256]{2,1,0:T(8,128)(2,1)S(1)} all-to-all(bf16[4,112,256]{2,1,0:T(8,128)(2,1)S(1)} %chip.1), channel_id=1, replica_groups=mesh['k'=4,'h'=2,'g'=2,'x'=4,'y'=4,'c'=2] {'g','h'}, dimensions={0} | all-to-all | bytes 458752 | tf_op jit(solution)/shard_map/all_to_all | solution.py:379
  101.1 0.3 deviation.1
  101.5 8.3 %all_to_all.38 = bf16[4,96,256]{2,1,0:T(8,128)(2,1)S(1)} all-to-all(bf16[4,96,256]{2,1,0:T(8,128)(2,1)S(1)} %deviation.1), channel_id=1, replica_groups=mesh['k'=4,'h'=2,'g'=2,'x'=4,'y'=4,'c'=2] {'g','h'}, dimensions={0} | all-to-all | bytes 393216 | tf_op jit(solution)/shard_map/all_to_all | solution.py:389
  109.8 4.8 %all-gather = bf16[8,96,256]{2,1,0:T(8,128)(2,1)S(1)} all-gather(bf16[4,96,256]{2,1,0:T(8,128)(2,1)S(1)} %all_to_all.38), channel_id=2, replica_groups=mesh['k'=4,'h'=2,'g'=2,'x'=4,'y'=4,'c'=2] {'c'}, dimensions={0}, use_global_device_ids=true | all-gather | bytes 589824 | tf_op jit(solution)/shard_map/all_gather | solution.py:389
  114.6 2.1 %pull.1 = bf16[2,16,136,128]{3,2,1,0:T(8,128)(2,1)S(1)} custom-call(bf16[2,4,96,256]{3,2,1,0:T(8,128)(2,1)S(1)} %bitcast.13, bf16[4,112,256]{2,1,0:T(8,128)(2,1)S(1)} %all_to_all.37.r_ref, bf16[8,256]{1,0:T(8,128)(2,1)S(1)} %get-tuple-element.19.tail_ref, bf16[2,1024,256]{2,1,0:T(8,128)(2,1)} %get-tuple-element.22.zc_in), custom_call_target="tpu_custom_call" | custom-call | tf_op jit(solution)/shard_map/pull/pallas_call | solution.py:390
  116.7 21.1 %all_to_all.39 = bf16[32,136,128]{2,1,0:T(8,128)(2,1)S(1)} all-to-all(bf16[32,136,128]{2,1,0:T(8,128)(2,1)S(1)} %bitcast.11), channel_id=1, replica_groups=mesh['k'=4,'h'=2,'g'=2,'x'=4,'y'=4,'c'=2] {'g','x','y'}, dimensions={0} | all-to-all | bytes 2228224 | tf_op jit(solution)/shard_map/all_to_all | solution.py:398
  137.8 4.1 %bwd.1 = bf16[8,24,256]{2,1,0:T(8,128)(2,1)S(1)} custom-call(bf16[2,16,136,128]{3,2,1,0:T(8,128)(2,1)S(1)} %bitcast.10, bf16[16,16,8,256]{3,2,1,0:T(8,128)(2,1)} %copy-done.1, bf16[16,16,8,256]{3,2,1,0:T(8,128)(2,1)} %copy-done, bf16[16,128,256]{2,1,0:T(8,128)(2,1)} %get-tuple-element.23.slope_in), custom_call_target="tpu_custom_call" | custom-call | tf_op jit(solution)/shard_map/bwd/pallas_call | solution.py:400
  142.0 15.8 %all_to_all.40.r_ref = bf16[8,24,256]{2,1,0:T(8,128)(2,1)S(1)} all-to-all(bf16[8,24,256]{2,1,0:T(8,128)(2,1)S(1)} %bwd.1), channel_id=1, replica_groups=mesh['k'=4,'h'=2,'g'=2,'x'=4,'y'=4,'c'=2] {'g','k'}, dimensions={0} | all-to-all | bytes 196608 | tf_op jit(solution)/shard_map/all_to_all | solution.py:408
  157.8 0.6 outputs.1
  (3 shorter events, 0.1 us)
Async XLA Ops:
  49.5 8.8 %copy-start.1 = (bf16[16,16,8,256]{3,2,1,0:T(8,128)(2,1)}, bf16[16,16,8,256]{3,2,1,0:T(8,128)(2,1)S(1)}, u32[]{:S(2)}) copy-start(bf16[16,16,8,256]{3,2,1,0:T(8,128)(2,1)S(1)} %all_to_all.36.own_in) | copy-start | bytes 3145732
  49.5 8.8 %collective-permute-start = (bf16[16,16,8,256]{3,2,1,0:T(8,128)(2,1)S(1)}, bf16[16,16,8,256]{3,2,1,0:T(8,128)(2,1)S(1)}, u32[]{:S(2)}, u32[]{:S(2)}) collective-permute-start(bf16[16,16,8,256]{3,2,1,0:T(8,128)(2,1)S(1)} %all_to_all.36.own_in), channel_id=1, source_target_pairs={{0,1},{1,0},{2,3},{3,2},{4,5},{5,4},{6,7},{7,6},{8,9},{9,8},{10,11... | collective-permute-start | bytes 3145736 | tf_op jit(solution)/shard_map/ppermute | solution.py:340
  58.3 5.0 %copy-start = (bf16[16,16,8,256]{3,2,1,0:T(8,128)(2,1)}, bf16[16,16,8,256]{3,2,1,0:T(8,128)(2,1)S(1)}, u32[]{:S(2)}) copy-start(bf16[16,16,8,256]{3,2,1,0:T(8,128)(2,1)S(1)} %collective-permute-done.other_in) | copy-start | bytes 3145732
  63.3 21.3 %all-to-all-start.2 = ((bf16[32,64,256]{2,1,0:T(8,128)(2,1)}), bf16[32,64,256]{2,1,0:T(8,128)(2,1)S(1)}, u32[]{:S(2)}, u32[]{:S(2)}) async-start(bf16[32,64,256]{2,1,0:T(8,128)(2,1)} %bitcast.15), calls=%async_computation.2 | async-start | bytes 2097152 | tf_op jit(solution)/shard_map/all_to_all | solution.py:356
  69.5 12.7 %collective-permute-start.1 = (bf16[8,256]{1,0:T(8,128)(2,1)S(1)}, bf16[8,256]{1,0:T(8,128)(2,1)S(1)}, u32[]{:S(2)}, u32[]{:S(2)}) collective-permute-start(bf16[8,256]{1,0:T(8,128)(2,1)S(1)} %dynamic-slice_bitcast_fusion.mine_ref), channel_id=1, source_target_pairs={{0,32},{32,0},{1,33},{33,1},{2,34},{34,2},{3,35},{35,3},{4,36},{36... | collective-permute-start | bytes 12296 | tf_op jit(solution)/shard_map/ppermute | solution.py:359
  86.0 5.0 %collective-permute-start.2 = (bf16[392,256]{1,0:T(8,128)(2,1)S(1)}, bf16[392,256]{1,0:T(8,128)(2,1)S(1)}, u32[]{:S(2)}, u32[]{:S(2)}) collective-permute-start(bf16[392,256]{1,0:T(8,128)(2,1)S(1)} %get-tuple-element.20), channel_id=1, source_target_pairs={{0,1},{1,0},{2,3},{3,2},{4,5},{5,4},{6,7},{7,6},{8,9},{9,8},{10,11... | collective-permute-start | bytes 602120 | tf_op jit(solution)/shard_map/ppermute | solution.py:375
